TPU v7x, 32 devices: a whole 2x2x4 slice. The times are simulated.
32 devices in a mesh: patch: 8 (over y, x, core), group: 4 (over z).
Axes of the slice: x: 2, y: 2, z: 4, core: 2. Of those that a mesh axis runs over, the one named last changes fastest.
Arguments:
- grid_latent: bfloat16 [16384, 512], P(('patch', 'group')), may hold values from -6 to 6
- mesh_latent: bfloat16 [8192, 512], P(('patch', 'group')), may hold values from -6 to 6
- cotangent: bfloat16 [8192, 512], P(('patch', 'group')), may hold values from -6 to 6
- halo_rows: int32 [8192], P(('patch', 'group')), may hold values from 0 to 511
- encoder_sender: int32 [24576], P(('patch', 'group')), may hold values from 0 to 767
- encoder_target: int32 [24576], P(('patch', 'group')), may hold values from 0 to 255
- encoder_count: int32 [32], P(('patch', 'group')), may hold values from 96 to 768, as said below
- process_sender: int32 [24576], P(('patch', 'group')), may hold values from 0 to 319
- process_target: int32 [24576], P(('patch', 'group')), may hold values from 0 to 255
- process_count: int32 [32], P(('patch', 'group')), may hold values from 96 to 768, as said below
- encoder_source: bfloat16 [512, 512], replicated, may hold values from -0.25 to 0.25
- encoder_dest: bfloat16 [512, 512], replicated, may hold values from -0.25 to 0.25
- encoder_output: bfloat16 [512, 512], replicated, may hold values from -0.25 to 0.25
- encoder_gain: float32 [512], replicated, may hold values from 0.5 to 1.5
- process_source: bfloat16 [512, 512], replicated, may hold values from -0.25 to 0.25
- process_dest: bfloat16 [512, 512], replicated, may hold values from -0.25 to 0.25
- process_output: bfloat16 [512, 512], replicated, may hold values from -0.25 to 0.25
- process_gain: float32 [512], replicated, may hold values from 0.5 to 1.5
Outputs:
- grid_grad: bfloat16 [16384, 512], P(('patch', 'group'))
- mesh_grad: bfloat16 [8192, 512], P(('patch', 'group'))
Inputs may be any that keep to these rules, and one draw needn't show every extreme that they name: `halo_rows`: a block's entries are rows of its own grid nodes. `encoder_sender`: rows of the block's extended grid table. `encoder_target`: rows of the block's own mesh nodes. The first encoder_count slots of a block are edges, the rest padding; some block is full in every draw. `process_sender`: rows of the block's sender table: its own mesh nodes, then the coarse nodes of its group. `process_target`: rows of the block's own mesh nodes. The first process_count slots of a block are edges, the rest padding; some block is full in every draw.
All inputs are finite; a program needn't handle non-finite values.
Results may differ from a plain program's by a relative error of at most 0.01.
Values may be sent and summed in bfloat16 or wider, within the bound.
No kernel may reach another device: no remote copies, remote signals or barrier semaphores. Data moves between devices by JAX's collectives and lax.ppermute only.
A program may use at most 64 MiB of HBM per device.

v0:
```python
import jax
import jax.numpy as jnp
from jax import lax
from jax.sharding import PartitionSpec as P

EPSILON = 1e-05


def padded_2(x, sides, width):
    for axis, dim in sides:
        size, length = (lax.axis_size(axis), x.shape[dim])
        up = [(i, (i + 1) % size) for i in range(size)]
        down = [(j, i) for i, j in up]
        last = lax.slice_in_dim(x, length - width, length, axis=dim)
        initial = lax.slice_in_dim(x, 0, width, axis=dim)
        before = lax.ppermute(last, axis, up)
        after = lax.ppermute(initial, axis, down)
        x = jnp.concatenate([before, x, after], axis=dim)
    return x


def silu_slope(values):
    logistic = jax.nn.sigmoid(values)
    return logistic * (1.0 + values * (1.0 - logistic))


def norm_forward(values, norm_gain):
    center = values - jnp.mean(values, axis=-1, keepdims=True)
    inverse = lax.rsqrt(jnp.mean(center * center, axis=-1, keepdims=True) + EPSILON)
    normed = center * inverse
    return (normed * norm_gain, normed, inverse)


def norm_backward(grad_out, normed, inverse, norm_gain):
    scaled = grad_out * norm_gain
    return inverse * (
        scaled
        - jnp.mean(scaled, axis=-1, keepdims=True)
        - normed * jnp.mean(scaled * normed, axis=-1, keepdims=True)
    )


def edge_forward(source, dest_proj, sender, target, live_count, out_weight, mesh_count):
    preact = source[sender] + dest_proj[target]
    hidden = jax.nn.silu(preact).astype(jnp.bfloat16)
    message = jnp.dot(hidden, out_weight, preferred_element_type=jnp.float32).astype(jnp.bfloat16)
    live_slots = jnp.arange(sender.shape[0], dtype=jnp.int32) < live_count
    onehot = (
        (target[None, :] == jnp.arange(mesh_count, dtype=jnp.int32)[:, None]) & live_slots[None, :]
    ).astype(jnp.bfloat16)
    gathered = jnp.dot(onehot, message, preferred_element_type=jnp.float32)
    return (gathered, preact, onehot, live_slots)


def edge_backward(
    grad_gathered, preact, onehot, live_slots, sender, target, out_weight, table_rows
):
    grad_message = jnp.where(live_slots[:, None], grad_gathered[target], 0.0).astype(jnp.bfloat16)
    grad_hidden = jnp.dot(grad_message, out_weight.T, preferred_element_type=jnp.float32)
    grad_preact = (grad_hidden * silu_slope(preact)).astype(jnp.bfloat16)
    chooser = (sender[None, :] == jnp.arange(table_rows, dtype=jnp.int32)[:, None]).astype(
        jnp.bfloat16
    )
    grad_source = jnp.dot(chooser, grad_preact, preferred_element_type=jnp.float32)
    grad_dest = jnp.dot(onehot, grad_preact, preferred_element_type=jnp.float32)
    return (grad_source, grad_dest)


def encoder_pass(
    extended,
    mesh_rows,
    sender,
    target,
    live_count,
    source_weight,
    dest_weight,
    out_weight,
    norm_gain,
):
    source = jnp.dot(extended, source_weight, preferred_element_type=jnp.float32)
    dest_proj = jnp.dot(mesh_rows, dest_weight, preferred_element_type=jnp.float32)
    gathered, preact, onehot, live_slots = edge_forward(
        source, dest_proj, sender, target, live_count, out_weight, mesh_rows.shape[0]
    )
    shifted, normed, inverse = norm_forward(gathered, norm_gain)
    updated = (mesh_rows.astype(jnp.float32) + shifted).astype(jnp.bfloat16)
    return (updated, (preact, onehot, live_slots, normed, inverse))


def encoder_backward(
    grad_updated, stored, table_rows, sender, target, dest_weight, out_weight, norm_gain
):
    preact, onehot, live_slots, normed, inverse = stored
    grad_gathered = norm_backward(grad_updated, normed, inverse, norm_gain)
    grad_source, grad_dest = edge_backward(
        grad_gathered, preact, onehot, live_slots, sender, target, out_weight, table_rows
    )
    mesh_grad = grad_updated + jnp.dot(
        grad_dest.astype(jnp.bfloat16), dest_weight.T, preferred_element_type=jnp.float32
    )
    return (mesh_grad, grad_source.astype(jnp.bfloat16))


def process_grads(
    updated,
    coarse_proj,
    sender,
    target,
    live_count,
    cotangent,
    source_weight,
    dest_weight,
    out_weight,
    norm_gain,
):
    local_proj = jnp.dot(updated, source_weight, preferred_element_type=jnp.float32)
    source = jnp.concatenate([local_proj, coarse_proj], axis=0)
    dest_proj = jnp.dot(updated, dest_weight, preferred_element_type=jnp.float32)
    gathered, preact, onehot, live_slots = edge_forward(
        source, dest_proj, sender, target, live_count, out_weight, updated.shape[0]
    )
    unused, normed, inverse = norm_forward(gathered, norm_gain)
    grad_out = cotangent.astype(jnp.float32)
    grad_gathered = norm_backward(grad_out, normed, inverse, norm_gain)
    grad_source, grad_dest = edge_backward(
        grad_gathered, preact, onehot, live_slots, sender, target, out_weight, source.shape[0]
    )
    mesh_count = updated.shape[0]
    grad_local = grad_out + jnp.dot(
        grad_source[:mesh_count].astype(jnp.bfloat16),
        source_weight.T,
        preferred_element_type=jnp.float32,
    )
    grad_local = grad_local + jnp.dot(
        grad_dest.astype(jnp.bfloat16), dest_weight.T, preferred_element_type=jnp.float32
    )
    return (grad_local, grad_source[mesh_count:])


def on_device(
    grid_latent,
    mesh_latent,
    cotangent,
    halo_rows,
    encoder_sender,
    encoder_target,
    encoder_count,
    process_sender,
    process_target,
    process_count,
    encoder_source,
    encoder_dest,
    encoder_output,
    encoder_gain,
    process_source,
    process_dest,
    process_output,
    process_gain,
):
    rim_size = halo_rows.shape[0] // 2
    grid_rows = grid_latent.shape[0]
    outgoing = grid_latent[halo_rows]
    padded = padded_2(outgoing, (("patch", 0),), rim_size)
    extended = jnp.concatenate([grid_latent, padded[:rim_size], padded[3 * rim_size :]], axis=0)
    updated, stored = encoder_pass(
        extended,
        mesh_latent,
        encoder_sender,
        encoder_target,
        encoder_count[0],
        encoder_source,
        encoder_dest,
        encoder_output,
        encoder_gain,
    )
    coarse_rows = mesh_latent.shape[0] // 16
    coarse_proj = jnp.dot(
        lax.all_gather(updated[:coarse_rows], "group", axis=0, tiled=True),
        process_source,
        preferred_element_type=jnp.float32,
    )
    grad_local, grad_coarse = process_grads(
        updated,
        coarse_proj,
        process_sender,
        process_target,
        process_count[0],
        cotangent,
        process_source,
        process_dest,
        process_output,
        process_gain,
    )
    back_weight = process_source.astype(jnp.float32).T
    coarse_grad = lax.psum_scatter(
        jnp.dot(
            grad_coarse,
            back_weight,
            precision=lax.Precision.HIGHEST,
            preferred_element_type=jnp.float32,
        ),
        "group",
        scatter_dimension=0,
        tiled=True,
    )
    grad_updated = grad_local.at[:coarse_rows].add(coarse_grad)
    mesh_grad, source_grads = encoder_backward(
        grad_updated,
        stored,
        extended.shape[0],
        encoder_sender,
        encoder_target,
        encoder_dest,
        encoder_output,
        encoder_gain,
    )
    own_grad = jnp.dot(
        source_grads[:grid_rows], encoder_source.T, preferred_element_type=jnp.float32
    )
    returned = padded_2(source_grads[grid_rows:], (("patch", 0),), rim_size)
    peer_sources = jnp.concatenate([returned[:rim_size], returned[3 * rim_size :]], axis=0)
    from_peers = jnp.dot(peer_sources, encoder_source.T, preferred_element_type=jnp.float32)
    grid_grad = own_grad.at[halo_rows].add(from_peers)
    return (grid_grad.astype(jnp.bfloat16), mesh_grad.astype(jnp.bfloat16))


def solution(mesh):
    return jax.shard_map(
        on_device,
        mesh=mesh,
        in_specs=(
            P(("patch", "group"), None),
            P(("patch", "group"), None),
            P(("patch", "group"), None),
            P(("patch", "group")),
            P(("patch", "group")),
            P(("patch", "group")),
            P(("patch", "group")),
            P(("patch", "group")),
            P(("patch", "group")),
            P(("patch", "group")),
            P(),
            P(),
            P(),
            P(),
            P(),
            P(),
            P(),
            P(),
        ),
        out_specs=(P(("patch", "group"), None), P(("patch", "group"), None)),
        check_vma=False,
    )
```

profile of v0, /device:TPU:0, one launch (start us, length us, event | category | flops | bytes accessed | tf_op | source)
XLA Modules:
  0.0 107.7 jit_solution(11747875148235382991)
XLA Ops:
  7.3 0.8 compare_select_fusion.4
  8.1 0.6 copy-done.13
  8.7 2.3 %gather_fusion = bf16[256,512]{1,0:T(8,128)(2,1)S(1)} fusion(bf16[512,512]{1,0:T(8,128)(2,1)} %param.20, s32[1024]{0:T(1024)S(1)} %pad_clamp_fusion.4), kind=kCustom, calls=%fused_computation | custom fusion | bytes 525312 | tf_op jit(solution)/shard_map/gather | solution.py:162
  11.0 0.5 collective-permute-start
  11.6 2.9 %collective-permute-start.1 = (bf16[128,512]{1,0:T(8,128)(2,1)S(1)}, bf16[128,512]{1,0:T(8,128)(2,1)S(1)}, u32[]{:S(2)}, u32[]{:S(2)}) collective-permute-start(bf16[128,512]{1,0:T(8,128)(2,1)S(1)} %get-tuple-element.21), channel_id=1, source_target_pairs={{4,0},{8,4},{12,8},{16,12},{20,16},{24,20},{28,24},{0,28},{5,1},{9... | collective-permute-start | bytes 393224 | tf_op jit(solution)/shard_map/ppermute | solution.py:17
  16.3 3.1 %gather_fusion.2 = f32[768,512]{1,0:T(8,128)} fusion(f32[256,512]{1,0:T(8,128)S(1)} %fusion.69, s32[1024]{0:T(1024)S(1)} %pad_clamp_fusion.2), kind=kCustom, calls=%fused_computation.2 | custom fusion | bytes 3148800 | tf_op jit(solution)/shard_map/gather | solution.py:44
  19.5 0.6 fusion.7
  20.0 3.1 %gather_fusion.1 = f32[768,512]{1,0:T(8,128)} fusion(f32[768,512]{1,0:T(8,128)S(1)} %fusion.7, s32[1024]{0:T(1024)S(1)} %pad_clamp_fusion.3), kind=kCustom, calls=%fused_computation.1 | custom fusion | bytes 3148800 | tf_op jit(solution)/shard_map/gather | solution.py:44
  23.2 2.9 %fusion.67 = (f32[256]{0:T(256)S(1)}, f32[256,512]{1,0:T(8,128)S(1)}) fusion(bf16[512,512]{1,0:T(8,128)(2,1)} %param.32, f32[768,512]{1,0:T(8,128)} %gather_fusion.1, f32[768,512]{1,0:T(8,128)} %gather_fusion.2, s32[768]{0:T(1024)S(1)} %copy-done.18, pred[768]{0:T(1024)(128)(4,1)S(1)} %iota_compare_fusion.9), kind=kOutput, calls=%fused_computation.111 | convolution fusion | flops 607256320 | bytes 4199168 | tf_op jit(solution)/shard_map/dot_general | solution.py:51
  26.5 14.3 %all_gather.3 = bf16[64,512]{1,0:T(8,128)(2,1)S(1)} all-gather(bf16[16,512]{1,0:T(8,128)(2,1)S(1)} %slice.72), channel_id=1, replica_groups=mesh['patch'=8,'group'=4] {'group'}, dimensions={0}, use_global_device_ids=true | all-gather | bytes 81920 | tf_op jit(solution)/shard_map/all_gather | solution.py:178
  41.7 3.1 %gather_fusion.3 = f32[768,512]{1,0:T(8,128)} fusion(f32[320,512]{1,0:T(8,128)S(1)} %pad_maximum_fusion, s32[1024]{0:T(1024)S(1)} %pad_clamp_fusion.1), kind=kCustom, calls=%fused_computation.3 | custom fusion | bytes 3148800 | tf_op jit(solution)/shard_map/gather | solution.py:44
  44.8 3.1 %gather_fusion.4 = f32[768,512]{1,0:T(8,128)} fusion(f32[256,512]{1,0:T(8,128)S(1)} %fusion.72, s32[1024]{0:T(1024)S(1)} %pad_clamp_fusion), kind=kCustom, calls=%fused_computation.4 | custom fusion | bytes 3148800 | tf_op jit(solution)/shard_map/gather | solution.py:44
  47.9 2.9 %fusion.68 = (f32[256]{0:T(256)S(1)}, f32[256,512]{1,0:T(8,128)S(1)}) fusion(bf16[512,512]{1,0:T(8,128)(2,1)} %param.36, f32[768,512]{1,0:T(8,128)} %gather_fusion.3, f32[768,512]{1,0:T(8,128)} %gather_fusion.4, s32[768]{0:T(1024)S(1)} %copy-done.10, pred[768]{0:T(1024)(128)(4,1)S(1)} %iota_compare_fusion.8), kind=kOutput, calls=%fused_computation.112 | convolution fusion | flops 607256320 | bytes 4199168 | tf_op jit(solution)/shard_map/dot_general | solution.py:51
  51.5 3.3 %gather_fusion.5 = bf16[768,512]{1,0:T(8,128)(2,1)} fusion(bf16[256,512]{1,0:T(8,128)(2,1)S(1)} %fusion.33, s32[1024]{0:T(1024)S(1)} %pad_clamp_fusion), kind=kCustom, calls=%fused_computation.5 | custom fusion | bytes 1575936 | tf_op jit(solution)/shard_map/gather | solution.py:58
  54.9 3.2 %multiply_convert_fusion.1 = bf16[768,512]{1,0:T(8,128)(2,1)S(1)} fusion(bf16[512,512]{1,0:T(8,128)(2,1)} %param.36, bf16[768,512]{1,0:T(8,128)(2,1)} %gather_fusion.5, pred[768]{0:T(1024)(128)(4,1)S(1)} %iota_compare_fusion.8, f32[768,512]{1,0:T(8,128)} %gather_fusion.3, f32[768,512]{1,0:T(8,128)} %gather_fusion.4), kind=kOutput, calls=%fused_computation.12 | convolution fusion | flops 406978560 | bytes 5243648 | tf_op jit(solution)/shard_map/dot_general | solution.py:59
  58.1 0.9 copy-done.6
  59.0 0.4 fusion.6
  59.4 1.3 %fusion.54 = f32[64,512]{1,0:T(8,128)} fusion(bf16[512,512]{1,0:T(8,128)(2,1)S(1)} %copy-done.1, f32[320,512]{1,0:T(8,128)S(1)} %fusion.6), kind=kOutput, calls=%fused_computation.79 | convolution fusion | flops 201326592 | bytes 786432 | tf_op jit(solution)/shard_map/dot_general | solution.py:196
  60.7 0.3 convolution_add_fusion.2
  61.0 1.7 %convolution_add_fusion.1 = f32[256,512]{1,0:T(8,128)S(1)} fusion(f32[256,512]{1,0:T(8,128)S(1)} %convolution_add_fusion.2, bf16[512,512]{1,0:T(8,128)(2,1)S(1)} %copy-done.4, bf16[768,512]{1,0:T(8,128)(2,1)} %copy-done.6, s32[768]{0:T(1024)S(1)} %copy-done.10, pred[768]{0:T(1024)(128)(4,1)} %copy-done.22), kind=kOutput, calls=%fused_computation.24 | convolution fusion | flops 336199680 | bytes 2363136 | tf_op jit(solution)/shard_map/dot_general | solution.py:134
  62.8 17.9 %reduce-scatter.2.cloned.1.call-done = f32[16,512]{1,0:T(8,128)} async-done(((f32[64,512]{1,0:T(8,128)}), f32[16,512]{1,0:T(8,128)}) %reduce-scatter.2.cloned.1.call-update) | async-done | bytes 32784 | tf_op jit(solution)/shard_map/reduce_scatter | solution.py:195
  80.7 0.8 fusion.56
  82.0 2.7 %gather_fusion.6 = bf16[768,512]{1,0:T(8,128)(2,1)S(1)} fusion(bf16[256,512]{1,0:T(8,128)(2,1)S(1)} %subtract_multiply_fusion, s32[1024]{0:T(1024)S(1)} %pad_clamp_fusion.2), kind=kCustom, calls=%fused_computation.6 | custom fusion | bytes 1575936 | tf_op jit(solution)/shard_map/gather | solution.py:58
  84.7 3.7 %multiply_convert_fusion = bf16[768,512]{1,0:T(8,128)(2,1)} fusion(bf16[512,512]{1,0:T(8,128)(2,1)S(1)} %copy-done.23, bf16[768,512]{1,0:T(8,128)(2,1)S(1)} %gather_fusion.6, pred[768]{0:T(1024)(128)(4,1)S(1)} %copy-done.25, f32[768,512]{1,0:T(8,128)} %gather_fusion.1, f32[768,512]{1,0:T(8,128)} %gather_fusion.2), kind=kOutput, calls=%fused_computation.10 | convolution fusion | flops 406978560 | bytes 5243648 | tf_op jit(solution)/shard_map/dot_general | solution.py:59
  88.5 2.5 %fusion.4 = bf16[256,512]{1,0:T(8,128)(2,1)} fusion(f32[256,512]{1,0:T(8,128)S(1)} %fusion.56, bf16[512,512]{1,0:T(8,128)(2,1)S(1)} %copy-done.8, bf16[768,512]{1,0:T(8,128)(2,1)} %multiply_convert_fusion, s32[768]{0:T(1024)S(1)} %copy-done.19, pred[768]{0:T(1024)(128)(4,1)S(1)} %copy-done.25), kind=kOutput, calls=%fused_computation.26 | convolution fusion | flops 336330752 | bytes 2100992 | tf_op jit(solution)/shard_map/dot_general | solution.py:98
  91.0 0.8 fusion.1
  91.9 2.6 %collective-permute-start.3 = (bf16[128,512]{1,0:T(8,128)(2,1)S(1)}, bf16[128,512]{1,0:T(8,128)(2,1)S(1)}, u32[]{:S(2)}, u32[]{:S(2)}) collective-permute-start(bf16[128,512]{1,0:T(8,128)(2,1)S(1)} %get-tuple-element.19), channel_id=1, source_target_pairs={{4,0},{8,4},{12,8},{16,12},{20,16},{24,20},{28,24},{0,28},{5,1},{9... | collective-permute-start | bytes 393224 | tf_op jit(solution)/shard_map/ppermute | solution.py:17
  94.5 0.5 fusion.35
  95.0 2.2 %collective-permute-done.2 = bf16[128,512]{1,0:T(8,128)(2,1)S(1)} collective-permute-done((bf16[128,512]{1,0:T(8,128)(2,1)S(1)}, bf16[128,512]{1,0:T(8,128)(2,1)S(1)}, u32[]{:S(2)}, u32[]{:S(2)}) %collective-permute-start.2) | collective-permute-done | bytes 131104 | tf_op jit(solution)/shard_map/ppermute | solution.py:16
  97.2 0.3 fusion.50
  97.5 2.5 %scatter_fusion = f32[512,512]{1,0:T(8,128)S(1)} fusion(f32[512,512]{1,0:T(8,128)S(1)} %fusion.35, s32[256]{0:T(256)S(1)} %copy-done.14, f32[256,512]{1,0:T(8,128)S(1)} %fusion.50), kind=kCustom, calls=%fused_computation.7 | custom fusion | flops 131072 | bytes 1573888 | tf_op jit(solution)/shard_map/scatter-add | solution.py:223
  100.0 0.9 convert_element_type.67
  (91 shorter events, 3.0 us)
Async XLA Ops:
  7.2 12.3 %copy-start = (bf16[512,512]{1,0:T(8,128)(2,1)S(1)}, bf16[512,512]{1,0:T(8,128)(2,1)}, u32[]{:S(2)}) copy-start(bf16[512,512]{1,0:T(8,128)(2,1)} %param.30) | copy-start | bytes 1572868
  7.2 8.6 %copy-start.20 = (s32[768]{0:T(1024)S(1)}, s32[768]{0:T(1024)}, u32[]{:S(2)}) copy-start(s32[768]{0:T(1024)} %param.24) | copy-start | bytes 9220
  7.2 8.7 %copy-start.16 = (s32[768]{0:T(1024)S(1)}, s32[768]{0:T(1024)}, u32[]{:S(2)}) copy-start(s32[768]{0:T(1024)} %param.27) | copy-start | bytes 9220
  7.2 8.7 %copy-start.18 = (s32[768]{0:T(1024)S(1)}, s32[768]{0:T(1024)}, u32[]{:S(2)}) copy-start(s32[768]{0:T(1024)} %param.25) | copy-start | bytes 9220
  7.2 8.7 %copy-start.10 = (s32[768]{0:T(1024)S(1)}, s32[768]{0:T(1024)}, u32[]{:S(2)}) copy-start(s32[768]{0:T(1024)} %param.28) | copy-start | bytes 9220
  7.2 8.7 %copy-start.7 = (bf16[512,512]{1,0:T(8,128)(2,1)S(1)}, bf16[512,512]{1,0:T(8,128)(2,1)}, u32[]{:S(2)}) copy-start(bf16[512,512]{1,0:T(8,128)(2,1)} %param.31) | copy-start | bytes 1572868
  7.2 8.7 %copy-start.5 = (bf16[256,512]{1,0:T(8,128)(2,1)S(1)}, bf16[256,512]{1,0:T(8,128)(2,1)}, u32[]{:S(2)}) copy-start(bf16[256,512]{1,0:T(8,128)(2,1)} %param.21) | copy-start | bytes 786436
  7.2 73.5 %reduce-scatter.2.cloned.1.call-start = ((), (), s32[]{:S(2)}) async-start(), calls=%async_computation.1 | async-start | bytes 163840 | tf_op jit(solution)/shard_map/reduce_scatter | solution.py:195
  8.1 0.6 copy-start.13
  11.0 8.4 %collective-permute-start = (bf16[128,512]{1,0:T(8,128)(2,1)S(1)}, bf16[128,512]{1,0:T(8,128)(2,1)S(1)}, u32[]{:S(2)}, u32[]{:S(2)}) collective-permute-start(bf16[128,512]{1,0:T(8,128)(2,1)S(1)} %get-tuple-element.20), channel_id=1, source_target_pairs={{0,4},{4,8},{8,12},{12,16},{16,20},{20,24},{24,28},{28,0},{1,5},{5... | collective-permute-start | bytes 393224 | tf_op jit(solution)/shard_map/ppermute | solution.py:16
  11.6 7.9 %collective-permute-start.1 = (bf16[128,512]{1,0:T(8,128)(2,1)S(1)}, bf16[128,512]{1,0:T(8,128)(2,1)S(1)}, u32[]{:S(2)}, u32[]{:S(2)}) collective-permute-start(bf16[128,512]{1,0:T(8,128)(2,1)S(1)} %get-tuple-element.21), channel_id=1, source_target_pairs={{4,0},{8,4},{12,8},{16,12},{20,16},{24,20},{28,24},{0,28},{5,1},{9... | collective-permute-start | bytes 393224 | tf_op jit(solution)/shard_map/ppermute | solution.py:17
  15.8 7.3 %copy-start.24 = (pred[768]{0:T(1024)(128)(4,1)}, pred[768]{0:T(1024)(128)(4,1)S(1)}, u32[]{:S(2)}) copy-start(pred[768]{0:T(1024)(128)(4,1)S(1)} %iota_compare_fusion.9) | copy-start | bytes 2308
  16.3 38.6 %copy-start.22 = (pred[768]{0:T(1024)(128)(4,1)}, pred[768]{0:T(1024)(128)(4,1)S(1)}, u32[]{:S(2)}) copy-start(pred[768]{0:T(1024)(128)(4,1)S(1)} %iota_compare_fusion.8) | copy-start | bytes 2308
  16.3 3.2 %copy-start.2 = (bf16[512,512]{1,0:T(8,128)(2,1)S(1)}, bf16[512,512]{1,0:T(8,128)(2,1)}, u32[]{:S(2)}) copy-start(bf16[512,512]{1,0:T(8,128)(2,1)} %param.20) | copy-start | bytes 1572868
  23.2 3.1 %copy-start.9 = (f32[512]{0:T(512)S(1)}, f32[512]{0:T(512)}, u32[]{:S(2)}) copy-start(f32[512]{0:T(512)} %param.33) | copy-start | bytes 6148
  26.0 14.8 %copy-start.1 = (bf16[512,512]{1,0:T(8,128)(2,1)S(1)}, bf16[512,512]{1,0:T(8,128)(2,1)}, u32[]{:S(2)}) copy-start(bf16[512,512]{1,0:T(8,128)(2,1)} %param.34) | copy-start | bytes 1572868
  26.3 15.0 %copy-start.11 = (f32[256]{0:T(256)}, f32[256]{0:T(256)S(1)}, u32[]{:S(2)}) copy-start(f32[256]{0:T(256)S(1)} %add_rsqrt_fusion.1) | copy-start | bytes 3076
  26.3 15.0 %copy-start.4 = (bf16[512,512]{1,0:T(8,128)(2,1)S(1)}, bf16[512,512]{1,0:T(8,128)(2,1)}, u32[]{:S(2)}) copy-start(bf16[512,512]{1,0:T(8,128)(2,1)} %param.35) | copy-start | bytes 1572868
  47.9 3.2 %copy-start.3 = (bf16[256,512]{1,0:T(8,128)(2,1)S(1)}, bf16[256,512]{1,0:T(8,128)(2,1)}, u32[]{:S(2)}) copy-start(bf16[256,512]{1,0:T(8,128)(2,1)} %param.22) | copy-start | bytes 786436
  47.9 3.2 %copy-start.15 = (f32[512]{0:T(512)S(1)}, f32[512]{0:T(512)}, u32[]{:S(2)}) copy-start(f32[512]{0:T(512)} %param.37) | copy-start | bytes 6148
  54.9 4.1 %copy-start.17 = (s32[768]{0:T(1024)S(1)}, s32[768]{0:T(1024)}, u32[]{:S(2)}) copy-start(s32[768]{0:T(1024)} %param.27) | copy-start | bytes 9220
  58.1 0.9 copy-start.6
  61.0 20.5 %copy-start.12 = (f32[256]{0:T(256)S(1)}, f32[256]{0:T(256)}, u32[]{:S(2)}) copy-start(f32[256]{0:T(256)} %copy-done.11) | copy-start | bytes 3076
  82.0 2.7 %copy-start.23 = (bf16[512,512]{1,0:T(8,128)(2,1)S(1)}, bf16[512,512]{1,0:T(8,128)(2,1)}, u32[]{:S(2)}) copy-start(bf16[512,512]{1,0:T(8,128)(2,1)} %param.32) | copy-start | bytes 1572868
  82.0 2.7 %copy-start.25 = (pred[768]{0:T(1024)(128)(4,1)S(1)}, pred[768]{0:T(1024)(128)(4,1)}, u32[]{:S(2)}) copy-start(pred[768]{0:T(1024)(128)(4,1)} %copy-done.24) | copy-start | bytes 2308
  84.7 3.8 %copy-start.8 = (bf16[512,512]{1,0:T(8,128)(2,1)S(1)}, bf16[512,512]{1,0:T(8,128)(2,1)}, u32[]{:S(2)}) copy-start(bf16[512,512]{1,0:T(8,128)(2,1)} %param.31) | copy-start | bytes 1572868
  84.7 3.8 %copy-start.19 = (s32[768]{0:T(1024)S(1)}, s32[768]{0:T(1024)}, u32[]{:S(2)}) copy-start(s32[768]{0:T(1024)} %param.25) | copy-start | bytes 9220
  88.5 2.5 %copy-start.21 = (s32[768]{0:T(1024)S(1)}, s32[768]{0:T(1024)}, u32[]{:S(2)}) copy-start(s32[768]{0:T(1024)} %param.24) | copy-start | bytes 9220
  88.5 2.5 %copy-start.26 = (bf16[768,512]{1,0:T(8,128)(2,1)S(1)}, bf16[768,512]{1,0:T(8,128)(2,1)}, u32[]{:S(2)}) copy-start(bf16[768,512]{1,0:T(8,128)(2,1)} %multiply_convert_fusion) | copy-start | bytes 2359300
  91.8 5.3 %collective-permute-start.2 = (bf16[128,512]{1,0:T(8,128)(2,1)S(1)}, bf16[128,512]{1,0:T(8,128)(2,1)S(1)}, u32[]{:S(2)}, u32[]{:S(2)}) collective-permute-start(bf16[128,512]{1,0:T(8,128)(2,1)S(1)} %get-tuple-element.18), channel_id=1, source_target_pairs={{0,4},{4,8},{8,12},{12,16},{16,20},{20,24},{24,28},{28,0},{1,5},{5... | collective-permute-start | bytes 393224 | tf_op jit(solution)/shard_map/ppermute | solution.py:16
  91.9 5.6 %copy-start.14 = (s32[256]{0:T(256)S(1)}, s32[256]{0:T(256)}, u32[]{:S(2)}) copy-start(s32[256]{0:T(256)} %copy-done.13) | copy-start | bytes 3076
  91.9 5.3 %collective-permute-start.3 = (bf16[128,512]{1,0:T(8,128)(2,1)S(1)}, bf16[128,512]{1,0:T(8,128)(2,1)S(1)}, u32[]{:S(2)}, u32[]{:S(2)}) collective-permute-start(bf16[128,512]{1,0:T(8,128)(2,1)S(1)} %get-tuple-element.19), channel_id=1, source_target_pairs={{4,0},{8,4},{12,8},{16,12},{20,16},{24,20},{28,24},{0,28},{5,1},{9... | collective-permute-start | bytes 393224 | tf_op jit(solution)/shard_map/ppermute | solution.py:17
Sparse Core Ops, SparseCore 0:
  61.2 19.4 reduce-scatter.1
where the time goes:
time: 109 us; the launch traced here: 108 us
  local copies, waits for them, and re-layouts  22.4 us (21%)
  matrix products  22.2 us (20%)
  waiting for transfers between devices  20.1 us (18%)
  between operations  15.9 us (15%)
  blocking collectives  14.3 us (13%)
  other arithmetic  6.52 us (6%)
  starting transfers between devices  6.2 us (6%)
    reduce_scatter x1, waiting for transfers between devices, on_device(): lax.psum_scatter(jnp.dot(grad_coarse, back_weight, precision=lax.Precisio...  17.9 us
    all_gather x1, blocking collectives, on_device(): lax.all_gather(updated[:coarse_rows], 'group', axis=0, tiled=True)  14.3 us
    gather x4, local copies, waits for them, and re-layouts, edge_forward(): preact = source[sender] + dest_proj[target]  12.5 us
    dot_general x2, matrix products, edge_backward(): jnp.dot(grad_message, out_weight.T, preferred_element_type=jnp.float32)  6.96 us
    gather x2, local copies, waits for them, and re-layouts, edge_backward(): grad_gathered[target]  6 us
    dot_general x2, matrix products, edge_forward(): gathered = jnp.dot(onehot, message, preferred_element_type=jnp.float32)  5.79 us
    ppermute x2, starting transfers between devices, padded_2(): after = lax.ppermute(initial, axis, down)  5.56 us
    dot_general x1, matrix products, encoder_backward(): jnp.dot(grad_dest.astype(jnp.bfloat16), dest_weight.T, preferred_element_...  2.51 us
  transfers between devices with their start and end apart: 5, of which 2 were waited for; matrix products, arithmetic and copies ran while one was open for 5% of the time, Pallas kernels for 0%

commit v1 on v0

v1 whole, which is shorter than its diff:
```python
import functools

import jax
import jax.numpy as jnp
from jax import lax
from jax.experimental import pallas as pl
from jax.experimental.pallas import tpu as pltpu
from jax.sharding import PartitionSpec as P

EPSILON = 1e-05
LANES = 128
F32 = jnp.float32
BF16 = jnp.bfloat16
I32 = jnp.int32


def mm(a, b):
    return jnp.dot(a, b, preferred_element_type=F32)


def mm_t(a, b):
    return lax.dot_general(a, b, (((1,), (1,)), ((), ())), preferred_element_type=F32)


def sigmoid(v):
    return 0.5 + 0.5 * jnp.tanh(0.5 * v)


def ceil_to(n, k):
    return (n + k - 1) // k * k


def to_columns(row):
    n = row.shape[1]
    parts = []
    for i in range(0, n, LANES):
        parts.append(jnp.broadcast_to(row[:, i : i + LANES], (LANES, LANES)).T)
    return jnp.concatenate(parts, axis=0)


def pick(columns, first, width):
    lane = lax.broadcasted_iota(I32, columns.shape, 1)
    parts = []
    for i in range(0, width, LANES):
        parts.append(jnp.where(columns == lane + (first + i), 1.0, 0.0).astype(BF16))
    return parts[0] if len(parts) == 1 else jnp.concatenate(parts, axis=1)


def spread(row, first, height):
    shape = (height, row.shape[1])
    return jnp.where(row == lax.broadcasted_iota(I32, shape, 0) + first, 1.0, 0.0).astype(BF16)


def live_targets(target, count):
    slot = lax.broadcasted_iota(I32, target.shape, 1)
    return jnp.where(slot < count, target, -1)


def normalise(values):
    center = values - jnp.mean(values, axis=-1, keepdims=True)
    inverse = lax.rsqrt(jnp.mean(center * center, axis=-1, keepdims=True) + EPSILON)
    return center * inverse, inverse


def normalise_back(scaled, normed, inverse):
    return inverse * (
        scaled
        - jnp.mean(scaled, axis=-1, keepdims=True)
        - normed * jnp.mean(scaled * normed, axis=-1, keepdims=True)
    )


def halves(rows, even):
    half = rows.shape[1] // 2
    first, second = rows[:, :half], rows[:, half:]
    return jnp.where(even, second, first), jnp.where(even, first, second)


def coarse_slots(sender, mesh_rows, coarse, me, groups):
    offset = sender - mesh_rows
    owner = offset // coarse
    row = offset - owner * coarse
    step = me - owner
    step = jnp.where(step < 0, step + groups, step)
    moved = jnp.where(step == 0, row, mesh_rows + (step - 1) * coarse + row)
    return jnp.where(offset < 0, sender, moved)


def select_kernel(place, halo, grid, near, far):
    even = place[0] == 0
    rows_near, rows_far = halves(halo[...], even)
    table = grid[...]
    near[...] = mm(pick(to_columns(rows_near), 0, table.shape[0]), table).astype(BF16)
    far[...] = mm(pick(to_columns(rows_far), 0, table.shape[0]), table).astype(BF16)


def encode_local_kernel(
    sender, target, count, grid, mesh, w_source, w_dest, preact, send_col, target_col
):
    send_col[...] = to_columns(sender[...])
    target_col[...] = to_columns(live_targets(target[...], count[0]))
    rows = grid.shape[0]
    source = mm(grid[...], w_source[...]).astype(BF16)
    dest = mm(mesh[...], w_dest[...]).astype(BF16)
    preact[...] = mm(pick(send_col[...], 0, rows), source) + mm(
        pick(target_col[...], 0, mesh.shape[0]), dest
    )


def encode_halo_kernel(
    grid_rows,
    place,
    count,
    near,
    far,
    part,
    send_col,
    target,
    mesh16,
    w_source,
    w_out,
    gain,
    hidden,
    slope,
    updated16,
):
    even = place[0] == 0
    rim = near.shape[0]
    source = mm(jnp.concatenate([near[...], far[...]], axis=0), w_source[...]).astype(BF16)
    near_first = jnp.where(even, grid_rows + rim, grid_rows)
    far_first = jnp.where(even, grid_rows, grid_rows + rim)
    chooser = jnp.concatenate(
        [pick(send_col[...], near_first, rim), pick(send_col[...], far_first, rim)], axis=1
    )
    preact = part[...] + mm(chooser, source)
    logistic = sigmoid(preact)
    hid = (preact * logistic).astype(BF16)
    hidden[...] = hid
    slope[...] = (logistic * (1.0 + preact * (1.0 - logistic))).astype(BF16)
    coarse = mesh16.shape[0]
    live = live_targets(target[...], count[0])
    summed = mm(spread(live, 0, coarse), hid).astype(BF16)
    normed, _ = normalise(mm(summed, w_out[...]))
    updated16[...] = (mesh16[...].astype(F32) + normed * gain[...]).astype(BF16)


def process_local_kernel(
    groups,
    coarse,
    place,
    count,
    process_count,
    hidden,
    target,
    mesh,
    sender2,
    target2,
    w_out,
    gain,
    w_source,
    w_dest,
    normed_ref,
    inverse_ref,
    part,
    send_col,
    target_col,
):
    rows = mesh.shape[0]
    moved = coarse_slots(sender2[...], rows, coarse, place[1], groups)
    send_col[...] = to_columns(moved)
    target_col[...] = to_columns(live_targets(target2[...], process_count[0]))
    live = live_targets(target[...], count[0])
    summed = mm(spread(live, 0, rows), hidden[...]).astype(BF16)
    normed, inverse = normalise(mm(summed, w_out[...]))
    normed_ref[...] = normed
    inverse_ref[...] = jnp.broadcast_to(inverse, inverse_ref.shape)
    updated = (mesh[...].astype(F32) + normed * gain[...]).astype(BF16)
    source = mm(updated, w_source[...]).astype(BF16)
    dest = mm(updated, w_dest[...]).astype(BF16)
    part[...] = mm(pick(send_col[...], 0, rows), source) + mm(
        pick(target_col[...], 0, rows), dest
    )


def process_kernel(
    groups,
    coarse,
    place,
    process_count,
    part,
    send_col,
    target_col,
    sender2,
    target2,
    cotangent,
    w_source,
    w_out,
    gain,
    *refs,
):
    peers = groups - 1
    received, grad_ref, returned = refs[:peers], refs[peers], refs[peers + 1 :]
    rows = cotangent.shape[0]
    width = ceil_to(peers * coarse, LANES)
    blocks = [r[...] for r in received]
    if width > peers * coarse:
        blocks.append(jnp.zeros((width - peers * coarse, w_source.shape[0]), BF16))
    source = mm(jnp.concatenate(blocks, axis=0), w_source[...]).astype(BF16)
    preact = part[...] + mm(pick(send_col[...], rows, width), source)
    logistic = sigmoid(preact)
    hid = (preact * logistic).astype(BF16)
    slope = logistic * (1.0 + preact * (1.0 - logistic))
    live = live_targets(target2[...], process_count[0])
    summed = mm(spread(live, 0, rows), hid).astype(BF16)
    normed, inverse = normalise(mm(summed, w_out[...]))
    scaled = cotangent[...].astype(F32) * gain[...]
    back = normalise_back(scaled, normed, inverse).astype(BF16)
    back = mm_t(back, w_out[...]).astype(BF16)
    grad = (mm(pick(target_col[...], 0, rows), back) * slope).astype(BF16)
    grad_ref[...] = grad
    moved = coarse_slots(sender2[...], rows, coarse, place[1], groups)
    sums = mm(spread(moved, rows, peers * coarse), grad)
    for i, out in enumerate(returned):
        out[...] = sums[i * coarse : (i + 1) * coarse].astype(BF16)


def process_back_kernel(
    groups,
    coarse,
    place,
    process_count,
    grad,
    sender2,
    target2,
    cotangent,
    w_source,
    w_dest,
    w_out,
    gain,
    normed,
    inverse,
    target_col,
    grad_local,
    raw,
):
    rows = cotangent.shape[0]
    moved = coarse_slots(sender2[...], rows, coarse, place[1], groups)
    live = live_targets(target2[...], process_count[0])
    table = mm(spread(moved, 0, rows), grad[...]).astype(BF16)
    dest = mm(spread(live, 0, rows), grad[...]).astype(BF16)
    local = cotangent[...].astype(F32) + mm_t(table, w_source[...]) + mm_t(dest, w_dest[...])
    grad_local[...] = local
    back = normalise_back(local * gain[...], normed[...], inverse[:, :1])
    fine = lax.broadcasted_iota(I32, back.shape, 0) >= coarse
    back = jnp.where(fine, back, 0.0).astype(BF16)
    back = mm_t(back, w_out[...]).astype(BF16)
    raw[...] = mm(pick(target_col[...], 0, rows), back)


def encode_back_kernel(
    groups,
    coarse,
    grid_rows,
    place,
    grad_local16,
    normed16,
    inverse16,
    raw,
    slope,
    target_col,
    sender,
    gain,
    w_source2,
    w_out,
    *refs,
):
    peers = groups - 1
    received = refs[:peers]
    grad_ref, near, far, updated16 = refs[peers:]
    total = received[0][...].astype(F32)
    for r in received[1:]:
        total = total + r[...].astype(F32)
    updated = grad_local16[...] + mm_t(total.astype(BF16), w_source2[...])
    updated16[...] = updated
    back = normalise_back(updated * gain[...], normed16[...], inverse16[:, :1]).astype(BF16)
    back = mm_t(back, w_out[...]).astype(BF16)
    back = jnp.concatenate([back, jnp.zeros((LANES - coarse, back.shape[1]), BF16)], axis=0)
    grad = ((raw[...] + mm(pick(target_col[...], 0, LANES), back)) * slope[...].astype(F32)).astype(
        BF16
    )
    grad_ref[...] = grad
    even = place[0] == 0
    rim = near.shape[0]
    near_first = jnp.where(even, grid_rows + rim, grid_rows)
    far_first = jnp.where(even, grid_rows, grid_rows + rim)
    near[...] = mm(spread(sender[...], near_first, rim), grad).astype(BF16)
    far[...] = mm(spread(sender[...], far_first, rim), grad).astype(BF16)


def own_back_kernel(
    count, grad, sender, target, grad_local, updated16, w_source, w_dest, mesh_grad, own
):
    coarse = updated16.shape[0]
    rows = grad_local.shape[0]
    live = live_targets(target[...], count[0])
    dest = mm(spread(live, 0, rows), grad[...]).astype(BF16)
    updated = jnp.concatenate([updated16[...], grad_local[coarse:, :]], axis=0)
    mesh_grad[...] = (updated + mm_t(dest, w_dest[...])).astype(BF16)
    source = mm(spread(sender[...], 0, own.shape[0]), grad[...]).astype(BF16)
    own[...] = mm_t(source, w_source[...])


def finish_kernel(place, halo, own, near, far, w_source, grid_grad):
    even = place[0] == 0
    rows_near, rows_far = halves(halo[...], even)
    peers = jnp.concatenate([near[...], far[...]], axis=0)
    projected = mm_t(peers, w_source[...]).astype(BF16)
    where = jnp.concatenate([rows_near, rows_far], axis=1)
    grid_grad[...] = (own[...] + mm(spread(where, 0, own.shape[0]), projected)).astype(BF16)


SMEM = pl.BlockSpec(memory_space=pltpu.SMEM)
VMEM = pl.BlockSpec(memory_space=pltpu.VMEM)


def call(kernel, name, scalars, arrays, outs, flops=0):
    args = list(scalars) + list(arrays)
    return pl.pallas_call(
        kernel,
        out_shape=[jax.ShapeDtypeStruct(s, d) for s, d in outs],
        in_specs=[SMEM] * len(scalars) + [VMEM] * len(arrays),
        out_specs=[VMEM] * len(outs),
        compiler_params=pltpu.CompilerParams(vmem_limit_bytes=24 << 20),
        cost_estimate=pl.CostEstimate(flops=flops, bytes_accessed=1 << 20, transcendentals=0),
        name=name,
    )(*args)


def pair_swaps(n):
    near = [(i, i ^ 1) for i in range(n)]
    far = [(i, (i + 1) % n if i % 2 else (i - 1) % n) for i in range(n)]
    return near, far


def on_device(
    grid_latent,
    mesh_latent,
    cotangent,
    halo_rows,
    encoder_sender,
    encoder_target,
    encoder_count,
    process_sender,
    process_target,
    process_count,
    encoder_source,
    encoder_dest,
    encoder_output,
    encoder_gain,
    process_source,
    process_dest,
    process_output,
    process_gain,
):
    patches, groups = lax.axis_size("patch"), lax.axis_size("group")
    near_swap, far_swap = pair_swaps(patches)
    grid_rows, width = grid_latent.shape
    mesh_rows = mesh_latent.shape[0]
    hidden_size = encoder_source.shape[1]
    coarse = mesh_rows // 16
    rim = halo_rows.shape[0] // 2
    slots, slots2 = encoder_sender.shape[0], process_sender.shape[0]
    halo = halo_rows[None]
    sender, target = encoder_sender[None], encoder_target[None]
    sender2, target2 = process_sender[None], process_target[None]
    gain, gain2 = encoder_gain[None], process_gain[None]
    place = jnp.stack([lax.axis_index("patch") % 2, lax.axis_index("group")]).astype(I32)
    big = 1 << 30

    near, far = call(
        select_kernel, "select", [place], [halo, grid_latent], [((rim, width), BF16)] * 2
    )
    far = lax.ppermute(far, "patch", far_swap)
    near = lax.ppermute(near, "patch", near_swap)
    part, send_col, target_col = call(
        lambda c, s, t, *r: encode_local_kernel(s, t, c, *r),
        "encode_local",
        [encoder_count],
        [sender, target, grid_latent, mesh_latent, encoder_source, encoder_dest],
        [((slots, hidden_size), F32), ((slots, LANES), I32), ((slots, LANES), I32)],
        big,
    )
    mesh16 = mesh_latent[:coarse]
    hidden, slope, updated16 = call(
        functools.partial(encode_halo_kernel, grid_rows),
        "encode_halo",
        [place, encoder_count],
        [near, far, part, send_col, target, mesh16, encoder_source, encoder_output, gain],
        [((slots, hidden_size), BF16), ((slots, hidden_size), BF16), ((coarse, width), BF16)],
    )
    shifts = [
        lax.ppermute(updated16, "group", [(i, (i + k) % groups) for i in range(groups)])
        for k in range(1, groups)
    ]
    normed, inverse, part2, send_col2, target_col2 = call(
        functools.partial(process_local_kernel, groups, coarse),
        "process_local",
        [place, encoder_count, process_count],
        [
            hidden,
            target,
            mesh_latent,
            sender2,
            target2,
            encoder_output,
            gain,
            process_source,
            process_dest,
        ],
        [
            ((mesh_rows, width), F32),
            ((mesh_rows, LANES), F32),
            ((slots2, hidden_size), F32),
            ((slots2, LANES), I32),
            ((slots2, LANES), I32),
        ],
        big,
    )
    grad2, *pieces = call(
        functools.partial(process_kernel, groups, coarse),
        "process",
        [place, process_count],
        [
            part2,
            send_col2,
            target_col2,
            sender2,
            target2,
            cotangent,
            process_source,
            process_output,
            gain2,
            *shifts,
        ],
        [((slots2, hidden_size), BF16)] + [((coarse, hidden_size), BF16)] * (groups - 1),
    )
    pieces = [
        lax.ppermute(piece, "group", [(i, (i - k) % groups) for i in range(groups)])
        for k, piece in enumerate(pieces, 1)
    ]
    grad_local, raw = call(
        functools.partial(process_back_kernel, groups, coarse),
        "process_back",
        [place, process_count],
        [
            grad2,
            sender2,
            target2,
            cotangent,
            process_source,
            process_dest,
            encoder_output,
            gain,
            normed,
            inverse,
            target_col,
        ],
        [((mesh_rows, width), F32), ((slots, hidden_size), F32)],
        big,
    )
    grad, near, far, grad16 = call(
        functools.partial(encode_back_kernel, groups, coarse, grid_rows),
        "encode_back",
        [place],
        [
            grad_local[:coarse],
            normed[:coarse],
            inverse[:coarse],
            raw,
            slope,
            target_col,
            sender,
            gain,
            process_source,
            encoder_output,
            *pieces,
        ],
        [((slots, hidden_size), BF16)] + [((rim, hidden_size), BF16)] * 2 + [((coarse, width), F32)],
    )
    far = lax.ppermute(far, "patch", far_swap)
    near = lax.ppermute(near, "patch", near_swap)
    mesh_grad, own = call(
        own_back_kernel,
        "own_back",
        [encoder_count],
        [grad, sender, target, grad_local, grad16, encoder_source, encoder_dest],
        [((mesh_rows, width), BF16), ((grid_rows, width), F32)],
        big,
    )
    (grid_grad,) = call(
        finish_kernel,
        "finish",
        [place],
        [halo, own, near, far, encoder_source],
        [((grid_rows, width), BF16)],
    )
    return grid_grad, mesh_grad


def solution(mesh):
    rows, flat, whole = P(("patch", "group"), None), P(("patch", "group")), P()
    return jax.shard_map(
        on_device,
        mesh=mesh,
        in_specs=(rows,) * 3 + (flat,) * 7 + (whole,) * 8,
        out_specs=(rows, rows),
        check_vma=False,
    )
```

time: 109 us -> 49.8 us (0.46)
  matrix products: 22.2 us -> 0 us
  Pallas kernels: 0 us -> 16.3 us
  blocking collectives: 14.3 us -> 0 us
  between operations: 15.9 us -> 2.14 us
  local copies, waits for them, and re-layouts: 22.4 us -> 9.33 us
  waiting for transfers between devices: 20.1 us -> 8.79 us
  starting transfers between devices: 6.2 us -> 12.7 us
  other arithmetic: 6.52 us -> 0.08 us
    dot_general x17 -> x0, matrix products: 22.2 us -> none  [the longest x2 6.96 us: edge_backward(): jnp.dot(grad_message, out_weight.T, preferred_element_type=jnp.float32)]
    gather x7 -> x0, local copies, waits for them, and re-layouts: 20.8 us -> none  [the longest x4 12.5 us: edge_forward(): preact = source[sender] + dest_proj[target]]
    reduce_scatter x1 -> x0, waiting for transfers between devices: 17.9 us -> none  [on_device(): lax.psum_scatter(jnp.dot(grad_coarse, back_weight, precision=lax.Precisio...]
    pallas_call x0 -> x9, Pallas kernels: none -> 16.3 us  [call(): pl.pallas_call(kernel, out_shape=[jax.ShapeDtypeStruct(s, d) for s, d in...]
    all_gather x1 -> x0, blocking collectives: 14.3 us -> none  [on_device(): lax.all_gather(updated[:coarse_rows], 'group', axis=0, tiled=True)]
    ppermute x4 -> x10, waiting for transfers between devices: 2.18 us -> 8.79 us  [the longest x2 4.5 us: on_device(): far = lax.ppermute(far, 'patch', far_swap)]
    ppermute x4 -> x10, starting transfers between devices: 6.16 us -> 12.7 us  [the longest x3 4.68 us: on_device(): lax.ppermute(updated16, 'group', [(i, (i + k) % groups) for i in range(gr...]
    unnamed x54 -> x34, local copies, waits for them, and re-layouts: 1.59 us -> 5.85 us
  transfers between devices with their start and end apart: 5 -> 10, of which waited for: 2 -> 5; matrix products, arithmetic and copies ran while one was open for 5% -> 7% of each run, Pallas kernels for 0% -> 14%
where the time goes in v1:
time: 49.8 us; the launch traced here: 49.3 us
  Pallas kernels  16.3 us (33%)
  starting transfers between devices  12.7 us (26%)
  local copies, waits for them, and re-layouts  9.33 us (19%)
  waiting for transfers between devices  8.79 us (18%)
  between operations  2.14 us (4%)
    pallas_call x9, Pallas kernels, call(): pl.pallas_call(kernel, out_shape=[jax.ShapeDtypeStruct(s, d) for s, d in...  16.3 us
    unnamed x34, local copies, waits for them, and re-layouts  5.85 us
    ppermute x3, starting transfers between devices, on_device(): lax.ppermute(updated16, 'group', [(i, (i + k) % groups) for i in range(gr...  4.68 us
    ppermute x2, waiting for transfers between devices, on_device(): far = lax.ppermute(far, 'patch', far_swap)  4.5 us
    ppermute x2, starting transfers between devices, on_device(): far = lax.ppermute(far, 'patch', far_swap)  4.15 us
    ppermute x3, starting transfers between devices, on_device(): lax.ppermute(piece, 'group', [(i, (i - k) % groups) for i in range(groups)])  3.2 us
    ppermute x3, waiting for transfers between devices, on_device(): lax.ppermute(updated16, 'group', [(i, (i + k) % groups) for i in range(gr...  2.17 us
    ppermute x3, waiting for transfers between devices, on_device(): lax.ppermute(piece, 'group', [(i, (i - k) % groups) for i in range(groups)])  2.12 us
  transfers between devices with their start and end apart: 10, of which 5 were waited for; matrix products, arithmetic and copies ran while one was open for 7% of the time, Pallas kernels for 14%

profile of v1, /device:TPU:0, one launch (start us, length us, event | category | flops | bytes accessed | tf_op | source)
XLA Modules:
  0.0 49.3 jit_solution(3855563813518976636)
XLA Ops:
  0.7 1.0 %copy-done.4 = bf16[512,512]{1,0:T(8,128)(2,1)S(1)} copy-done((bf16[512,512]{1,0:T(8,128)(2,1)S(1)}, bf16[512,512]{1,0:T(8,128)(2,1)}, u32[]{:S(2)}) %copy-start.4) | copy-done | bytes 524312
  1.8 0.7 %copy-done.9 = s32[256]{0:T(256)S(1)} copy-done((s32[256]{0:T(256)S(1)}, s32[256]{0:T(256)}, u32[]{:S(2)}) %copy-start.9) | copy-done | bytes 1048
  2.4 0.9 %select.3 = (bf16[128,512]{1,0:T(8,128)(2,1)S(1)}, bf16[128,512]{1,0:T(8,128)(2,1)S(1)}) custom-call(s32[2]{0:T(128)S(1)} %pad_add_fusion.place, s32[1,256]{1,0:T(1,128)S(1)} %bitcast.9, bf16[512,512]{1,0:T(8,128)(2,1)S(1)} %copy-done.4), custom_call_target="tpu_custom_call" | custom-call | bytes 1048576 | tf_op jit(solution)/shard_map/select/pallas_call | solution.py:328
  3.3 0.6 %collective-permute-start = (bf16[128,512]{1,0:T(8,128)(2,1)S(1)}, bf16[128,512]{1,0:T(8,128)(2,1)S(1)}, u32[]{:S(2)}, u32[]{:S(2)}) collective-permute-start(bf16[128,512]{1,0:T(8,128)(2,1)S(1)} %get-tuple-element.27), channel_id=1, source_target_pairs={{0,4},{4,0},{8,12},{12,8},{16,20},{20,16},{24,28},{28,24},{1,5},{5... | collective-permute-start | bytes 393224 | tf_op jit(solution)/shard_map/ppermute | solution.py:384
  3.9 3.5 %collective-permute-start.1 = (bf16[128,512]{1,0:T(8,128)(2,1)S(1)}, bf16[128,512]{1,0:T(8,128)(2,1)S(1)}, u32[]{:S(2)}, u32[]{:S(2)}) collective-permute-start(bf16[128,512]{1,0:T(8,128)(2,1)S(1)} %get-tuple-element.28), channel_id=1, source_target_pairs={{0,28},{4,8},{8,4},{12,16},{16,12},{20,24},{24,20},{28,0},{1,29},{... | collective-permute-start | bytes 393224 | tf_op jit(solution)/shard_map/ppermute | solution.py:383
  8.7 0.7 %broadcast_in_dim.23.t.target = s32[1,768]{1,0:T(1,128)S(1)} reshape(s32[768]{0:T(1024)} %param.23) | data formatting | bytes 6144 | tf_op jit(solution)/shard_map/broadcast_in_dim | solution.py:374
  9.4 0.7 %broadcast_in_dim.22.s.sender = s32[1,768]{1,0:T(1,128)S(1)} reshape(s32[768]{0:T(1024)} %param.22) | data formatting | bytes 6144 | tf_op jit(solution)/shard_map/broadcast_in_dim | solution.py:374
  10.1 0.7 %broadcast_in_dim.25.sender2 = s32[1,768]{1,0:T(1,128)S(1)} reshape(s32[768]{0:T(1024)} %param.25) | data formatting | bytes 6144 | tf_op jit(solution)/shard_map/broadcast_in_dim | solution.py:375
  10.8 0.7 %broadcast_in_dim.26.target2 = s32[1,768]{1,0:T(1,128)S(1)} reshape(s32[768]{0:T(1024)} %param.26) | data formatting | bytes 6144 | tf_op jit(solution)/shard_map/broadcast_in_dim | solution.py:375
  11.5 0.7 %slice.12.mesh16 = bf16[16,512]{1,0:T(8,128)(2,1)S(1)} slice(bf16[256,512]{1,0:T(8,128)(2,1)} %mesh.1), slice={[0:16], [0:512]} | slice | bytes 32768 | tf_op jit(solution)/shard_map/slice | solution.py:393
  12.2 1.0 %copy-done.2 = bf16[512,512]{1,0:T(8,128)(2,1)S(1)} copy-done((bf16[512,512]{1,0:T(8,128)(2,1)S(1)}, bf16[512,512]{1,0:T(8,128)(2,1)}, u32[]{:S(2)}) %copy-start.2) | copy-done | bytes 524312
  13.3 1.0 %copy-done.5 = bf16[512,512]{1,0:T(8,128)(2,1)S(1)} copy-done((bf16[512,512]{1,0:T(8,128)(2,1)S(1)}, bf16[512,512]{1,0:T(8,128)(2,1)}, u32[]{:S(2)}) %copy-start.5) | copy-done | bytes 524312
  14.3 0.9 %copy-done.12 = bf16[256,512]{1,0:T(8,128)(2,1)S(1)} copy-done((bf16[256,512]{1,0:T(8,128)(2,1)S(1)}, bf16[256,512]{1,0:T(8,128)(2,1)}, u32[]{:S(2)}) %copy-start.12) | copy-done | bytes 262168
  15.2 1.0 %copy-done.15 = bf16[512,512]{1,0:T(8,128)(2,1)S(1)} copy-done((bf16[512,512]{1,0:T(8,128)(2,1)S(1)}, bf16[512,512]{1,0:T(8,128)(2,1)}, u32[]{:S(2)}) %copy-start.15) | copy-done | bytes 524312
  16.3 1.3 %encode_local.1 = (f32[768,512]{1,0:T(8,128)S(1)}, s32[768,128]{1,0:T(8,128)S(1)}, s32[768,128]{1,0:T(8,128)S(1)}) custom-call(s32[1]{0:T(128)S(6)} %copy.20.c.count, s32[1,768]{1,0:T(1,128)S(1)} %broadcast_in_dim.22.s.sender, s32[1,768]{1,0:T(1,128)S(1)} %broadcast_in_dim.23.t.target, bf16[512,512]{1,0:T(8,128)(2,1)S(1)} %copy-done.5, ...), custom_call_target="tpu_custom_call" | custom-call | flops 1073741824 | bytes 1048576 | tf_op jit(solution)/shard_map/encode_local/pallas_call | solution.py:328
  17.7 2.0 %encode_halo.1 = (bf16[768,512]{1,0:T(8,128)(2,1)S(1)}, bf16[768,512]{1,0:T(8,128)(2,1)S(1)}, bf16[16,512]{1,0:T(8,128)(2,1)S(1)}) custom-call(s32[2]{0:T(128)S(1)} %pad_add_fusion.place, s32[1]{0:T(128)S(6)} %copy.20.c.count, bf16[128,512]{1,0:T(8,128)(2,1)S(1)} %collective-permute-done.near, bf16[128,512]{1,0:T(8,128)(2,1)S(1)} %collective-permute-done.1.far, ...), custom_call_target="tpu_custom_call" | custom-call | bytes 1048576 | tf_op jit(solution)/shard_map/encode_halo/pallas_call | solution.py:328
  19.7 3.7 %collective-permute-start.4 = (bf16[16,512]{1,0:T(8,128)(2,1)S(1)}, bf16[16,512]{1,0:T(8,128)(2,1)S(1)}, u32[]{:S(2)}, u32[]{:S(2)}) collective-permute-start(bf16[16,512]{1,0:T(8,128)(2,1)S(1)} %get-tuple-element.35), channel_id=1, source_target_pairs={{0,3},{1,0},{2,1},{3,2},{4,7},{5,4},{6,5},{7,6},{8,11},{9,8},{10,9... | collective-permute-start | bytes 49160 | tf_op jit(solution)/shard_map/ppermute | solution.py:402
  23.4 1.0 %collective-permute-start.2 = (bf16[16,512]{1,0:T(8,128)(2,1)S(1)}, bf16[16,512]{1,0:T(8,128)(2,1)S(1)}, u32[]{:S(2)}, u32[]{:S(2)}) collective-permute-start(bf16[16,512]{1,0:T(8,128)(2,1)S(1)} %get-tuple-element.35), channel_id=1, source_target_pairs={{0,1},{1,2},{2,3},{3,0},{4,5},{5,6},{6,7},{7,4},{8,9},{9,10},{10,1... | collective-permute-start | bytes 49160 | tf_op jit(solution)/shard_map/ppermute | solution.py:402
  24.4 2.3 %process_local.1 = (f32[256,512]{1,0:T(8,128)S(1)}, f32[256,128]{1,0:T(8,128)S(1)}, f32[768,512]{1,0:T(8,128)S(1)}, s32[768,128]{1,0:T(8,128)S(1)}, s32[768,128]{1,0:T(8,128)S(1)}) custom-call(s32[2]{0:T(128)S(1)} %pad_add_fusion.place, s32[1]{0:T(128)S(6)} %copy.20.c.count, s32[1]{0:T(128)S(6)} %copy.21.process_count, ...), custom_call_target="tpu_custom_call" | custom-call | flops 1073741824 | bytes 1048576 | tf_op jit(solution)/shard_map/process_local/pallas_call | solution.py:328
  26.7 1.3 %collective-permute-done.3.refs_1_ = bf16[16,512]{1,0:T(8,128)(2,1)S(1)} collective-permute-done((bf16[16,512]{1,0:T(8,128)(2,1)S(1)}, bf16[16,512]{1,0:T(8,128)(2,1)S(1)}, u32[]{:S(2)}, u32[]{:S(2)}) %collective-permute-start.3) | collective-permute-done | bytes 16416 | tf_op jit(solution)/shard_map/ppermute | solution.py:402
  28.0 0.9 %collective-permute-done.2.refs_0_ = bf16[16,512]{1,0:T(8,128)(2,1)S(1)} collective-permute-done((bf16[16,512]{1,0:T(8,128)(2,1)S(1)}, bf16[16,512]{1,0:T(8,128)(2,1)S(1)}, u32[]{:S(2)}, u32[]{:S(2)}) %collective-permute-start.2) | collective-permute-done | bytes 16416 | tf_op jit(solution)/shard_map/ppermute | solution.py:402
  28.9 2.8 %process.1 = (bf16[768,512]{1,0:T(8,128)(2,1)S(1)}, bf16[16,512]{1,0:T(8,128)(2,1)S(1)}, bf16[16,512]{1,0:T(8,128)(2,1)S(1)}, bf16[16,512]{1,0:T(8,128)(2,1)S(1)}) custom-call(s32[2]{0:T(128)S(1)} %pad_add_fusion.place, s32[1]{0:T(128)S(6)} %copy.21.process_count, f32[768,512]{1,0:T(8,128)S(1)} %get-tuple-element.32.part, ...), custom_call_target="tpu_custom_call" | custom-call | bytes 1048576 | tf_op jit(solution)/shard_map/process/pallas_call | solution.py:328
  31.7 0.7 %collective-permute-start.5 = (bf16[16,512]{1,0:T(8,128)(2,1)S(1)}, bf16[16,512]{1,0:T(8,128)(2,1)S(1)}, u32[]{:S(2)}, u32[]{:S(2)}) collective-permute-start(bf16[16,512]{1,0:T(8,128)(2,1)S(1)} %get-tuple-element.43), channel_id=1, source_target_pairs={{0,3},{1,0},{2,1},{3,2},{4,7},{5,4},{6,5},{7,6},{8,11},{9,8},{10,9... | collective-permute-start | bytes 49160 | tf_op jit(solution)/shard_map/ppermute | solution.py:448
  32.4 1.1 %collective-permute-start.6 = (bf16[16,512]{1,0:T(8,128)(2,1)S(1)}, bf16[16,512]{1,0:T(8,128)(2,1)S(1)}, u32[]{:S(2)}, u32[]{:S(2)}) collective-permute-start(bf16[16,512]{1,0:T(8,128)(2,1)S(1)} %get-tuple-element.44), channel_id=1, source_target_pairs={{0,2},{1,3},{2,0},{3,1},{4,6},{5,7},{6,4},{7,5},{8,10},{9,11},{10,... | collective-permute-start | bytes 49160 | tf_op jit(solution)/shard_map/ppermute | solution.py:448
  33.6 1.3 %collective-permute-start.7 = (bf16[16,512]{1,0:T(8,128)(2,1)S(1)}, bf16[16,512]{1,0:T(8,128)(2,1)S(1)}, u32[]{:S(2)}, u32[]{:S(2)}) collective-permute-start(bf16[16,512]{1,0:T(8,128)(2,1)S(1)} %get-tuple-element.45), channel_id=1, source_target_pairs={{0,1},{1,2},{2,3},{3,0},{4,5},{5,6},{6,7},{7,4},{8,9},{9,10},{10,1... | collective-permute-start | bytes 49160 | tf_op jit(solution)/shard_map/ppermute | solution.py:448
  34.9 2.1 %process_back.1 = (f32[256,512]{1,0:T(8,128)S(1)}, f32[768,512]{1,0:T(8,128)S(1)}) custom-call(s32[2]{0:T(128)S(1)} %pad_add_fusion.place, s32[1]{0:T(128)S(6)} %copy.21.process_count, bf16[768,512]{1,0:T(8,128)(2,1)S(1)} %get-tuple-element.36.grad, s32[1,768]{1,0:T(1,128)S(1)} %broadcast_in_dim.25.sender2, s32[1,768]{1,0:T(1,128)S(1)} %broadcast_in_dim.26.target2, ...), custom_call_target="tpu_custom_call" | custom-call | flops 1073741824 | bytes 1048576 | tf_op jit(solution)/shard_map/process_back/pallas_call | solution.py:328
  37.1 2.0 %collective-permute-done.7.refs_2_ = bf16[16,512]{1,0:T(8,128)(2,1)S(1)} collective-permute-done((bf16[16,512]{1,0:T(8,128)(2,1)S(1)}, bf16[16,512]{1,0:T(8,128)(2,1)S(1)}, u32[]{:S(2)}, u32[]{:S(2)}) %collective-permute-start.7) | collective-permute-done | bytes 16416 | tf_op jit(solution)/shard_map/ppermute | solution.py:448
  39.1 1.7 %encode_back.1 = (bf16[768,512]{1,0:T(8,128)(2,1)S(1)}, bf16[128,512]{1,0:T(8,128)(2,1)S(1)}, bf16[128,512]{1,0:T(8,128)(2,1)S(1)}, f32[16,512]{1,0:T(8,128)S(1)}) custom-call(s32[2]{0:T(128)S(1)} %pad_add_fusion.place, f32[16,512]{1,0:T(8,128)S(1)} %slice.13.grad_local16, f32[16,512]{1,0:T(8,128)S(1)} %slice.14.normed16, f32[16,128]{1,0:T(8,128)S(1)} %slice.15.inverse16, ...), custom_call_target="tpu_custom_call" | custom-call | bytes 1048576 | tf_op jit(solution)/shard_map/encode_back/pallas_call | solution.py:328
  40.9 0.6 %collective-permute-start.9 = (bf16[128,512]{1,0:T(8,128)(2,1)S(1)}, bf16[128,512]{1,0:T(8,128)(2,1)S(1)}, u32[]{:S(2)}, u32[]{:S(2)}) collective-permute-start(bf16[128,512]{1,0:T(8,128)(2,1)S(1)} %get-tuple-element.50), channel_id=1, source_target_pairs={{0,28},{4,8},{8,4},{12,16},{16,12},{20,24},{24,20},{28,0},{1,29},{... | collective-permute-start | bytes 393224 | tf_op jit(solution)/shard_map/ppermute | solution.py:490
  41.6 1.3 %own_back.1 = (bf16[256,512]{1,0:T(8,128)(2,1)}, f32[512,512]{1,0:T(8,128)S(1)}) custom-call(s32[1]{0:T(128)S(6)} %copy.20.c.count, bf16[768,512]{1,0:T(8,128)(2,1)S(1)} %get-tuple-element.46.grad, s32[1,768]{1,0:T(1,128)S(1)} %broadcast_in_dim.22.s.sender, s32[1,768]{1,0:T(1,128)S(1)} %broadcast_in_dim.23.t.target, ...), custom_call_target="tpu_custom_call" | custom-call | flops 1073741824 | bytes 1048576 | tf_op jit(solution)/shard_map/own_back/pallas_call | solution.py:328
  42.9 4.5 %collective-permute-done.9.far = bf16[128,512]{1,0:T(8,128)(2,1)S(1)} collective-permute-done((bf16[128,512]{1,0:T(8,128)(2,1)S(1)}, bf16[128,512]{1,0:T(8,128)(2,1)S(1)}, u32[]{:S(2)}, u32[]{:S(2)}) %collective-permute-start.9) | collective-permute-done | bytes 131104 | tf_op jit(solution)/shard_map/ppermute | solution.py:490
  47.4 1.9 %finish.1 = bf16[512,512]{1,0:T(8,128)(2,1)} custom-call(s32[2]{0:T(128)S(1)} %pad_add_fusion.place, s32[1,256]{1,0:T(1,128)S(1)} %bitcast.10, f32[512,512]{1,0:T(8,128)S(1)} %get-tuple-element.48.own, bf16[128,512]{1,0:T(8,128)(2,1)S(1)} %collective-permute-done.8.near, bf16[128,512]{1,0:T(8,128)(2,1)S(1)} %collective-permute-done.9.far, ...), custom_call_target="tpu_custom_call" | custom-call | bytes 1048576 | tf_op jit(solution)/shard_map/finish/pallas_call | solution.py:328
  (40 shorter events, 0.3 us)
Async XLA Ops:
  0.7 1.0 %copy-start.4 = (bf16[512,512]{1,0:T(8,128)(2,1)S(1)}, bf16[512,512]{1,0:T(8,128)(2,1)}, u32[]{:S(2)}) copy-start(bf16[512,512]{1,0:T(8,128)(2,1)} %r_0_.1) | copy-start | bytes 1572868
  1.8 0.7 %copy-start.9 = (s32[256]{0:T(256)S(1)}, s32[256]{0:T(256)}, u32[]{:S(2)}) copy-start(s32[256]{0:T(256)} %param.21) | copy-start | bytes 3076
  3.3 14.3 %collective-permute-start = (bf16[128,512]{1,0:T(8,128)(2,1)S(1)}, bf16[128,512]{1,0:T(8,128)(2,1)S(1)}, u32[]{:S(2)}, u32[]{:S(2)}) collective-permute-start(bf16[128,512]{1,0:T(8,128)(2,1)S(1)} %get-tuple-element.27), channel_id=1, source_target_pairs={{0,4},{4,0},{8,12},{12,8},{16,20},{20,16},{24,28},{28,24},{1,5},{5... | collective-permute-start | bytes 393224 | tf_op jit(solution)/shard_map/ppermute | solution.py:384
  3.9 13.8 %collective-permute-start.1 = (bf16[128,512]{1,0:T(8,128)(2,1)S(1)}, bf16[128,512]{1,0:T(8,128)(2,1)S(1)}, u32[]{:S(2)}, u32[]{:S(2)}) collective-permute-start(bf16[128,512]{1,0:T(8,128)(2,1)S(1)} %get-tuple-element.28), channel_id=1, source_target_pairs={{0,28},{4,8},{8,4},{12,16},{16,12},{20,24},{24,20},{28,0},{1,29},{... | collective-permute-start | bytes 393224 | tf_op jit(solution)/shard_map/ppermute | solution.py:383
  12.2 1.0 %copy-start.2 = (bf16[512,512]{1,0:T(8,128)(2,1)S(1)}, bf16[512,512]{1,0:T(8,128)(2,1)}, u32[]{:S(2)}) copy-start(bf16[512,512]{1,0:T(8,128)(2,1)} %w_source.11) | copy-start | bytes 1572868
  13.3 1.0 %copy-start.5 = (bf16[512,512]{1,0:T(8,128)(2,1)S(1)}, bf16[512,512]{1,0:T(8,128)(2,1)}, u32[]{:S(2)}) copy-start(bf16[512,512]{1,0:T(8,128)(2,1)} %r_0_.1) | copy-start | bytes 1572868
  14.3 0.9 %copy-start.12 = (bf16[256,512]{1,0:T(8,128)(2,1)S(1)}, bf16[256,512]{1,0:T(8,128)(2,1)}, u32[]{:S(2)}) copy-start(bf16[256,512]{1,0:T(8,128)(2,1)} %mesh.1) | copy-start | bytes 786436
  15.2 1.0 %copy-start.15 = (bf16[512,512]{1,0:T(8,128)(2,1)S(1)}, bf16[512,512]{1,0:T(8,128)(2,1)}, u32[]{:S(2)}) copy-start(bf16[512,512]{1,0:T(8,128)(2,1)} %w_dest.5) | copy-start | bytes 1572868
  16.3 1.4 %copy-start = (bf16[512,512]{1,0:T(8,128)(2,1)S(1)}, bf16[512,512]{1,0:T(8,128)(2,1)}, u32[]{:S(2)}) copy-start(bf16[512,512]{1,0:T(8,128)(2,1)} %w_out.9) | copy-start | bytes 1572868
  16.3 1.4 %copy-start.3 = (bf16[512,512]{1,0:T(8,128)(2,1)S(1)}, bf16[512,512]{1,0:T(8,128)(2,1)}, u32[]{:S(2)}) copy-start(bf16[512,512]{1,0:T(8,128)(2,1)} %w_source.11) | copy-start | bytes 1572868
  16.3 1.4 %copy-start.8 = (f32[512]{0:T(512)S(1)}, f32[512]{0:T(512)}, u32[]{:S(2)}) copy-start(f32[512]{0:T(512)} %param.31) | copy-start | bytes 6148
  17.7 6.7 %copy-start.1 = (bf16[512,512]{1,0:T(8,128)(2,1)S(1)}, bf16[512,512]{1,0:T(8,128)(2,1)}, u32[]{:S(2)}) copy-start(bf16[512,512]{1,0:T(8,128)(2,1)} %w_source2.1) | copy-start | bytes 1572868
  17.7 6.7 %copy-start.13 = (bf16[256,512]{1,0:T(8,128)(2,1)S(1)}, bf16[256,512]{1,0:T(8,128)(2,1)}, u32[]{:S(2)}) copy-start(bf16[256,512]{1,0:T(8,128)(2,1)} %mesh.1) | copy-start | bytes 786436
  17.7 6.7 %copy-start.14 = (bf16[512,512]{1,0:T(8,128)(2,1)S(1)}, bf16[512,512]{1,0:T(8,128)(2,1)}, u32[]{:S(2)}) copy-start(bf16[512,512]{1,0:T(8,128)(2,1)} %w_dest.4) | copy-start | bytes 1572868
  19.7 7.0 %collective-permute-start.4 = (bf16[16,512]{1,0:T(8,128)(2,1)S(1)}, bf16[16,512]{1,0:T(8,128)(2,1)S(1)}, u32[]{:S(2)}, u32[]{:S(2)}) collective-permute-start(bf16[16,512]{1,0:T(8,128)(2,1)S(1)} %get-tuple-element.35), channel_id=1, source_target_pairs={{0,3},{1,0},{2,1},{3,2},{4,7},{5,4},{6,5},{7,6},{8,11},{9,8},{10,9... | collective-permute-start | bytes 49160 | tf_op jit(solution)/shard_map/ppermute | solution.py:402
  23.4 4.6 %collective-permute-start.3 = (bf16[16,512]{1,0:T(8,128)(2,1)S(1)}, bf16[16,512]{1,0:T(8,128)(2,1)S(1)}, u32[]{:S(2)}, u32[]{:S(2)}) collective-permute-start(bf16[16,512]{1,0:T(8,128)(2,1)S(1)} %get-tuple-element.35), channel_id=1, source_target_pairs={{0,2},{1,3},{2,0},{3,1},{4,6},{5,7},{6,4},{7,5},{8,10},{9,11},{10,... | collective-permute-start | bytes 49160 | tf_op jit(solution)/shard_map/ppermute | solution.py:402
  23.4 5.5 %collective-permute-start.2 = (bf16[16,512]{1,0:T(8,128)(2,1)S(1)}, bf16[16,512]{1,0:T(8,128)(2,1)S(1)}, u32[]{:S(2)}, u32[]{:S(2)}) collective-permute-start(bf16[16,512]{1,0:T(8,128)(2,1)S(1)} %get-tuple-element.35), channel_id=1, source_target_pairs={{0,1},{1,2},{2,3},{3,0},{4,5},{5,6},{6,7},{7,4},{8,9},{9,10},{10,1... | collective-permute-start | bytes 49160 | tf_op jit(solution)/shard_map/ppermute | solution.py:402
  24.4 4.5 %copy-start.6 = (bf16[512,512]{1,0:T(8,128)(2,1)S(1)}, bf16[512,512]{1,0:T(8,128)(2,1)}, u32[]{:S(2)}) copy-start(bf16[512,512]{1,0:T(8,128)(2,1)} %w_out.7) | copy-start | bytes 1572868
  24.4 4.5 %copy-start.7 = (bf16[256,512]{1,0:T(8,128)(2,1)S(1)}, bf16[256,512]{1,0:T(8,128)(2,1)}, u32[]{:S(2)}) copy-start(bf16[256,512]{1,0:T(8,128)(2,1)} %cotangent.3) | copy-start | bytes 786436
  24.4 4.5 %copy-start.11 = (f32[512]{0:T(512)S(1)}, f32[512]{0:T(512)}, u32[]{:S(2)}) copy-start(f32[512]{0:T(512)} %param.35) | copy-start | bytes 6148
  31.7 5.3 %collective-permute-start.5 = (bf16[16,512]{1,0:T(8,128)(2,1)S(1)}, bf16[16,512]{1,0:T(8,128)(2,1)S(1)}, u32[]{:S(2)}, u32[]{:S(2)}) collective-permute-start(bf16[16,512]{1,0:T(8,128)(2,1)S(1)} %get-tuple-element.43), channel_id=1, source_target_pairs={{0,3},{1,0},{2,1},{3,2},{4,7},{5,4},{6,5},{7,6},{8,11},{9,8},{10,9... | collective-permute-start | bytes 49160 | tf_op jit(solution)/shard_map/ppermute | solution.py:448
  32.4 4.6 %collective-permute-start.6 = (bf16[16,512]{1,0:T(8,128)(2,1)S(1)}, bf16[16,512]{1,0:T(8,128)(2,1)S(1)}, u32[]{:S(2)}, u32[]{:S(2)}) collective-permute-start(bf16[16,512]{1,0:T(8,128)(2,1)S(1)} %get-tuple-element.44), channel_id=1, source_target_pairs={{0,2},{1,3},{2,0},{3,1},{4,6},{5,7},{6,4},{7,5},{8,10},{9,11},{10,... | collective-permute-start | bytes 49160 | tf_op jit(solution)/shard_map/ppermute | solution.py:448
  33.6 5.5 %collective-permute-start.7 = (bf16[16,512]{1,0:T(8,128)(2,1)S(1)}, bf16[16,512]{1,0:T(8,128)(2,1)S(1)}, u32[]{:S(2)}, u32[]{:S(2)}) collective-permute-start(bf16[16,512]{1,0:T(8,128)(2,1)S(1)} %get-tuple-element.45), channel_id=1, source_target_pairs={{0,1},{1,2},{2,3},{3,0},{4,5},{5,6},{6,7},{7,4},{8,9},{9,10},{10,1... | collective-permute-start | bytes 49160 | tf_op jit(solution)/shard_map/ppermute | solution.py:448
  39.1 2.4 %copy-start.16 = (bf16[512,512]{1,0:T(8,128)(2,1)S(1)}, bf16[512,512]{1,0:T(8,128)(2,1)}, u32[]{:S(2)}) copy-start(bf16[512,512]{1,0:T(8,128)(2,1)} %w_dest.5) | copy-start | bytes 1572868
  40.9 2.0 %collective-permute-start.8 = (bf16[128,512]{1,0:T(8,128)(2,1)S(1)}, bf16[128,512]{1,0:T(8,128)(2,1)S(1)}, u32[]{:S(2)}, u32[]{:S(2)}) collective-permute-start(bf16[128,512]{1,0:T(8,128)(2,1)S(1)} %get-tuple-element.49), channel_id=1, source_target_pairs={{0,4},{4,0},{8,12},{12,8},{16,20},{20,16},{24,28},{28,24},{1,5},{5... | collective-permute-start | bytes 393224 | tf_op jit(solution)/shard_map/ppermute | solution.py:491
  40.9 6.4 %collective-permute-start.9 = (bf16[128,512]{1,0:T(8,128)(2,1)S(1)}, bf16[128,512]{1,0:T(8,128)(2,1)S(1)}, u32[]{:S(2)}, u32[]{:S(2)}) collective-permute-start(bf16[128,512]{1,0:T(8,128)(2,1)S(1)} %get-tuple-element.50), channel_id=1, source_target_pairs={{0,28},{4,8},{8,4},{12,16},{16,12},{20,24},{24,20},{28,0},{1,29},{... | collective-permute-start | bytes 393224 | tf_op jit(solution)/shard_map/ppermute | solution.py:490
  41.6 5.8 %copy-start.10 = (s32[256]{0:T(256)S(1)}, s32[256]{0:T(256)}, u32[]{:S(2)}) copy-start(s32[256]{0:T(256)} %param.21) | copy-start | bytes 3076

commit v2 on v1

v2 whole, which is shorter than its diff:
```python
import functools

import jax
import jax.numpy as jnp
from jax import lax
from jax.experimental import pallas as pl
from jax.experimental.pallas import tpu as pltpu
from jax.sharding import PartitionSpec as P

EPSILON = 1e-05
LANES = 128
F32 = jnp.float32
BF16 = jnp.bfloat16
I32 = jnp.int32


def mm(a, b):
    return jnp.dot(a, b, preferred_element_type=F32)


def mm_t(a, b):
    return lax.dot_general(a, b, (((1,), (1,)), ((), ())), preferred_element_type=F32)


def sigmoid(v):
    return 0.5 + 0.5 * jnp.tanh(0.5 * v)


def ceil_to(n, k):
    return (n + k - 1) // k * k


def to_columns(row):
    n = row.shape[1]
    parts = []
    for i in range(0, n, LANES):
        parts.append(jnp.broadcast_to(row[:, i : i + LANES], (LANES, LANES)).T)
    return jnp.concatenate(parts, axis=0)


def pick(columns, first, width):
    lane = lax.broadcasted_iota(I32, columns.shape, 1)
    parts = []
    for i in range(0, width, LANES):
        parts.append(jnp.where(columns == lane + (first + i), 1.0, 0.0).astype(BF16))
    return parts[0] if len(parts) == 1 else jnp.concatenate(parts, axis=1)


def spread(row, first, height):
    shape = (height, row.shape[1])
    return jnp.where(row == lax.broadcasted_iota(I32, shape, 0) + first, 1.0, 0.0).astype(BF16)


def live_targets(target, count):
    slot = lax.broadcasted_iota(I32, target.shape, 1)
    return jnp.where(slot < count, target, -1)


def normalise(values):
    center = values - jnp.mean(values, axis=-1, keepdims=True)
    inverse = lax.rsqrt(jnp.mean(center * center, axis=-1, keepdims=True) + EPSILON)
    return center * inverse, inverse


def normalise_back(scaled, normed, inverse):
    return inverse * (
        scaled
        - jnp.mean(scaled, axis=-1, keepdims=True)
        - normed * jnp.mean(scaled * normed, axis=-1, keepdims=True)
    )


def halves(rows, even):
    half = rows.shape[1] // 2
    first, second = rows[:, :half], rows[:, half:]
    return jnp.where(even, second, first), jnp.where(even, first, second)


def coarse_slots(sender, mesh_rows, coarse, me, groups):
    offset = sender - mesh_rows
    owner = offset // coarse
    row = offset - owner * coarse
    step = me - owner
    step = jnp.where(step < 0, step + groups, step)
    moved = jnp.where(step == 0, row, mesh_rows + (step - 1) * coarse + row)
    return jnp.where(offset < 0, sender, moved)


def even_patch():
    return lax.rem(lax.axis_index("patch"), 2) == 0


def as_row(ref):
    return ref[...].reshape(1, ref.shape[0])


def select_kernel(halo_hbm, grid_hbm, near, far, table, halo, sems):
    copies = [
        pltpu.make_async_copy(halo_hbm, halo, sems.at[0]),
        pltpu.make_async_copy(grid_hbm, table, sems.at[1]),
    ]
    for copy in copies:
        copy.start()
    copies[0].wait()
    rows_near, rows_far = halves(as_row(halo), even_patch())
    pick_near = pick(to_columns(rows_near), 0, table.shape[0])
    pick_far = pick(to_columns(rows_far), 0, table.shape[0])
    copies[1].wait()
    near[...] = mm(pick_near, table[...]).astype(BF16)
    far[...] = mm(pick_far, table[...]).astype(BF16)


def encode_local_kernel(
    groups,
    coarse,
    counts,
    sender,
    target,
    sender2,
    target2,
    grid,
    mesh,
    w_source,
    w_dest,
    part,
    send_row,
    send_col,
    live_row,
    live_col,
    send_row2,
    send_col2,
    live_row2,
    live_col2,
):
    rows = mesh.shape[0]
    send_row[...] = as_row(sender)
    send_col[...] = to_columns(as_row(sender))
    send_row2[...] = coarse_slots(as_row(sender2), rows, coarse, lax.axis_index("group"), groups)
    send_col2[...] = to_columns(send_row2[...])
    source = mm(grid[...], w_source[...]).astype(BF16)
    dest = mm(mesh[...], w_dest[...]).astype(BF16)
    live_row[...] = live_targets(as_row(target), counts[0])
    live_col[...] = to_columns(live_row[...])
    live_row2[...] = live_targets(as_row(target2), counts[1])
    live_col2[...] = to_columns(live_row2[...])
    part[...] = mm(pick(send_col[...], 0, grid.shape[0]), source) + mm(
        pick(live_col[...], 0, rows), dest
    )


def rim_starts(grid_rows, rim):
    even = even_patch()
    return (
        jnp.where(even, grid_rows + rim, grid_rows),
        jnp.where(even, grid_rows, grid_rows + rim),
    )


def encode_halo_kernel(
    grid_rows,
    coarse,
    near,
    far,
    part,
    send_col,
    live_row,
    mesh,
    w_source,
    w_out,
    gain,
    hidden,
    slope,
    updated16,
):
    rim = near.shape[0]
    source = mm(jnp.concatenate([near[...], far[...]], axis=0), w_source[...]).astype(BF16)
    near_first, far_first = rim_starts(grid_rows, rim)
    chooser = jnp.concatenate(
        [pick(send_col[...], near_first, rim), pick(send_col[...], far_first, rim)], axis=1
    )
    preact = part[...] + mm(chooser, source)
    logistic = sigmoid(preact)
    hid = (preact * logistic).astype(BF16)
    hidden[...] = hid
    slope[...] = (logistic * (1.0 + preact * (1.0 - logistic))).astype(BF16)
    summed = mm(spread(live_row[...], 0, coarse), hid).astype(BF16)
    normed, _ = normalise(mm(summed, w_out[...]))
    updated16[...] = (mesh[:coarse, :].astype(F32) + normed * as_row(gain)).astype(BF16)


def process_local_kernel(
    hidden,
    live_row,
    mesh,
    send_col2,
    live_col2,
    w_out,
    gain,
    w_source,
    w_dest,
    normed_ref,
    inverse_ref,
    part,
):
    rows = mesh.shape[0]
    summed = mm(spread(live_row[...], 0, rows), hidden[...]).astype(BF16)
    normed, inverse = normalise(mm(summed, w_out[...]))
    normed_ref[...] = normed
    inverse_ref[...] = jnp.broadcast_to(inverse, inverse_ref.shape)
    updated = (mesh[...].astype(F32) + normed * as_row(gain)).astype(BF16)
    source = mm(updated, w_source[...]).astype(BF16)
    dest = mm(updated, w_dest[...]).astype(BF16)
    part[...] = mm(pick(send_col2[...], 0, rows), source) + mm(pick(live_col2[...], 0, rows), dest)


def process_kernel(
    groups,
    coarse,
    part,
    send_row2,
    send_col2,
    live_row2,
    live_col2,
    cotangent,
    w_source,
    w_out,
    gain,
    *refs,
):
    peers = groups - 1
    received, grad_ref, returned = refs[:peers], refs[peers], refs[peers + 1 :]
    rows = cotangent.shape[0]
    width = ceil_to(peers * coarse, LANES)
    blocks = [r[...] for r in received]
    if width > peers * coarse:
        blocks.append(jnp.zeros((width - peers * coarse, w_source.shape[0]), BF16))
    source = mm(jnp.concatenate(blocks, axis=0), w_source[...]).astype(BF16)
    preact = part[...] + mm(pick(send_col2[...], rows, width), source)
    logistic = sigmoid(preact)
    hid = (preact * logistic).astype(BF16)
    slope = logistic * (1.0 + preact * (1.0 - logistic))
    summed = mm(spread(live_row2[...], 0, rows), hid).astype(BF16)
    normed, inverse = normalise(mm(summed, w_out[...]))
    scaled = cotangent[...].astype(F32) * as_row(gain)
    back = normalise_back(scaled, normed, inverse).astype(BF16)
    back = mm_t(back, w_out[...]).astype(BF16)
    grad = (mm(pick(live_col2[...], 0, rows), back) * slope).astype(BF16)
    grad_ref[...] = grad
    sums = mm(spread(send_row2[...], rows, peers * coarse), grad)
    for i, out in enumerate(returned):
        out[...] = sums[i * coarse : (i + 1) * coarse].astype(BF16)


def process_back_kernel(
    coarse,
    grad,
    send_row2,
    live_row2,
    cotangent,
    w_source,
    w_dest,
    w_out,
    gain,
    normed,
    inverse,
    live_col,
    grad_local,
    raw,
):
    rows = cotangent.shape[0]
    table = mm(spread(send_row2[...], 0, rows), grad[...]).astype(BF16)
    dest = mm(spread(live_row2[...], 0, rows), grad[...]).astype(BF16)
    local = cotangent[...].astype(F32) + mm_t(table, w_source[...]) + mm_t(dest, w_dest[...])
    grad_local[...] = local
    back = normalise_back(local * as_row(gain), normed[...], inverse[:, :1])
    fine = lax.broadcasted_iota(I32, back.shape, 0) >= coarse
    back = jnp.where(fine, back, 0.0).astype(BF16)
    back = mm_t(back, w_out[...]).astype(BF16)
    raw[...] = mm(pick(live_col[...], 0, rows), back)


def encode_back_kernel(
    groups,
    coarse,
    grid_rows,
    grad_local,
    normed,
    inverse,
    raw,
    slope,
    live_col,
    send_row,
    gain,
    w_source2,
    w_out,
    *refs,
):
    peers = groups - 1
    received = refs[:peers]
    grad_ref, near, far, updated16 = refs[peers:]
    total = received[0][...].astype(F32)
    for r in received[1:]:
        total = total + r[...].astype(F32)
    updated = grad_local[:coarse, :] + mm_t(total.astype(BF16), w_source2[...])
    updated16[...] = updated
    back = normalise_back(updated * as_row(gain), normed[:coarse, :], inverse[:coarse, :1])
    back = mm_t(back.astype(BF16), w_out[...]).astype(BF16)
    back = jnp.concatenate([back, jnp.zeros((LANES - coarse, back.shape[1]), BF16)], axis=0)
    more = mm(pick(live_col[...], 0, LANES), back)
    grad = ((raw[...] + more) * slope[...].astype(F32)).astype(BF16)
    grad_ref[...] = grad
    rim = near.shape[0]
    near_first, far_first = rim_starts(grid_rows, rim)
    near[...] = mm(spread(send_row[...], near_first, rim), grad).astype(BF16)
    far[...] = mm(spread(send_row[...], far_first, rim), grad).astype(BF16)


def own_back_kernel(
    grad, send_row, live_row, grad_local, updated16, w_source, w_dest, mesh_grad, own
):
    coarse = updated16.shape[0]
    rows = grad_local.shape[0]
    dest = mm(spread(live_row[...], 0, rows), grad[...]).astype(BF16)
    updated = jnp.concatenate([updated16[...], grad_local[coarse:, :]], axis=0)
    mesh_grad[...] = (updated + mm_t(dest, w_dest[...])).astype(BF16)
    source = mm(spread(send_row[...], 0, own.shape[0]), grad[...]).astype(BF16)
    own[...] = mm_t(source, w_source[...])


def finish_kernel(halo, own, near, far, w_source, grid_grad):
    rows_near, rows_far = halves(as_row(halo), even_patch())
    peers = jnp.concatenate([near[...], far[...]], axis=0)
    projected = mm_t(peers, w_source[...]).astype(BF16)
    where = jnp.concatenate([rows_near, rows_far], axis=1)
    grid_grad[...] = (own[...] + mm(spread(where, 0, own.shape[0]), projected)).astype(BF16)


SMEM = pl.BlockSpec(memory_space=pltpu.SMEM)
HBM = pl.BlockSpec(memory_space=pltpu.HBM)
VMEM = pl.BlockSpec(memory_space=pltpu.VMEM)
MICROSECOND = 1 << 30


def call(kernel, name, arrays, outs, cost, raw=0, scalars=0, scratch=()):
    return pl.pallas_call(
        kernel,
        out_shape=[jax.ShapeDtypeStruct(s, d) for s, d in outs],
        in_specs=[HBM] * raw + [SMEM] * scalars + [VMEM] * (len(arrays) - raw - scalars),
        out_specs=[VMEM] * len(outs),
        scratch_shapes=list(scratch),
        compiler_params=pltpu.CompilerParams(vmem_limit_bytes=24 << 20),
        cost_estimate=pl.CostEstimate(
            flops=int(cost * MICROSECOND), bytes_accessed=1 << 20, transcendentals=0
        ),
        name=name,
    )(*(pltpu.with_memory_space_constraint(x, pltpu.HBM) for x in arrays[:raw]), *arrays[raw:])


def pair_swaps(n):
    near = [(i, i ^ 1) for i in range(n)]
    far = [(i, (i + 1) % n if i % 2 else (i - 1) % n) for i in range(n)]
    return near, far


def on_device(
    grid_latent,
    mesh_latent,
    cotangent,
    halo_rows,
    encoder_sender,
    encoder_target,
    encoder_count,
    process_sender,
    process_target,
    process_count,
    encoder_source,
    encoder_dest,
    encoder_output,
    encoder_gain,
    process_source,
    process_dest,
    process_output,
    process_gain,
):
    patches, groups = lax.axis_size("patch"), lax.axis_size("group")
    near_swap, far_swap = pair_swaps(patches)
    grid_rows, width = grid_latent.shape
    mesh_rows = mesh_latent.shape[0]
    hidden_size = encoder_source.shape[1]
    coarse = mesh_rows // 16
    rim = halo_rows.shape[0] // 2
    slots, slots2 = encoder_sender.shape[0], process_sender.shape[0]

    near, far, grid = call(
        select_kernel,
        "select",
        [halo_rows, grid_latent],
        [((rim, width), BF16)] * 2 + [((grid_rows, width), BF16)],
        4,
        raw=2,
        scratch=[pltpu.VMEM(halo_rows.shape, I32), pltpu.SemaphoreType.DMA((2,))],
    )
    far = lax.ppermute(far, "patch", far_swap)
    near = lax.ppermute(near, "patch", near_swap)
    part, send_row, send_col, live_row, live_col, send_row2, send_col2, live_row2, live_col2 = call(
        functools.partial(encode_local_kernel, groups, coarse),
        "encode_local",
        [
            jnp.concatenate([encoder_count, process_count]),
            encoder_sender,
            encoder_target,
            process_sender,
            process_target,
            grid,
            mesh_latent,
            encoder_source,
            encoder_dest,
        ],
        [((slots, hidden_size), F32)]
        + [((1, slots), I32), ((slots, LANES), I32)] * 2
        + [((1, slots2), I32), ((slots2, LANES), I32)] * 2,
        2,
        scalars=1,
    )
    hidden, slope, updated16 = call(
        functools.partial(encode_halo_kernel, grid_rows, coarse),
        "encode_halo",
        [
            near,
            far,
            part,
            send_col,
            live_row,
            mesh_latent,
            encoder_source,
            encoder_output,
            encoder_gain,
        ],
        [((slots, hidden_size), BF16), ((slots, hidden_size), BF16), ((coarse, width), BF16)],
        2,
    )
    shifts = [
        lax.ppermute(updated16, "group", [(i, (i + k) % groups) for i in range(groups)])
        for k in range(1, groups)
    ]
    normed, inverse, part2 = call(
        process_local_kernel,
        "process_local",
        [
            hidden,
            live_row,
            mesh_latent,
            send_col2,
            live_col2,
            encoder_output,
            encoder_gain,
            process_source,
            process_dest,
        ],
        [
            ((mesh_rows, width), F32),
            ((mesh_rows, LANES), F32),
            ((slots2, hidden_size), F32),
        ],
        2,
    )
    grad2, *pieces = call(
        functools.partial(process_kernel, groups, coarse),
        "process",
        [
            part2,
            send_row2,
            send_col2,
            live_row2,
            live_col2,
            cotangent,
            process_source,
            process_output,
            process_gain,
            *shifts,
        ],
        [((slots2, hidden_size), BF16)] + [((coarse, hidden_size), BF16)] * (groups - 1),
        2,
    )
    pieces = [
        lax.ppermute(piece, "group", [(i, (i - k) % groups) for i in range(groups)])
        for k, piece in enumerate(pieces, 1)
    ]
    grad_local, raw = call(
        functools.partial(process_back_kernel, coarse),
        "process_back",
        [
            grad2,
            send_row2,
            live_row2,
            cotangent,
            process_source,
            process_dest,
            encoder_output,
            encoder_gain,
            normed,
            inverse,
            live_col,
        ],
        [((mesh_rows, width), F32), ((slots, hidden_size), F32)],
        2,
    )
    grad, near, far, grad16 = call(
        functools.partial(encode_back_kernel, groups, coarse, grid_rows),
        "encode_back",
        [
            grad_local,
            normed,
            inverse,
            raw,
            slope,
            live_col,
            send_row,
            encoder_gain,
            process_source,
            encoder_output,
            *pieces,
        ],
        [((slots, hidden_size), BF16)]
        + [((rim, hidden_size), BF16)] * 2
        + [((coarse, width), F32)],
        2,
    )
    far = lax.ppermute(far, "patch", far_swap)
    near = lax.ppermute(near, "patch", near_swap)
    mesh_grad, own = call(
        own_back_kernel,
        "own_back",
        [grad, send_row, live_row, grad_local, grad16, encoder_source, encoder_dest],
        [((mesh_rows, width), BF16), ((grid_rows, width), F32)],
        2,
    )
    (grid_grad,) = call(
        finish_kernel,
        "finish",
        [halo_rows, own, near, far, encoder_source],
        [((grid_rows, width), BF16)],
        2,
    )
    return grid_grad, mesh_grad


def solution(mesh):
    rows, flat, whole = P(("patch", "group"), None), P(("patch", "group")), P()
    return jax.shard_map(
        on_device,
        mesh=mesh,
        in_specs=(rows,) * 3 + (flat,) * 7 + (whole,) * 8,
        out_specs=(rows, rows),
        check_vma=False,
    )
```

time: 49.8 us -> 38.2 us (0.77)
  local copies, waits for them, and re-layouts: 9.33 us -> 0.07 us
  Pallas kernels: 16.3 us -> 14.2 us
  starting transfers between devices: 12.7 us -> 14 us
  waiting for transfers between devices: 8.79 us -> 7.55 us
    unnamed x34 -> x30, local copies, waits for them, and re-layouts: 5.85 us -> 0.07 us
    broadcast_in_dim x4 -> x0, local copies, waits for them, and re-layouts: 2.76 us -> none  [the longest x2 1.38 us: on_device(): sender, target = (encoder_sender[None], encoder_target[None])]
    pallas_call x9, Pallas kernels: 16.3 us -> 14.2 us  [call(): pl.pallas_call(kernel, out_shape=[jax.ShapeDtypeStruct(s, d) for s, d in...]
    ppermute x2, waiting for transfers between devices: 4.5 us -> 2.7 us  [on_device(): far = lax.ppermute(far, 'patch', far_swap)]
    ppermute x2, starting transfers between devices: 4.15 us -> 5.31 us  [on_device(): far = lax.ppermute(far, 'patch', far_swap)]
    slice x4 -> x0, local copies, waits for them, and re-layouts: 0.73 us -> none  [the longest x1 0.72 us: on_device(): mesh16 = mesh_latent[:coarse]]
    ppermute x3, waiting for transfers between devices: 2.17 us -> 2.76 us  [on_device(): lax.ppermute(updated16, 'group', [(i, (i + k) % groups) for i in range(gr...]
  transfers between devices with their start and end apart: 10 -> 10, of which waited for: 5 -> 5; matrix products, arithmetic and copies ran while one was open for 7% -> 0% of each run, Pallas kernels for 14% -> 17%
where the time goes in v2:
time: 38.2 us; the launch traced here: 38.1 us
  Pallas kernels  14.2 us (37%)
  starting transfers between devices  14 us (37%)
  waiting for transfers between devices  7.55 us (20%)
  between operations  2.18 us (6%)
    pallas_call x9, Pallas kernels, call(): pl.pallas_call(kernel, out_shape=[jax.ShapeDtypeStruct(s, d) for s, d in...  14.2 us
    ppermute x2, starting transfers between devices, on_device(): far = lax.ppermute(far, 'patch', far_swap)  5.31 us
    ppermute x3, starting transfers between devices, on_device(): lax.ppermute(updated16, 'group', [(i, (i + k) % groups) for i in range(gr...  4.82 us
    ppermute x3, starting transfers between devices, on_device(): lax.ppermute(piece, 'group', [(i, (i - k) % groups) for i in range(groups)])  3.2 us
    ppermute x3, waiting for transfers between devices, on_device(): lax.ppermute(updated16, 'group', [(i, (i + k) % groups) for i in range(gr...  2.76 us
    ppermute x2, waiting for transfers between devices, on_device(): far = lax.ppermute(far, 'patch', far_swap)  2.7 us
    ppermute x3, waiting for transfers between devices, on_device(): lax.ppermute(piece, 'group', [(i, (i - k) % groups) for i in range(groups)])  2.08 us
  transfers between devices with their start and end apart: 10, of which 5 were waited for; matrix products, arithmetic and copies ran while one was open for 0% of the time, Pallas kernels for 17%

profile of v2, /device:TPU:0, one launch (start us, length us, event | category | flops | bytes accessed | tf_op | source)
XLA Modules:
  0.0 38.1 jit_solution(15672869503261607854)
XLA Ops:
  0.7 1.5 %select.1 = (bf16[128,512]{1,0:T(8,128)(2,1)S(1)}, bf16[128,512]{1,0:T(8,128)(2,1)S(1)}, bf16[512,512]{1,0:T(8,128)(2,1)S(1)}) custom-call(s32[256]{0:T(256)} %halo.1, bf16[512,512]{1,0:T(8,128)(2,1)} %grid_hbm.1), custom_call_target="tpu_custom_call" | custom-call | flops 4294967296 | bytes 1048576 | tf_op jit(solution)/shard_map/select/pallas_call | solution.py:345
  2.2 0.6 %collective-permute-start = (bf16[128,512]{1,0:T(8,128)(2,1)S(1)}, bf16[128,512]{1,0:T(8,128)(2,1)S(1)}, u32[]{:S(2)}, u32[]{:S(2)}) collective-permute-start(bf16[128,512]{1,0:T(8,128)(2,1)S(1)} %get-tuple-element.32), channel_id=1, source_target_pairs={{0,4},{4,0},{8,12},{12,8},{16,20},{20,16},{24,28},{28,24},{1,5},{5... | collective-permute-start | bytes 393224 | tf_op jit(solution)/shard_map/ppermute | solution.py:404
  2.7 3.5 %collective-permute-start.1 = (bf16[128,512]{1,0:T(8,128)(2,1)S(1)}, bf16[128,512]{1,0:T(8,128)(2,1)S(1)}, u32[]{:S(2)}, u32[]{:S(2)}) collective-permute-start(bf16[128,512]{1,0:T(8,128)(2,1)S(1)} %get-tuple-element.33), channel_id=1, source_target_pairs={{0,28},{4,8},{8,4},{12,16},{16,12},{20,24},{24,20},{28,0},{1,29},{... | collective-permute-start | bytes 393224 | tf_op jit(solution)/shard_map/ppermute | solution.py:403
  7.6 0.1 pad_add_fusion.counts
  7.7 0.0 copy-start.2
  7.7 0.0 copy-start.13
  7.7 1.9 %encode_local.1 = (f32[768,512]{1,0:T(8,128)S(1)}, s32[1,768]{1,0:T(1,128)S(1)}, s32[768,128]{1,0:T(8,128)S(1)}, s32[1,768]{1,0:T(1,128)S(1)}, s32[768,128]{1,0:...) custom-call(s32[2]{0:T(128)S(1)} %pad_add_fusion.counts, ...), custom_call_target="tpu_custom_call" | custom-call | flops 2147483648 | bytes 1048576 | tf_op jit(solution)/shard_map/encode_local/pallas_call | solution.py:345
  9.6 0.0 collective-permute-done.near
  9.7 0.0 copy-start.1
  9.7 0.0 copy-start.3
  9.7 1.5 %encode_halo.1 = (bf16[768,512]{1,0:T(8,128)(2,1)S(1)}, bf16[768,512]{1,0:T(8,128)(2,1)S(1)}, bf16[16,512]{1,0:T(8,128)(2,1)S(1)}) custom-call(bf16[128,512]{1,0:T(8,128)(2,1)S(1)} %collective-permute-done.near, bf16[128,512]{1,0:T(8,128)(2,1)S(1)} %collective-permute-done.1.far, f32[768,512]{1,0:T(8,128)S(1)} %get-tuple-element.35.part, ...), custom_call_target="tpu_custom_call" | custom-call | flops 2147483648 | bytes 1048576 | tf_op jit(solution)/shard_map/encode_halo/pallas_call | solution.py:345
  11.2 3.8 %collective-permute-start.4 = (bf16[16,512]{1,0:T(8,128)(2,1)S(1)}, bf16[16,512]{1,0:T(8,128)(2,1)S(1)}, u32[]{:S(2)}, u32[]{:S(2)}) collective-permute-start(bf16[16,512]{1,0:T(8,128)(2,1)S(1)} %get-tuple-element.44), channel_id=1, source_target_pairs={{0,3},{1,0},{2,1},{3,2},{4,7},{5,4},{6,5},{7,6},{8,11},{9,8},{10,9... | collective-permute-start | bytes 49160 | tf_op jit(solution)/shard_map/ppermute | solution.py:443
  15.0 1.0 %collective-permute-start.2 = (bf16[16,512]{1,0:T(8,128)(2,1)S(1)}, bf16[16,512]{1,0:T(8,128)(2,1)S(1)}, u32[]{:S(2)}, u32[]{:S(2)}) collective-permute-start(bf16[16,512]{1,0:T(8,128)(2,1)S(1)} %get-tuple-element.44), channel_id=1, source_target_pairs={{0,1},{1,2},{2,3},{3,0},{4,5},{5,6},{6,7},{7,4},{8,9},{9,10},{10,1... | collective-permute-start | bytes 49160 | tf_op jit(solution)/shard_map/ppermute | solution.py:443
  16.0 0.0 copy-start.12
  16.0 1.7 %process_local.1 = (f32[256,512]{1,0:T(8,128)S(1)}, f32[256,128]{1,0:T(8,128)S(1)}, f32[768,512]{1,0:T(8,128)S(1)}) custom-call(bf16[768,512]{1,0:T(8,128)(2,1)S(1)} %get-tuple-element.38.hidden, s32[1,768]{1,0:T(1,128)S(1)} %get-tuple-element.37.live_row, bf16[256,512]{1,0:T(8,128)(2,1)S(1)} %copy-done.6, s32[768,128]{1,0:T(8,128)S(1)} %get-tuple-element.39.send_col2, ...), custom_call_target="tpu_custom_call" | custom-call | flops 2147483648 | bytes 1048576 | tf_op jit(solution)/shard_map/process_local/pallas_call | solution.py:345
  17.8 1.9 %collective-permute-done.3.refs_1_ = bf16[16,512]{1,0:T(8,128)(2,1)S(1)} collective-permute-done((bf16[16,512]{1,0:T(8,128)(2,1)S(1)}, bf16[16,512]{1,0:T(8,128)(2,1)S(1)}, u32[]{:S(2)}, u32[]{:S(2)}) %collective-permute-start.3) | collective-permute-done | bytes 16416 | tf_op jit(solution)/shard_map/ppermute | solution.py:443
  19.6 0.9 %collective-permute-done.2.refs_0_ = bf16[16,512]{1,0:T(8,128)(2,1)S(1)} collective-permute-done((bf16[16,512]{1,0:T(8,128)(2,1)S(1)}, bf16[16,512]{1,0:T(8,128)(2,1)S(1)}, u32[]{:S(2)}, u32[]{:S(2)}) %collective-permute-start.2) | collective-permute-done | bytes 16416 | tf_op jit(solution)/shard_map/ppermute | solution.py:443
  20.5 2.3 %process.1 = (bf16[768,512]{1,0:T(8,128)(2,1)S(1)}, bf16[16,512]{1,0:T(8,128)(2,1)S(1)}, bf16[16,512]{1,0:T(8,128)(2,1)S(1)}, bf16[16,512]{1,0:T(8,128)(2,1)S(1)}) custom-call(f32[768,512]{1,0:T(8,128)S(1)} %get-tuple-element.41.part, s32[1,768]{1,0:T(1,128)S(1)} %get-tuple-element.42.send_row2, s32[768,128]{1,0:T(8,128)S(1)} %get-tuple-element.39.send_col2, ...), custom_call_target="tpu_custom_call" | custom-call | flops 2147483648 | bytes 1048576 | tf_op jit(solution)/shard_map/process/pallas_call | solution.py:345
  22.8 0.6 %collective-permute-start.5 = (bf16[16,512]{1,0:T(8,128)(2,1)S(1)}, bf16[16,512]{1,0:T(8,128)(2,1)S(1)}, u32[]{:S(2)}, u32[]{:S(2)}) collective-permute-start(bf16[16,512]{1,0:T(8,128)(2,1)S(1)} %get-tuple-element.53), channel_id=1, source_target_pairs={{0,3},{1,0},{2,1},{3,2},{4,7},{5,4},{6,5},{7,6},{8,11},{9,8},{10,9... | collective-permute-start | bytes 49160 | tf_op jit(solution)/shard_map/ppermute | solution.py:486
  23.4 0.7 %collective-permute-start.6 = (bf16[16,512]{1,0:T(8,128)(2,1)S(1)}, bf16[16,512]{1,0:T(8,128)(2,1)S(1)}, u32[]{:S(2)}, u32[]{:S(2)}) collective-permute-start(bf16[16,512]{1,0:T(8,128)(2,1)S(1)} %get-tuple-element.54), channel_id=1, source_target_pairs={{0,2},{1,3},{2,0},{3,1},{4,6},{5,7},{6,4},{7,5},{8,10},{9,11},{10,... | collective-permute-start | bytes 49160 | tf_op jit(solution)/shard_map/ppermute | solution.py:486
  24.1 1.9 %collective-permute-start.7 = (bf16[16,512]{1,0:T(8,128)(2,1)S(1)}, bf16[16,512]{1,0:T(8,128)(2,1)S(1)}, u32[]{:S(2)}, u32[]{:S(2)}) collective-permute-start(bf16[16,512]{1,0:T(8,128)(2,1)S(1)} %get-tuple-element.55), channel_id=1, source_target_pairs={{0,1},{1,2},{2,3},{3,0},{4,5},{5,6},{6,7},{7,4},{8,9},{9,10},{10,1... | collective-permute-start | bytes 49160 | tf_op jit(solution)/shard_map/ppermute | solution.py:486
  26.0 1.5 %process_back.1 = (f32[256,512]{1,0:T(8,128)S(1)}, f32[768,512]{1,0:T(8,128)S(1)}) custom-call(bf16[768,512]{1,0:T(8,128)(2,1)S(1)} %get-tuple-element.45.grad, s32[1,768]{1,0:T(1,128)S(1)} %get-tuple-element.42.send_row2, s32[1,768]{1,0:T(1,128)S(1)} %get-tuple-element.43.live_row2, bf16[256,512]{1,0:T(8,128)(2,1)S(1)} %copy-done.7, ...), custom_call_target="tpu_custom_call" | custom-call | flops 2147483648 | bytes 1048576 | tf_op jit(solution)/shard_map/process_back/pallas_call | solution.py:345
  27.5 0.0 collective-permute-done.5.refs_0_
  27.5 0.5 %collective-permute-done.6.refs_1_ = bf16[16,512]{1,0:T(8,128)(2,1)S(1)} collective-permute-done((bf16[16,512]{1,0:T(8,128)(2,1)S(1)}, bf16[16,512]{1,0:T(8,128)(2,1)S(1)}, u32[]{:S(2)}, u32[]{:S(2)}) %collective-permute-start.6) | collective-permute-done | bytes 16416 | tf_op jit(solution)/shard_map/ppermute | solution.py:486
  28.1 1.6 %collective-permute-done.7.refs_2_ = bf16[16,512]{1,0:T(8,128)(2,1)S(1)} collective-permute-done((bf16[16,512]{1,0:T(8,128)(2,1)S(1)}, bf16[16,512]{1,0:T(8,128)(2,1)S(1)}, u32[]{:S(2)}, u32[]{:S(2)}) %collective-permute-start.7) | collective-permute-done | bytes 16416 | tf_op jit(solution)/shard_map/ppermute | solution.py:486
  29.6 1.2 %encode_back.1 = (bf16[768,512]{1,0:T(8,128)(2,1)S(1)}, bf16[128,512]{1,0:T(8,128)(2,1)S(1)}, bf16[128,512]{1,0:T(8,128)(2,1)S(1)}, f32[16,512]{1,0:T(8,128)S(1)}) custom-call(f32[256,512]{1,0:T(8,128)S(1)} %get-tuple-element.49.grad_local, f32[256,512]{1,0:T(8,128)S(1)} %get-tuple-element.46.normed, f32[256,128]{1,0:T(8,128)S(1)} %get-tuple-element.47.inverse, ...), custom_call_target="tpu_custom_call" | custom-call | flops 2147483648 | bytes 1048576 | tf_op jit(solution)/shard_map/encode_back/pallas_call | solution.py:345
  30.8 0.1 collective-permute-start.8
  30.9 1.8 %collective-permute-start.9 = (bf16[128,512]{1,0:T(8,128)(2,1)S(1)}, bf16[128,512]{1,0:T(8,128)(2,1)S(1)}, u32[]{:S(2)}, u32[]{:S(2)}) collective-permute-start(bf16[128,512]{1,0:T(8,128)(2,1)S(1)} %get-tuple-element.60), channel_id=1, source_target_pairs={{0,28},{4,8},{8,4},{12,16},{16,12},{20,24},{24,20},{28,0},{1,29},{... | collective-permute-start | bytes 393224 | tf_op jit(solution)/shard_map/ppermute | solution.py:529
  32.7 1.3 %own_back.1 = (bf16[256,512]{1,0:T(8,128)(2,1)}, f32[512,512]{1,0:T(8,128)S(1)}) custom-call(bf16[768,512]{1,0:T(8,128)(2,1)S(1)} %get-tuple-element.56.grad, s32[1,768]{1,0:T(1,128)S(1)} %get-tuple-element.52.send_row, s32[1,768]{1,0:T(1,128)S(1)} %get-tuple-element.37.live_row, f32[256,512]{1,0:T(8,128)S(1)} %get-tuple-element.49.grad_local, ...), custom_call_target="tpu_custom_call" | custom-call | flops 2147483648 | bytes 1048576 | tf_op jit(solution)/shard_map/own_back/pallas_call | solution.py:345
  34.0 0.0 collective-permute-done.8.near
  34.0 2.7 %collective-permute-done.9.far = bf16[128,512]{1,0:T(8,128)(2,1)S(1)} collective-permute-done((bf16[128,512]{1,0:T(8,128)(2,1)S(1)}, bf16[128,512]{1,0:T(8,128)(2,1)S(1)}, u32[]{:S(2)}, u32[]{:S(2)}) %collective-permute-start.9) | collective-permute-done | bytes 131104 | tf_op jit(solution)/shard_map/ppermute | solution.py:529
  36.7 1.4 %finish.1 = bf16[512,512]{1,0:T(8,128)(2,1)} custom-call(s32[256]{0:T(256)S(1)} %copy-done.14, f32[512,512]{1,0:T(8,128)S(1)} %get-tuple-element.58.own, bf16[128,512]{1,0:T(8,128)(2,1)S(1)} %collective-permute-done.8.near, bf16[128,512]{1,0:T(8,128)(2,1)S(1)} %collective-permute-done.9.far, bf16[512,512]{1,0:T(8,128)(2,1)S(1)} %copy-done.5), custom_call_target="tpu_custom_call" | custom-call | flops 2147483648 | bytes 1048576 | tf_op jit(solution)/shard_map/finish/pallas_call | solution.py:345
  (28 shorter events, 0.1 us)
Async XLA Ops:
  0.6 7.0 %copy-start.5 = (bf16[512,512]{1,0:T(8,128)(2,1)S(1)}, bf16[512,512]{1,0:T(8,128)(2,1)}, u32[]{:S(2)}) copy-start(bf16[512,512]{1,0:T(8,128)(2,1)} %w_source.13) | copy-start | bytes 1572868
  0.6 7.0 %copy-start.6 = (bf16[256,512]{1,0:T(8,128)(2,1)S(1)}, bf16[256,512]{1,0:T(8,128)(2,1)}, u32[]{:S(2)}) copy-start(bf16[256,512]{1,0:T(8,128)(2,1)} %mesh.5) | copy-start | bytes 786436
  0.7 7.0 %copy-start.4 = (bf16[512,512]{1,0:T(8,128)(2,1)S(1)}, bf16[512,512]{1,0:T(8,128)(2,1)}, u32[]{:S(2)}) copy-start(bf16[512,512]{1,0:T(8,128)(2,1)} %w_dest.7) | copy-start | bytes 1572868
  0.7 7.0 %copy-start.11 = (s32[768]{0:T(1024)S(1)}, s32[768]{0:T(1024)}, u32[]{:S(2)}) copy-start(s32[768]{0:T(1024)} %target2.1) | copy-start | bytes 9220
  0.7 7.0 %copy-start.10 = (s32[768]{0:T(1024)S(1)}, s32[768]{0:T(1024)}, u32[]{:S(2)}) copy-start(s32[768]{0:T(1024)} %sender2.1) | copy-start | bytes 9220
  0.7 7.0 %copy-start.9 = (s32[768]{0:T(1024)S(1)}, s32[768]{0:T(1024)}, u32[]{:S(2)}) copy-start(s32[768]{0:T(1024)} %target.1) | copy-start | bytes 9220
  0.7 7.0 %copy-start.8 = (s32[768]{0:T(1024)S(1)}, s32[768]{0:T(1024)}, u32[]{:S(2)}) copy-start(s32[768]{0:T(1024)} %sender.1) | copy-start | bytes 9220
  2.2 7.4 %collective-permute-start = (bf16[128,512]{1,0:T(8,128)(2,1)S(1)}, bf16[128,512]{1,0:T(8,128)(2,1)S(1)}, u32[]{:S(2)}, u32[]{:S(2)}) collective-permute-start(bf16[128,512]{1,0:T(8,128)(2,1)S(1)} %get-tuple-element.32), channel_id=1, source_target_pairs={{0,4},{4,0},{8,12},{12,8},{16,20},{20,16},{24,28},{28,24},{1,5},{5... | collective-permute-start | bytes 393224 | tf_op jit(solution)/shard_map/ppermute | solution.py:404
  2.7 6.9 %collective-permute-start.1 = (bf16[128,512]{1,0:T(8,128)(2,1)S(1)}, bf16[128,512]{1,0:T(8,128)(2,1)S(1)}, u32[]{:S(2)}, u32[]{:S(2)}) collective-permute-start(bf16[128,512]{1,0:T(8,128)(2,1)S(1)} %get-tuple-element.33), channel_id=1, source_target_pairs={{0,28},{4,8},{8,4},{12,16},{16,12},{20,24},{24,20},{28,0},{1,29},{... | collective-permute-start | bytes 393224 | tf_op jit(solution)/shard_map/ppermute | solution.py:403
  7.7 1.9 %copy-start.2 = (bf16[512,512]{1,0:T(8,128)(2,1)S(1)}, bf16[512,512]{1,0:T(8,128)(2,1)}, u32[]{:S(2)}) copy-start(bf16[512,512]{1,0:T(8,128)(2,1)} %w_out.9) | copy-start | bytes 1572868
  7.7 1.9 %copy-start.13 = (f32[512]{0:T(512)S(1)}, f32[512]{0:T(512)}, u32[]{:S(2)}) copy-start(f32[512]{0:T(512)} %gain.9) | copy-start | bytes 6148
  9.7 6.3 %copy-start.1 = (bf16[512,512]{1,0:T(8,128)(2,1)S(1)}, bf16[512,512]{1,0:T(8,128)(2,1)}, u32[]{:S(2)}) copy-start(bf16[512,512]{1,0:T(8,128)(2,1)} %w_dest.6) | copy-start | bytes 1572868
  9.7 6.3 %copy-start.3 = (bf16[512,512]{1,0:T(8,128)(2,1)S(1)}, bf16[512,512]{1,0:T(8,128)(2,1)}, u32[]{:S(2)}) copy-start(bf16[512,512]{1,0:T(8,128)(2,1)} %w_source2.1) | copy-start | bytes 1572868
  11.2 6.6 %collective-permute-start.4 = (bf16[16,512]{1,0:T(8,128)(2,1)S(1)}, bf16[16,512]{1,0:T(8,128)(2,1)S(1)}, u32[]{:S(2)}, u32[]{:S(2)}) collective-permute-start(bf16[16,512]{1,0:T(8,128)(2,1)S(1)} %get-tuple-element.44), channel_id=1, source_target_pairs={{0,3},{1,0},{2,1},{3,2},{4,7},{5,4},{6,5},{7,6},{8,11},{9,8},{10,9... | collective-permute-start | bytes 49160 | tf_op jit(solution)/shard_map/ppermute | solution.py:443
  15.0 4.6 %collective-permute-start.3 = (bf16[16,512]{1,0:T(8,128)(2,1)S(1)}, bf16[16,512]{1,0:T(8,128)(2,1)S(1)}, u32[]{:S(2)}, u32[]{:S(2)}) collective-permute-start(bf16[16,512]{1,0:T(8,128)(2,1)S(1)} %get-tuple-element.44), channel_id=1, source_target_pairs={{0,2},{1,3},{2,0},{3,1},{4,6},{5,7},{6,4},{7,5},{8,10},{9,11},{10,... | collective-permute-start | bytes 49160 | tf_op jit(solution)/shard_map/ppermute | solution.py:443
  15.0 5.5 %collective-permute-start.2 = (bf16[16,512]{1,0:T(8,128)(2,1)S(1)}, bf16[16,512]{1,0:T(8,128)(2,1)S(1)}, u32[]{:S(2)}, u32[]{:S(2)}) collective-permute-start(bf16[16,512]{1,0:T(8,128)(2,1)S(1)} %get-tuple-element.44), channel_id=1, source_target_pairs={{0,1},{1,2},{2,3},{3,0},{4,5},{5,6},{6,7},{7,4},{8,9},{9,10},{10,1... | collective-permute-start | bytes 49160 | tf_op jit(solution)/shard_map/ppermute | solution.py:443
  16.0 4.5 %copy-start = (bf16[512,512]{1,0:T(8,128)(2,1)S(1)}, bf16[512,512]{1,0:T(8,128)(2,1)}, u32[]{:S(2)}) copy-start(bf16[512,512]{1,0:T(8,128)(2,1)} %w_out.7) | copy-start | bytes 1572868
  16.0 4.5 %copy-start.7 = (bf16[256,512]{1,0:T(8,128)(2,1)S(1)}, bf16[256,512]{1,0:T(8,128)(2,1)}, u32[]{:S(2)}) copy-start(bf16[256,512]{1,0:T(8,128)(2,1)} %cotangent.3) | copy-start | bytes 786436
  16.0 4.5 %copy-start.12 = (f32[512]{0:T(512)S(1)}, f32[512]{0:T(512)}, u32[]{:S(2)}) copy-start(f32[512]{0:T(512)} %gain.7) | copy-start | bytes 6148
  22.8 4.7 %collective-permute-start.5 = (bf16[16,512]{1,0:T(8,128)(2,1)S(1)}, bf16[16,512]{1,0:T(8,128)(2,1)S(1)}, u32[]{:S(2)}, u32[]{:S(2)}) collective-permute-start(bf16[16,512]{1,0:T(8,128)(2,1)S(1)} %get-tuple-element.53), channel_id=1, source_target_pairs={{0,3},{1,0},{2,1},{3,2},{4,7},{5,4},{6,5},{7,6},{8,11},{9,8},{10,9... | collective-permute-start | bytes 49160 | tf_op jit(solution)/shard_map/ppermute | solution.py:486
  23.4 4.6 %collective-permute-start.6 = (bf16[16,512]{1,0:T(8,128)(2,1)S(1)}, bf16[16,512]{1,0:T(8,128)(2,1)S(1)}, u32[]{:S(2)}, u32[]{:S(2)}) collective-permute-start(bf16[16,512]{1,0:T(8,128)(2,1)S(1)} %get-tuple-element.54), channel_id=1, source_target_pairs={{0,2},{1,3},{2,0},{3,1},{4,6},{5,7},{6,4},{7,5},{8,10},{9,11},{10,... | collective-permute-start | bytes 49160 | tf_op jit(solution)/shard_map/ppermute | solution.py:486
  24.1 5.5 %collective-permute-start.7 = (bf16[16,512]{1,0:T(8,128)(2,1)S(1)}, bf16[16,512]{1,0:T(8,128)(2,1)S(1)}, u32[]{:S(2)}, u32[]{:S(2)}) collective-permute-start(bf16[16,512]{1,0:T(8,128)(2,1)S(1)} %get-tuple-element.55), channel_id=1, source_target_pairs={{0,1},{1,2},{2,3},{3,0},{4,5},{5,6},{6,7},{7,4},{8,9},{9,10},{10,1... | collective-permute-start | bytes 49160 | tf_op jit(solution)/shard_map/ppermute | solution.py:486
  30.8 3.1 %collective-permute-start.8 = (bf16[128,512]{1,0:T(8,128)(2,1)S(1)}, bf16[128,512]{1,0:T(8,128)(2,1)S(1)}, u32[]{:S(2)}, u32[]{:S(2)}) collective-permute-start(bf16[128,512]{1,0:T(8,128)(2,1)S(1)} %get-tuple-element.59), channel_id=1, source_target_pairs={{0,4},{4,0},{8,12},{12,8},{16,20},{20,16},{24,28},{28,24},{1,5},{5... | collective-permute-start | bytes 393224 | tf_op jit(solution)/shard_map/ppermute | solution.py:530
  30.9 5.8 %collective-permute-start.9 = (bf16[128,512]{1,0:T(8,128)(2,1)S(1)}, bf16[128,512]{1,0:T(8,128)(2,1)S(1)}, u32[]{:S(2)}, u32[]{:S(2)}) collective-permute-start(bf16[128,512]{1,0:T(8,128)(2,1)S(1)} %get-tuple-element.60), channel_id=1, source_target_pairs={{0,28},{4,8},{8,4},{12,16},{16,12},{20,24},{24,20},{28,0},{1,29},{... | collective-permute-start | bytes 393224 | tf_op jit(solution)/shard_map/ppermute | solution.py:529
  32.7 4.0 %copy-start.14 = (s32[256]{0:T(256)S(1)}, s32[256]{0:T(256)}, u32[]{:S(2)}) copy-start(s32[256]{0:T(256)} %halo.1) | copy-start | bytes 3076

commit v3 on v2

v3 whole, which is shorter than its diff:
```python
import functools

import jax
import jax.numpy as jnp
from jax import lax
from jax.experimental import pallas as pl
from jax.experimental.pallas import tpu as pltpu
from jax.sharding import PartitionSpec as P


EPSILON = 1e-05
LANES = 128
F32 = jnp.float32
BF16 = jnp.bfloat16
I32 = jnp.int32


def mm(a, b):
    return jnp.dot(a, b, preferred_element_type=F32)


def mm_t(a, b):
    return lax.dot_general(a, b, (((1,), (1,)), ((), ())), preferred_element_type=F32)


def half_silu(u):
    t = jnp.tanh(u)
    a = 1.0 + t
    value = u * a
    return value, a + value * (1.0 - t)


def ceil_to(n, k):
    return (n + k - 1) // k * k


def to_columns(row):
    n = row.shape[1]
    parts = []
    for i in range(0, n, LANES):
        parts.append(jnp.broadcast_to(row[:, i : i + LANES], (LANES, LANES)).T)
    return jnp.concatenate(parts, axis=0)


def pick(columns, first, width):
    lane = lax.broadcasted_iota(I32, columns.shape, 1)
    parts = []
    for i in range(0, width, LANES):
        parts.append(jnp.where(columns == lane + (first + i), 1.0, 0.0).astype(BF16))
    return parts[0] if len(parts) == 1 else jnp.concatenate(parts, axis=1)


def spread(row, first, height):
    shape = (height, row.shape[1])
    return jnp.where(row == lax.broadcasted_iota(I32, shape, 0) + first, 1.0, 0.0).astype(BF16)


def only_live(rows, count):
    slot = lax.broadcasted_iota(I32, rows.shape, 1)
    return jnp.where(slot < count, rows, -1)


def normalise(values):
    center = values - jnp.mean(values, axis=-1, keepdims=True)
    inverse = lax.rsqrt(jnp.mean(center * center, axis=-1, keepdims=True) + EPSILON)
    return center * inverse, inverse


def centred(values):
    return values - jnp.mean(values, axis=-1, keepdims=True)


def normalise_back(centre, normed, inverse):
    return inverse * (centre - normed * jnp.mean(centre * normed, axis=-1, keepdims=True))


def halves(rows, even):
    half = rows.shape[1] // 2
    first, second = rows[:, :half], rows[:, half:]
    return jnp.where(even, second, first), jnp.where(even, first, second)


def coarse_slots(sender, mesh_rows, coarse, me):
    offset = sender - mesh_rows
    owner = offset // coarse
    row = offset - owner * coarse
    mask = owner ^ me
    moved = jnp.where(mask == 0, row, mesh_rows + (mask - 1) * coarse + row)
    return jnp.where(offset < 0, sender, moved)


def even_patch():
    return lax.rem(lax.axis_index("patch"), 2) == 0


def as_row(ref):
    return ref[...].reshape(1, ref.shape[0])


def select_kernel(halo_hbm, grid_hbm, near, far, table, halo, sems):
    copies = [
        pltpu.make_async_copy(halo_hbm, halo, sems.at[0]),
        pltpu.make_async_copy(grid_hbm, table, sems.at[1]),
    ]
    for copy in copies:
        copy.start()
    copies[0].wait()
    rows_near, rows_far = halves(as_row(halo), even_patch())
    pick_near = pick(to_columns(rows_near), 0, table.shape[0])
    pick_far = pick(to_columns(rows_far), 0, table.shape[0])
    copies[1].wait()
    near[...] = mm(pick_near, table[...]).astype(BF16)
    far[...] = mm(pick_far, table[...]).astype(BF16)


def rim_starts(grid_rows, rim):
    even = even_patch()
    return (
        jnp.where(even, grid_rows + rim, grid_rows),
        jnp.where(even, grid_rows, grid_rows + rim),
    )


def encode_local_kernel(
    coarse,
    counts,
    sender,
    target,
    sender2,
    target2,
    grid,
    mesh,
    w_source,
    w_dest,
    part,
    live_send,
    live_goal,
    live_send2,
    live_goal2,
    send_col2,
    goal_col2,
    pick_rim,
    pick_goal,
):
    rows, grid_rows = mesh.shape[0], grid.shape[0]
    rim = pick_rim.shape[1] // 2
    source = (0.5 * mm(grid[...], w_source[...])).astype(BF16)
    dest = (0.5 * mm(mesh[...], w_dest[...])).astype(BF16)
    send_col = to_columns(as_row(sender))
    near_first, far_first = rim_starts(grid_rows, rim)
    pick_rim[:, :rim] = pick(send_col, near_first, rim)
    pick_rim[:, rim:] = pick(send_col, far_first, rim)
    pick_goal[...] = pick(to_columns(as_row(target)), 0, rows)
    moved = coarse_slots(as_row(sender2), rows, coarse, lax.axis_index("group"))
    send_col2[...] = to_columns(moved)
    goal_col2[...] = to_columns(as_row(target2))
    part[...] = mm(pick(send_col, 0, grid_rows), source) + mm(pick_goal[...], dest)
    live_send[...] = only_live(as_row(sender), counts[0])
    live_goal[...] = only_live(as_row(target), counts[0])
    live_send2[...] = only_live(moved, counts[1])
    live_goal2[...] = only_live(as_row(target2), counts[1])


def pieces_of(n, size):
    return [slice(i, min(i + size, n)) for i in range(0, n, size)]


def encode_halo_kernel(
    coarse,
    near,
    far,
    part,
    pick_rim,
    live_goal,
    mesh,
    w_source,
    w_out,
    gain,
    hidden,
    half,
    updated16,
):
    halo = jnp.concatenate([near[...], far[...]], axis=0)
    source = (0.5 * mm(halo, w_source[...])).astype(BF16)
    for c in pieces_of(part.shape[0], 256):
        u = part[c, :] + mm(pick_rim[c, :], source)
        half[c, :] = u
        hidden[c, :] = (u + u * jnp.tanh(u)).astype(BF16)
    summed = mm(spread(live_goal[...], 0, coarse), hidden[...]).astype(BF16)
    normed, _ = normalise(mm(summed, w_out[...]))
    updated16[...] = (mesh[:coarse, :].astype(F32) + normed * as_row(gain)).astype(BF16)


def process_local_kernel(
    hidden,
    live_goal,
    mesh,
    send_col2,
    goal_col2,
    live_send2,
    live_goal2,
    cotangent,
    w_out,
    gain,
    gain2,
    w_source,
    w_dest,
    normed_ref,
    inverse_ref,
    part,
    pick_goal2,
    pick_coarse,
    sum_goal2,
    sum_coarse,
    centre2,
):
    rows = mesh.shape[0]
    summed = mm(spread(live_goal[...], 0, rows), hidden[...]).astype(BF16)
    normed, inverse = normalise(mm(summed, w_out[...]))
    normed_ref[...] = normed
    inverse_ref[...] = jnp.broadcast_to(inverse, inverse_ref.shape)
    updated = (mesh[...].astype(F32) + normed * as_row(gain)).astype(BF16)
    source = (0.5 * mm(updated, w_source[...])).astype(BF16)
    dest = (0.5 * mm(updated, w_dest[...])).astype(BF16)
    pick_goal2[...] = pick(goal_col2[...], 0, rows)
    pick_coarse[...] = pick(send_col2[...], rows, pick_coarse.shape[1])
    sum_goal2[...] = spread(live_goal2[...], 0, rows)
    sum_coarse[...] = spread(live_send2[...], rows, sum_coarse.shape[0])
    centre2[...] = centred(cotangent[...].astype(F32) * as_row(gain2))
    part[...] = mm(pick(send_col2[...], 0, rows), source) + mm(pick_goal2[...], dest)


def process_kernel(
    coarse,
    part,
    pick_goal2,
    pick_coarse,
    sum_goal2,
    sum_coarse,
    centre2,
    w_source,
    w_out,
    *refs,
):
    peers = sum_coarse.shape[0] // coarse
    received, grad, returned = refs[:peers], refs[peers], refs[peers + 1 : -2]
    hidden, slope = refs[-2:]
    rows = jnp.concatenate([r[...] for r in received], axis=0)
    source = (0.5 * mm(rows, w_source[...])).astype(BF16)
    spare = pick_coarse.shape[1] - source.shape[0]
    if spare:
        source = jnp.concatenate([source, jnp.zeros((spare, source.shape[1]), BF16)], axis=0)
    for c in pieces_of(part.shape[0], 256):
        value, double = half_silu(part[c, :] + mm(pick_coarse[c, :], source))
        hidden[c, :] = value.astype(BF16)
        slope[c, :] = double
    summed = mm(sum_goal2[...], hidden[...]).astype(BF16)
    normed, inverse = normalise(mm(summed, w_out[...]))
    back = normalise_back(centre2[...], normed, inverse).astype(BF16)
    back = (0.5 * mm_t(back, w_out[...])).astype(BF16)
    for c in pieces_of(part.shape[0], 256):
        grad[c, :] = (mm(pick_goal2[c, :], back) * slope[c, :]).astype(BF16)
    sums = mm(sum_coarse[...], grad[...])
    for i, out in enumerate(returned):
        out[...] = sums[i * coarse : (i + 1) * coarse].astype(BF16)


def process_back_kernel(
    grid_rows,
    half,
    grad,
    live_send,
    live_send2,
    sum_goal2,
    cotangent,
    w_source,
    w_dest,
    w_out,
    gain,
    normed,
    inverse,
    grad_local,
    back_ref,
    slope,
    sum_rim,
):
    rows = cotangent.shape[0]
    rim = sum_rim.shape[0] // 2
    near_first, far_first = rim_starts(grid_rows, rim)
    sum_rim[:rim, :] = spread(live_send[...], near_first, rim)
    sum_rim[rim:, :] = spread(live_send[...], far_first, rim)
    table = mm(spread(live_send2[...], 0, rows), grad[...]).astype(BF16)
    dest = mm(sum_goal2[...], grad[...]).astype(BF16)
    local = cotangent[...].astype(F32) + mm_t(table, w_source[...]) + mm_t(dest, w_dest[...])
    grad_local[...] = local
    back = normalise_back(centred(local * as_row(gain)), normed[...], inverse[:, :1])
    back_ref[...] = (0.5 * mm_t(back.astype(BF16), w_out[...])).astype(BF16)
    for c in pieces_of(half.shape[0], 128):
        slope[c, :] = half_silu(half[c, :])[1].astype(BF16)


def encode_back_kernel(
    grad_local, back_local, normed, inverse, slope, pick_goal, sum_rim, gain, w_source2, w_out, *refs
):
    received, (grad, near, far, updated16) = refs[:-4], refs[-4:]
    coarse = updated16.shape[0]
    rim = near.shape[0]
    total = received[0][...].astype(F32)
    for r in received[1:]:
        total = total + r[...].astype(F32)
    updated = grad_local[:coarse, :] + mm_t(total.astype(BF16), w_source2[...])
    updated16[...] = updated
    back = normalise_back(
        centred(updated * as_row(gain)), normed[:coarse, :], inverse[:coarse, :1]
    )
    back = (0.5 * mm_t(back.astype(BF16), w_out[...])).astype(BF16)
    back = jnp.concatenate([back, back_local[coarse:, :]], axis=0)
    for c in pieces_of(slope.shape[0], 256):
        grad[c, :] = (mm(pick_goal[c, :], back) * slope[c, :].astype(F32)).astype(BF16)
    near[...] = mm(sum_rim[:rim, :], grad[...]).astype(BF16)
    far[...] = mm(sum_rim[rim:, :], grad[...]).astype(BF16)


def own_back_kernel(
    grad, live_send, live_goal, grad_local, updated16, w_source, w_dest, mesh_grad, own
):
    coarse = updated16.shape[0]
    rows = grad_local.shape[0]
    dest = mm(spread(live_goal[...], 0, rows), grad[...]).astype(BF16)
    updated = jnp.concatenate([updated16[...], grad_local[coarse:, :]], axis=0)
    mesh_grad[...] = (updated + mm_t(dest, w_dest[...])).astype(BF16)
    source = mm(spread(live_send[...], 0, own.shape[0]), grad[...]).astype(BF16)
    own[...] = mm_t(source, w_source[...])


def finish_kernel(halo, own, near, far, w_source, out_hbm, out, sems):
    rows_near, rows_far = halves(as_row(halo), even_patch())
    peers = jnp.concatenate([near[...], far[...]], axis=0)
    projected = mm_t(peers, w_source[...]).astype(BF16)
    where = jnp.concatenate([rows_near, rows_far], axis=1)
    copies = []
    for i, c in enumerate(pieces_of(own.shape[0], own.shape[0] // 4)):
        chosen = spread(where, c.start, c.stop - c.start)
        out[c, :] = (own[c, :] + mm(chosen, projected)).astype(BF16)
        copies.append(pltpu.make_async_copy(out.at[c], out_hbm.at[c], sems.at[i]))
        copies[-1].start()
    for copy in copies:
        copy.wait()


SMEM = pl.BlockSpec(memory_space=pltpu.SMEM)
HBM = pl.BlockSpec(memory_space=pltpu.HBM)
VMEM = pl.BlockSpec(memory_space=pltpu.VMEM)
MICROSECOND = 1 << 30


def call(kernel, arrays, outs, cost, raw=0, scalars=0, scratch=(), out_space=None):
    return pl.pallas_call(
        kernel,
        out_shape=[jax.ShapeDtypeStruct(s, d) for s, d in outs],
        in_specs=[HBM] * raw + [SMEM] * scalars + [VMEM] * (len(arrays) - raw - scalars),
        out_specs=[out_space or VMEM] * len(outs),
        scratch_shapes=list(scratch),
        compiler_params=pltpu.CompilerParams(vmem_limit_bytes=24 << 20),
        cost_estimate=pl.CostEstimate(
            flops=int(cost * MICROSECOND), bytes_accessed=1 << 20, transcendentals=0
        ),
    )(*(pltpu.with_memory_space_constraint(x, pltpu.HBM) for x in arrays[:raw]), *arrays[raw:])


def swap_halo(near, far, n):
    far_pairs = [(i, (i + 1) % n if i % 2 else (i - 1) % n) for i in range(n)]
    far = lax.ppermute(far, "patch", far_pairs)
    near = lax.ppermute(near, "patch", [(i, i ^ 1) for i in range(n)])
    return near, far


def swap_coarse(pieces, n):
    out = []
    for k, piece in enumerate(pieces, 1):
        out.append(lax.ppermute(piece, "group", [(i, i ^ k) for i in range(n)]))
    return out


def on_device(
    grid_latent,
    mesh_latent,
    cotangent,
    halo_rows,
    encoder_sender,
    encoder_target,
    encoder_count,
    process_sender,
    process_target,
    process_count,
    encoder_source,
    encoder_dest,
    encoder_output,
    encoder_gain,
    process_source,
    process_dest,
    process_output,
    process_gain,
):
    patches, groups = lax.axis_size("patch"), lax.axis_size("group")
    grid_rows, width = grid_latent.shape
    mesh_rows = mesh_latent.shape[0]
    hidden_size = encoder_source.shape[1]
    coarse = mesh_rows // 16
    rim = halo_rows.shape[0] // 2
    slots, slots2 = encoder_sender.shape[0], process_sender.shape[0]

    row_form, row_form2 = ((1, slots), I32), ((1, slots2), I32)
    column_form2 = ((slots2, LANES), I32)
    remote = coarse * (groups - 1)
    near, far, grid = call(
        select_kernel,
        [halo_rows, grid_latent],
        [((rim, width), BF16)] * 2 + [((grid_rows, width), BF16)],
        4,
        raw=2,
        scratch=[pltpu.VMEM(halo_rows.shape, I32), pltpu.SemaphoreType.DMA((2,))],
    )
    near, far = swap_halo(near, far, patches)
    (
        part,
        live_send,
        live_goal,
        live_send2,
        live_goal2,
        send_col2,
        goal_col2,
        pick_rim,
        pick_goal,
    ) = call(
        functools.partial(encode_local_kernel, coarse),
        [
            jnp.concatenate([encoder_count, process_count]),
            encoder_sender,
            encoder_target,
            process_sender,
            process_target,
            grid,
            mesh_latent,
            encoder_source,
            encoder_dest,
        ],
        [((slots, hidden_size), F32), row_form, row_form, row_form2, row_form2]
        + [column_form2, column_form2]
        + [((slots, 2 * rim), BF16), ((slots, mesh_rows), BF16)],
        2,
        scalars=1,
    )
    hidden, half, updated16 = call(
        functools.partial(encode_halo_kernel, coarse),
        [
            near,
            far,
            part,
            pick_rim,
            live_goal,
            mesh_latent,
            encoder_source,
            encoder_output,
            encoder_gain,
        ],
        [((slots, hidden_size), BF16), ((slots, hidden_size), F32), ((coarse, width), BF16)],
        2,
    )
    shifts = swap_coarse([updated16] * (groups - 1), groups)
    normed, inverse, part2, pick_goal2, pick_coarse, sum_goal2, sum_coarse, centre2 = call(
        process_local_kernel,
        [
            hidden,
            live_goal,
            mesh_latent,
            send_col2,
            goal_col2,
            live_send2,
            live_goal2,
            cotangent,
            encoder_output,
            encoder_gain,
            process_gain,
            process_source,
            process_dest,
        ],
        [
            ((mesh_rows, width), F32),
            ((mesh_rows, LANES), F32),
            ((slots2, hidden_size), F32),
            ((slots2, mesh_rows), BF16),
            ((slots2, ceil_to(remote, LANES)), BF16),
            ((mesh_rows, slots2), BF16),
            ((remote, slots2), BF16),
            ((mesh_rows, width), F32),
        ],
        2,
    )
    grad2, *pieces = call(
        functools.partial(process_kernel, coarse),
        [
            part2,
            pick_goal2,
            pick_coarse,
            sum_goal2,
            sum_coarse,
            centre2,
            process_source,
            process_output,
            *shifts,
        ],
        [((slots2, hidden_size), BF16)] + [((coarse, hidden_size), BF16)] * (groups - 1),
        2,
        scratch=[pltpu.VMEM((slots2, hidden_size), BF16), pltpu.VMEM((slots2, hidden_size), F32)],
    )
    pieces = swap_coarse(pieces, groups)
    grad_local, back, slope, sum_rim = call(
        functools.partial(process_back_kernel, grid_rows),
        [
            half,
            grad2,
            live_send,
            live_send2,
            sum_goal2,
            cotangent,
            process_source,
            process_dest,
            encoder_output,
            encoder_gain,
            normed,
            inverse,
        ],
        [
            ((mesh_rows, width), F32),
            ((mesh_rows, hidden_size), BF16),
            ((slots, hidden_size), BF16),
            ((2 * rim, slots), BF16),
        ],
        2,
    )
    grad, near, far, grad16 = call(
        encode_back_kernel,
        [
            grad_local,
            back,
            normed,
            inverse,
            slope,
            pick_goal,
            sum_rim,
            encoder_gain,
            process_source,
            encoder_output,
            *pieces,
        ],
        [((slots, hidden_size), BF16)]
        + [((rim, hidden_size), BF16)] * 2
        + [((coarse, width), F32)],
        2,
    )
    near, far = swap_halo(near, far, patches)
    mesh_grad, own = call(
        own_back_kernel,
        [grad, live_send, live_goal, grad_local, grad16, encoder_source, encoder_dest],
        [((mesh_rows, width), BF16), ((grid_rows, width), F32)],
        2,
    )
    (grid_grad,) = call(
        finish_kernel,
        [halo_rows, own, near, far, encoder_source],
        [((grid_rows, width), BF16)],
        2,
        scratch=[pltpu.VMEM((grid_rows, width), BF16), pltpu.SemaphoreType.DMA((4,))],
        out_space=HBM,
    )
    return grid_grad, mesh_grad


def solution(mesh):
    rows, flat, whole = P(("patch", "group"), None), P(("patch", "group")), P()
    return jax.shard_map(
        on_device,
        mesh=mesh,
        in_specs=(rows,) * 3 + (flat,) * 7 + (whole,) * 8,
        out_specs=(rows, rows),
        check_vma=False,
    )
```

time: 38.2 us -> 37.9 us (level)
  waiting for transfers between devices: 7.55 us -> 6.27 us
  starting transfers between devices: 14 us -> 14.9 us
    ppermute x10, waiting for transfers between devices: 7.55 us -> 6.27 us  [the longest x6 3.61 us: swap_coarse(): out.append(lax.ppermute(piece, 'group', [(i, i ^ k) for i in range(n)]))]
    ppermute x10, starting transfers between devices: 14 us -> 14.9 us  [the longest x6 8.9 us: swap_coarse(): out.append(lax.ppermute(piece, 'group', [(i, i ^ k) for i in range(n)]))]
  transfers between devices with their start and end apart: 10 -> 10, of which waited for: 5 -> 4; matrix products, arithmetic and copies ran while one was open for 0% -> 0% of each run, Pallas kernels for 17% -> 18%
where the time goes in v3:
time: 37.9 us; the launch traced here: 37.7 us
  starting transfers between devices  14.9 us (39%)
  Pallas kernels  14.2 us (37%)
  waiting for transfers between devices  6.27 us (17%)
  between operations  2.2 us (6%)
    pallas_call x9, Pallas kernels, call(): pl.pallas_call(kernel, out_shape=[jax.ShapeDtypeStruct(s, d) for s, d in...  14.2 us
    ppermute x6, starting transfers between devices, swap_coarse(): out.append(lax.ppermute(piece, 'group', [(i, i ^ k) for i in range(n)]))  8.9 us
    ppermute x2, starting transfers between devices, swap_halo(): far = lax.ppermute(far, 'patch', far_pairs)  5.36 us
    ppermute x6, waiting for transfers between devices, swap_coarse(): out.append(lax.ppermute(piece, 'group', [(i, i ^ k) for i in range(n)]))  3.61 us
    ppermute x2, waiting for transfers between devices, swap_halo(): far = lax.ppermute(far, 'patch', far_pairs)  2.65 us
  transfers between devices with their start and end apart: 10, of which 4 were waited for; matrix products, arithmetic and copies ran while one was open for 0% of the time, Pallas kernels for 18%

profile of v3, /device:TPU:0, one launch (start us, length us, event | category | flops | bytes accessed | tf_op | source)
XLA Modules:
  0.0 37.7 jit_solution(18117766000243508430)
XLA Ops:
  0.7 1.5 %shard_map.185 = (bf16[128,512]{1,0:T(8,128)(2,1)S(1)}, bf16[128,512]{1,0:T(8,128)(2,1)S(1)}, bf16[512,512]{1,0:T(8,128)(2,1)S(1)}) custom-call(s32[256]{0:T(256)} %halo.1, bf16[512,512]{1,0:T(8,128)(2,1)} %grid_hbm.1), custom_call_target="tpu_custom_call" | custom-call | flops 4294967296 | bytes 1048576 | tf_op jit(solution)/shard_map/pallas_call | solution.py:358
  2.2 0.6 %collective-permute-start = (bf16[128,512]{1,0:T(8,128)(2,1)S(1)}, bf16[128,512]{1,0:T(8,128)(2,1)S(1)}, u32[]{:S(2)}, u32[]{:S(2)}) collective-permute-start(bf16[128,512]{1,0:T(8,128)(2,1)S(1)} %get-tuple-element.39), channel_id=1, source_target_pairs={{0,4},{4,0},{8,12},{12,8},{16,20},{20,16},{24,28},{28,24},{1,5},{5... | collective-permute-start | bytes 393224 | tf_op jit(solution)/shard_map/ppermute | solution.py:374
  2.7 3.5 %collective-permute-start.1 = (bf16[128,512]{1,0:T(8,128)(2,1)S(1)}, bf16[128,512]{1,0:T(8,128)(2,1)S(1)}, u32[]{:S(2)}, u32[]{:S(2)}) collective-permute-start(bf16[128,512]{1,0:T(8,128)(2,1)S(1)} %get-tuple-element.40), channel_id=1, source_target_pairs={{0,28},{4,8},{8,4},{12,16},{16,12},{20,24},{24,20},{28,0},{1,29},{... | collective-permute-start | bytes 393224 | tf_op jit(solution)/shard_map/ppermute | solution.py:373
  7.6 0.1 pad_add_fusion.counts
  7.7 0.0 copy-start.2
  7.7 0.0 copy-start.13
  7.7 2.0 %shard_map.186 = (f32[768,512]{1,0:T(8,128)S(1)}, s32[1,768]{1,0:T(1,128)S(1)}, s32[1,768]{1,0:T(1,128)S(1)}, s32[1,768]{1,0:T(1,128)S(1)}, s32[1,768]{1,0:T(1,1...) custom-call(s32[2]{0:T(128)S(1)} %pad_add_fusion.counts, ...), custom_call_target="tpu_custom_call" | custom-call | flops 2147483648 | bytes 1048576 | tf_op jit(solution)/shard_map/pallas_call | solution.py:358
  9.7 0.0 collective-permute-done.near
  9.7 0.0 copy-start.1
  9.8 0.0 copy-start.3
  9.8 0.0 copy-start.7
  9.8 0.0 copy-start.12
  9.8 1.2 %shard_map.187 = (bf16[768,512]{1,0:T(8,128)(2,1)S(1)}, f32[768,512]{1,0:T(8,128)S(1)}, bf16[16,512]{1,0:T(8,128)(2,1)S(1)}) custom-call(bf16[128,512]{1,0:T(8,128)(2,1)S(1)} %collective-permute-done.near, bf16[128,512]{1,0:T(8,128)(2,1)S(1)} %collective-permute-done.1.far, f32[768,512]{1,0:T(8,128)S(1)} %get-tuple-element.42.part, ...), custom_call_target="tpu_custom_call" | custom-call | flops 2147483648 | bytes 1048576 | tf_op jit(solution)/shard_map/pallas_call | solution.py:358
  11.0 1.7 %collective-permute-start.2 = (bf16[16,512]{1,0:T(8,128)(2,1)S(1)}, bf16[16,512]{1,0:T(8,128)(2,1)S(1)}, u32[]{:S(2)}, u32[]{:S(2)}) collective-permute-start(bf16[16,512]{1,0:T(8,128)(2,1)S(1)} %get-tuple-element.57), channel_id=1, source_target_pairs={{0,1},{1,0},{2,3},{3,2},{4,5},{5,4},{6,7},{7,6},{8,9},{9,8},{10,11... | collective-permute-start | bytes 49160 | tf_op jit(solution)/shard_map/ppermute | solution.py:381
  12.7 2.6 %collective-permute-start.3 = (bf16[16,512]{1,0:T(8,128)(2,1)S(1)}, bf16[16,512]{1,0:T(8,128)(2,1)S(1)}, u32[]{:S(2)}, u32[]{:S(2)}) collective-permute-start(bf16[16,512]{1,0:T(8,128)(2,1)S(1)} %get-tuple-element.57), channel_id=1, source_target_pairs={{0,2},{1,3},{2,0},{3,1},{4,6},{5,7},{6,4},{7,5},{8,10},{9,11},{10,... | collective-permute-start | bytes 49160 | tf_op jit(solution)/shard_map/ppermute | solution.py:381
  15.3 0.1 collective-permute-start.4
  15.4 0.0 copy-start
  15.5 1.8 %shard_map.188 = (f32[256,512]{1,0:T(8,128)S(1)}, f32[256,128]{1,0:T(8,128)S(1)}, f32[768,512]{1,0:T(8,128)S(1)}, bf16[768,256]{1,0:T(8,128)(2,1)S(1)}, bf16[768...) custom-call(bf16[768,512]{1,0:T(8,128)(2,1)S(1)} %get-tuple-element.4, ...), custom_call_target="tpu_custom_call" | custom-call | flops 2147483648 | bytes 1048576 | tf_op jit(solution)/shard_map/pallas_call | solution.py:358
  17.3 0.1 collective-permute-done.3.refs_1_
  17.3 3.5 %collective-permute-done.4.refs_2_ = bf16[16,512]{1,0:T(8,128)(2,1)S(1)} collective-permute-done((bf16[16,512]{1,0:T(8,128)(2,1)S(1)}, bf16[16,512]{1,0:T(8,128)(2,1)S(1)}, u32[]{:S(2)}, u32[]{:S(2)}) %collective-permute-start.4) | collective-permute-done | bytes 16416 | tf_op jit(solution)/shard_map/ppermute | solution.py:381
  20.8 2.1 %shard_map.189 = (bf16[768,512]{1,0:T(8,128)(2,1)S(1)}, bf16[16,512]{1,0:T(8,128)(2,1)S(1)}, bf16[16,512]{1,0:T(8,128)(2,1)S(1)}, bf16[16,512]{1,0:T(8,128)(2,1)S(1)}) custom-call(f32[768,512]{1,0:T(8,128)S(1)} %get-tuple-element.51.part, bf16[768,256]{1,0:T(8,128)(2,1)S(1)} %get-tuple-element.52.pick_goal2, ...), custom_call_target="tpu_custom_call" | custom-call | flops 2147483648 | bytes 1048576 | tf_op jit(solution)/shard_map/pallas_call | solution.py:358
  22.9 0.1 collective-permute-start.5
  23.0 0.7 %collective-permute-start.6 = (bf16[16,512]{1,0:T(8,128)(2,1)S(1)}, bf16[16,512]{1,0:T(8,128)(2,1)S(1)}, u32[]{:S(2)}, u32[]{:S(2)}) collective-permute-start(bf16[16,512]{1,0:T(8,128)(2,1)S(1)} %get-tuple-element.68), channel_id=1, source_target_pairs={{0,2},{1,3},{2,0},{3,1},{4,6},{5,7},{6,4},{7,5},{8,10},{9,11},{10,... | collective-permute-start | bytes 49160 | tf_op jit(solution)/shard_map/ppermute | solution.py:381
  23.7 3.6 %collective-permute-start.7 = (bf16[16,512]{1,0:T(8,128)(2,1)S(1)}, bf16[16,512]{1,0:T(8,128)(2,1)S(1)}, u32[]{:S(2)}, u32[]{:S(2)}) collective-permute-start(bf16[16,512]{1,0:T(8,128)(2,1)S(1)} %get-tuple-element.69), channel_id=1, source_target_pairs={{0,3},{1,2},{2,1},{3,0},{4,7},{5,6},{6,5},{7,4},{8,11},{9,10},{10,... | collective-permute-start | bytes 49160 | tf_op jit(solution)/shard_map/ppermute | solution.py:381
  27.4 1.8 %shard_map.190 = (f32[256,512]{1,0:T(8,128)S(1)}, bf16[256,512]{1,0:T(8,128)(2,1)S(1)}, bf16[768,512]{1,0:T(8,128)(2,1)S(1)}, bf16[256,768]{1,0:T(8,128)(2,1)S(1)}) custom-call(f32[768,512]{1,0:T(8,128)S(1)} %get-tuple-element.45.half, bf16[768,512]{1,0:T(8,128)(2,1)S(1)} %get-tuple-element.58.grad, s32[1,768]{1,0:T(1,128)S(1)} %get-tuple-element.59.live_send, ...), custom_call_target="tpu_custom_call" | custom-call | flops 2147483648 | bytes 1048576 | tf_op jit(solution)/shard_map/pallas_call | solution.py:358
  29.2 0.1 collective-permute-done.7.refs_2_
  29.3 1.3 %shard_map.191 = (bf16[768,512]{1,0:T(8,128)(2,1)S(1)}, bf16[128,512]{1,0:T(8,128)(2,1)S(1)}, bf16[128,512]{1,0:T(8,128)(2,1)S(1)}, f32[16,512]{1,0:T(8,128)S(1)}) custom-call(f32[256,512]{1,0:T(8,128)S(1)} %get-tuple-element.62.grad_local, bf16[256,512]{1,0:T(8,128)(2,1)S(1)} %get-tuple-element.63.back_local, f32[256,512]{1,0:T(8,128)S(1)} %get-tuple-element.60.normed, ...), custom_call_target="tpu_custom_call" | custom-call | flops 2147483648 | bytes 1048576 | tf_op jit(solution)/shard_map/pallas_call | solution.py:358
  30.5 0.1 collective-permute-start.8
  30.6 1.8 %collective-permute-start.9 = (bf16[128,512]{1,0:T(8,128)(2,1)S(1)}, bf16[128,512]{1,0:T(8,128)(2,1)S(1)}, u32[]{:S(2)}, u32[]{:S(2)}) collective-permute-start(bf16[128,512]{1,0:T(8,128)(2,1)S(1)} %get-tuple-element.74), channel_id=1, source_target_pairs={{0,28},{4,8},{8,4},{12,16},{16,12},{20,24},{24,20},{28,0},{1,29},{... | collective-permute-start | bytes 393224 | tf_op jit(solution)/shard_map/ppermute | solution.py:373
  32.4 1.3 %shard_map.192 = (bf16[256,512]{1,0:T(8,128)(2,1)}, f32[512,512]{1,0:T(8,128)S(1)}) custom-call(bf16[768,512]{1,0:T(8,128)(2,1)S(1)} %get-tuple-element.70.grad, s32[1,768]{1,0:T(1,128)S(1)} %get-tuple-element.59.live_send, s32[1,768]{1,0:T(1,128)S(1)} %get-tuple-element.44.live_goal, f32[256,512]{1,0:T(8,128)S(1)} %get-tuple-element.62.grad_local, ...), custom_call_target="tpu_custom_call" | custom-call | flops 2147483648 | bytes 1048576 | tf_op jit(solution)/shard_map/pallas_call | solution.py:358
  33.7 2.7 %collective-permute-done.9.far = bf16[128,512]{1,0:T(8,128)(2,1)S(1)} collective-permute-done((bf16[128,512]{1,0:T(8,128)(2,1)S(1)}, bf16[128,512]{1,0:T(8,128)(2,1)S(1)}, u32[]{:S(2)}, u32[]{:S(2)}) %collective-permute-start.9) | collective-permute-done | bytes 131104 | tf_op jit(solution)/shard_map/ppermute | solution.py:373
  36.4 1.3 %shard_map.193 = bf16[512,512]{1,0:T(8,128)(2,1)} custom-call(s32[256]{0:T(256)S(1)} %copy-done.14, f32[512,512]{1,0:T(8,128)S(1)} %get-tuple-element.72.own, bf16[128,512]{1,0:T(8,128)(2,1)S(1)} %collective-permute-done.8.near, bf16[128,512]{1,0:T(8,128)(2,1)S(1)} %collective-permute-done.9.far, bf16[512,512]{1,0:T(8,128)(2,1)S(1)} %copy-done.5), custom_call_target="tpu_custom_call" | custom-call | flops 2147483648 | bytes 1048576 | tf_op jit(solution)/shard_map/pallas_call | solution.py:358
  (28 shorter events, 0.1 us)
Async XLA Ops:
  0.6 7.0 %copy-start.6 = (bf16[256,512]{1,0:T(8,128)(2,1)S(1)}, bf16[256,512]{1,0:T(8,128)(2,1)}, u32[]{:S(2)}) copy-start(bf16[256,512]{1,0:T(8,128)(2,1)} %mesh.5) | copy-start | bytes 786436
  0.6 7.0 %copy-start.8 = (s32[768]{0:T(1024)S(1)}, s32[768]{0:T(1024)}, u32[]{:S(2)}) copy-start(s32[768]{0:T(1024)} %sender.1) | copy-start | bytes 9220
  0.7 7.0 %copy-start.9 = (s32[768]{0:T(1024)S(1)}, s32[768]{0:T(1024)}, u32[]{:S(2)}) copy-start(s32[768]{0:T(1024)} %target.1) | copy-start | bytes 9220
  0.7 7.0 %copy-start.10 = (s32[768]{0:T(1024)S(1)}, s32[768]{0:T(1024)}, u32[]{:S(2)}) copy-start(s32[768]{0:T(1024)} %sender2.1) | copy-start | bytes 9220
  0.7 7.0 %copy-start.11 = (s32[768]{0:T(1024)S(1)}, s32[768]{0:T(1024)}, u32[]{:S(2)}) copy-start(s32[768]{0:T(1024)} %target2.1) | copy-start | bytes 9220
  0.7 7.0 %copy-start.5 = (bf16[512,512]{1,0:T(8,128)(2,1)S(1)}, bf16[512,512]{1,0:T(8,128)(2,1)}, u32[]{:S(2)}) copy-start(bf16[512,512]{1,0:T(8,128)(2,1)} %w_source.13) | copy-start | bytes 1572868
  0.7 7.0 %copy-start.4 = (bf16[512,512]{1,0:T(8,128)(2,1)S(1)}, bf16[512,512]{1,0:T(8,128)(2,1)}, u32[]{:S(2)}) copy-start(bf16[512,512]{1,0:T(8,128)(2,1)} %w_dest.7) | copy-start | bytes 1572868
  2.2 7.5 %collective-permute-start = (bf16[128,512]{1,0:T(8,128)(2,1)S(1)}, bf16[128,512]{1,0:T(8,128)(2,1)S(1)}, u32[]{:S(2)}, u32[]{:S(2)}) collective-permute-start(bf16[128,512]{1,0:T(8,128)(2,1)S(1)} %get-tuple-element.39), channel_id=1, source_target_pairs={{0,4},{4,0},{8,12},{12,8},{16,20},{20,16},{24,28},{28,24},{1,5},{5... | collective-permute-start | bytes 393224 | tf_op jit(solution)/shard_map/ppermute | solution.py:374
  2.7 7.0 %collective-permute-start.1 = (bf16[128,512]{1,0:T(8,128)(2,1)S(1)}, bf16[128,512]{1,0:T(8,128)(2,1)S(1)}, u32[]{:S(2)}, u32[]{:S(2)}) collective-permute-start(bf16[128,512]{1,0:T(8,128)(2,1)S(1)} %get-tuple-element.40), channel_id=1, source_target_pairs={{0,28},{4,8},{8,4},{12,16},{16,12},{20,24},{24,20},{28,0},{1,29},{... | collective-permute-start | bytes 393224 | tf_op jit(solution)/shard_map/ppermute | solution.py:373
  7.7 2.0 %copy-start.2 = (bf16[512,512]{1,0:T(8,128)(2,1)S(1)}, bf16[512,512]{1,0:T(8,128)(2,1)}, u32[]{:S(2)}) copy-start(bf16[512,512]{1,0:T(8,128)(2,1)} %w_out.9) | copy-start | bytes 1572868
  7.7 2.0 %copy-start.13 = (f32[512]{0:T(512)S(1)}, f32[512]{0:T(512)}, u32[]{:S(2)}) copy-start(f32[512]{0:T(512)} %gain.7) | copy-start | bytes 6148
  9.7 5.7 %copy-start.1 = (bf16[512,512]{1,0:T(8,128)(2,1)S(1)}, bf16[512,512]{1,0:T(8,128)(2,1)}, u32[]{:S(2)}) copy-start(bf16[512,512]{1,0:T(8,128)(2,1)} %w_dest.6) | copy-start | bytes 1572868
  9.8 5.7 %copy-start.3 = (bf16[512,512]{1,0:T(8,128)(2,1)S(1)}, bf16[512,512]{1,0:T(8,128)(2,1)}, u32[]{:S(2)}) copy-start(bf16[512,512]{1,0:T(8,128)(2,1)} %w_source2.1) | copy-start | bytes 1572868
  9.8 5.7 %copy-start.7 = (bf16[256,512]{1,0:T(8,128)(2,1)S(1)}, bf16[256,512]{1,0:T(8,128)(2,1)}, u32[]{:S(2)}) copy-start(bf16[256,512]{1,0:T(8,128)(2,1)} %cotangent.3) | copy-start | bytes 786436
  9.8 5.7 %copy-start.12 = (f32[512]{0:T(512)S(1)}, f32[512]{0:T(512)}, u32[]{:S(2)}) copy-start(f32[512]{0:T(512)} %gain2.1) | copy-start | bytes 6148
  11.0 6.3 %collective-permute-start.2 = (bf16[16,512]{1,0:T(8,128)(2,1)S(1)}, bf16[16,512]{1,0:T(8,128)(2,1)S(1)}, u32[]{:S(2)}, u32[]{:S(2)}) collective-permute-start(bf16[16,512]{1,0:T(8,128)(2,1)S(1)} %get-tuple-element.57), channel_id=1, source_target_pairs={{0,1},{1,0},{2,3},{3,2},{4,5},{5,4},{6,7},{7,6},{8,9},{9,8},{10,11... | collective-permute-start | bytes 49160 | tf_op jit(solution)/shard_map/ppermute | solution.py:381
  12.7 4.6 %collective-permute-start.3 = (bf16[16,512]{1,0:T(8,128)(2,1)S(1)}, bf16[16,512]{1,0:T(8,128)(2,1)S(1)}, u32[]{:S(2)}, u32[]{:S(2)}) collective-permute-start(bf16[16,512]{1,0:T(8,128)(2,1)S(1)} %get-tuple-element.57), channel_id=1, source_target_pairs={{0,2},{1,3},{2,0},{3,1},{4,6},{5,7},{6,4},{7,5},{8,10},{9,11},{10,... | collective-permute-start | bytes 49160 | tf_op jit(solution)/shard_map/ppermute | solution.py:381
  15.3 5.5 %collective-permute-start.4 = (bf16[16,512]{1,0:T(8,128)(2,1)S(1)}, bf16[16,512]{1,0:T(8,128)(2,1)S(1)}, u32[]{:S(2)}, u32[]{:S(2)}) collective-permute-start(bf16[16,512]{1,0:T(8,128)(2,1)S(1)} %get-tuple-element.57), channel_id=1, source_target_pairs={{0,3},{1,2},{2,1},{3,0},{4,7},{5,6},{6,5},{7,4},{8,11},{9,10},{10,... | collective-permute-start | bytes 49160 | tf_op jit(solution)/shard_map/ppermute | solution.py:381
  15.4 5.4 %copy-start = (bf16[512,512]{1,0:T(8,128)(2,1)S(1)}, bf16[512,512]{1,0:T(8,128)(2,1)}, u32[]{:S(2)}) copy-start(bf16[512,512]{1,0:T(8,128)(2,1)} %w_out.7) | copy-start | bytes 1572868
  22.9 6.3 %collective-permute-start.5 = (bf16[16,512]{1,0:T(8,128)(2,1)S(1)}, bf16[16,512]{1,0:T(8,128)(2,1)S(1)}, u32[]{:S(2)}, u32[]{:S(2)}) collective-permute-start(bf16[16,512]{1,0:T(8,128)(2,1)S(1)} %get-tuple-element.67), channel_id=1, source_target_pairs={{0,1},{1,0},{2,3},{3,2},{4,5},{5,4},{6,7},{7,6},{8,9},{9,8},{10,11... | collective-permute-start | bytes 49160 | tf_op jit(solution)/shard_map/ppermute | solution.py:381
  23.0 6.2 %collective-permute-start.6 = (bf16[16,512]{1,0:T(8,128)(2,1)S(1)}, bf16[16,512]{1,0:T(8,128)(2,1)S(1)}, u32[]{:S(2)}, u32[]{:S(2)}) collective-permute-start(bf16[16,512]{1,0:T(8,128)(2,1)S(1)} %get-tuple-element.68), channel_id=1, source_target_pairs={{0,2},{1,3},{2,0},{3,1},{4,6},{5,7},{6,4},{7,5},{8,10},{9,11},{10,... | collective-permute-start | bytes 49160 | tf_op jit(solution)/shard_map/ppermute | solution.py:381
  23.7 5.5 %collective-permute-start.7 = (bf16[16,512]{1,0:T(8,128)(2,1)S(1)}, bf16[16,512]{1,0:T(8,128)(2,1)S(1)}, u32[]{:S(2)}, u32[]{:S(2)}) collective-permute-start(bf16[16,512]{1,0:T(8,128)(2,1)S(1)} %get-tuple-element.69), channel_id=1, source_target_pairs={{0,3},{1,2},{2,1},{3,0},{4,7},{5,6},{6,5},{7,4},{8,11},{9,10},{10,... | collective-permute-start | bytes 49160 | tf_op jit(solution)/shard_map/ppermute | solution.py:381
  30.5 3.2 %collective-permute-start.8 = (bf16[128,512]{1,0:T(8,128)(2,1)S(1)}, bf16[128,512]{1,0:T(8,128)(2,1)S(1)}, u32[]{:S(2)}, u32[]{:S(2)}) collective-permute-start(bf16[128,512]{1,0:T(8,128)(2,1)S(1)} %get-tuple-element.73), channel_id=1, source_target_pairs={{0,4},{4,0},{8,12},{12,8},{16,20},{20,16},{24,28},{28,24},{1,5},{5... | collective-permute-start | bytes 393224 | tf_op jit(solution)/shard_map/ppermute | solution.py:374
  30.6 5.8 %collective-permute-start.9 = (bf16[128,512]{1,0:T(8,128)(2,1)S(1)}, bf16[128,512]{1,0:T(8,128)(2,1)S(1)}, u32[]{:S(2)}, u32[]{:S(2)}) collective-permute-start(bf16[128,512]{1,0:T(8,128)(2,1)S(1)} %get-tuple-element.74), channel_id=1, source_target_pairs={{0,28},{4,8},{8,4},{12,16},{16,12},{20,24},{24,20},{28,0},{1,29},{... | collective-permute-start | bytes 393224 | tf_op jit(solution)/shard_map/ppermute | solution.py:373
  32.4 4.0 %copy-start.14 = (s32[256]{0:T(256)S(1)}, s32[256]{0:T(256)}, u32[]{:S(2)}) copy-start(s32[256]{0:T(256)} %halo.1) | copy-start | bytes 3076

commit v4 on v3

--- a/solution.py
+++ b/solution.py
@@ -10,9 +10,11 @@
 
 EPSILON = 1e-05
 LANES = 128
+FIRST = 256
 F32 = jnp.float32
 BF16 = jnp.bfloat16
 I32 = jnp.int32
+I16 = jnp.int16
 
 
 def mm(a, b):
@@ -38,21 +40,24 @@
     n = row.shape[1]
     parts = []
     for i in range(0, n, LANES):
-        parts.append(jnp.broadcast_to(row[:, i : i + LANES], (LANES, LANES)).T)
+        parts.append(jnp.broadcast_to(row[:, i : i + LANES], (LANES, LANES)).T.astype(I16))
     return jnp.concatenate(parts, axis=0)
+
+
+def one_hot(equal):
+    return jnp.where(equal, jnp.ones((), BF16), jnp.zeros((), BF16))
 
 
 def pick(columns, first, width):
     lane = lax.broadcasted_iota(I32, columns.shape, 1)
-    parts = []
-    for i in range(0, width, LANES):
-        parts.append(jnp.where(columns == lane + (first + i), 1.0, 0.0).astype(BF16))
+    parts = [one_hot(columns == (lane + (first + i)).astype(I16)) for i in range(0, width, LANES)]
     return parts[0] if len(parts) == 1 else jnp.concatenate(parts, axis=1)
 
 
 def spread(row, first, height):
     shape = (height, row.shape[1])
-    return jnp.where(row == lax.broadcasted_iota(I32, shape, 0) + first, 1.0, 0.0).astype(BF16)
+    number = lax.broadcasted_iota(I32, shape, 0) + first
+    return one_hot(jnp.broadcast_to(row, shape).astype(I16) == number.astype(I16))
 
 
 def only_live(rows, count):
@@ -121,6 +126,38 @@
     )
 
 
+def arrange(first, rows):
+    slots = first.shape[1]
+    groups = slots // LANES
+    flags = [first[:, i * LANES : (i + 1) * LANES] for i in range(groups)]
+    spare = ceil_to(groups, 8) - groups
+    stack = jnp.concatenate(flags + [jnp.zeros((spare, LANES), F32)] * bool(spare), axis=0)
+    shape = (LANES, LANES)
+    before = lax.broadcasted_iota(I32, shape, 0) <= lax.broadcasted_iota(I32, shape, 1)
+    sums = mm(stack.astype(BF16), jnp.where(before, 1.0, 0.0).astype(BF16))
+    total = jnp.zeros((1, 1), F32)
+    counted = []
+    for i in range(groups):
+        counted.append(sums[i : i + 1, :] + total)
+        total = total + sums[i : i + 1, LANES - 1 :]
+    counted = jnp.concatenate(counted, axis=1)
+    slot = lax.broadcasted_iota(I32, first.shape, 1).astype(F32)
+    place = jnp.where(first > 0.0, counted - 1.0, total + slot - counted)
+    order = spread(place.astype(I32), 0, slots)
+    digits = [d for row in rows for d in (row // LANES, row % LANES)]
+    digits = [d.astype(F32) for d in digits]
+    spare = ceil_to(len(digits), 8) - len(digits)
+    digits = jnp.concatenate(digits + [jnp.zeros((spare, slots), F32)] * bool(spare), axis=0)
+    moved = mm_t(digits.astype(BF16), order).astype(I32)
+    moved = [moved[2 * i : 2 * i + 1, :] * LANES + moved[2 * i + 1 : 2 * i + 2, :] for i in range(len(rows))]
+    return total, moved
+
+
+def flagged(condition, count):
+    slot = lax.broadcasted_iota(I32, condition.shape, 1)
+    return jnp.where(condition & (slot < count), 1.0, 0.0)
+
+
 def encode_local_kernel(
     coarse,
     counts,
@@ -132,7 +169,10 @@
     mesh,
     w_source,
     w_dest,
+    early,
     part,
+    hidden,
+    summed16,
     live_send,
     live_goal,
     live_send2,
@@ -146,19 +186,29 @@
     rim = pick_rim.shape[1] // 2
     source = (0.5 * mm(grid[...], w_source[...])).astype(BF16)
     dest = (0.5 * mm(mesh[...], w_dest[...])).astype(BF16)
-    send_col = to_columns(as_row(sender))
+    send = as_row(sender)
+    total, (send, goal) = arrange(flagged(send >= grid_rows, counts[0]), [send, as_row(target)])
+    early[:1, :] = jnp.broadcast_to(total, (1, LANES)).astype(I32)
+    send_col = to_columns(send)
     near_first, far_first = rim_starts(grid_rows, rim)
     pick_rim[:, :rim] = pick(send_col, near_first, rim)
     pick_rim[:, rim:] = pick(send_col, far_first, rim)
-    pick_goal[...] = pick(to_columns(as_row(target)), 0, rows)
-    moved = coarse_slots(as_row(sender2), rows, coarse, lax.axis_index("group"))
-    send_col2[...] = to_columns(moved)
-    goal_col2[...] = to_columns(as_row(target2))
-    part[...] = mm(pick(send_col, 0, grid_rows), source) + mm(pick_goal[...], dest)
-    live_send[...] = only_live(as_row(sender), counts[0])
-    live_goal[...] = only_live(as_row(target), counts[0])
-    live_send2[...] = only_live(moved, counts[1])
-    live_goal2[...] = only_live(as_row(target2), counts[1])
+    pick_goal[...] = pick(to_columns(goal), 0, rows)
+    live_send[...] = only_live(send, counts[0])
+    live_goal[...] = only_live(goal, counts[0])
+    for c in pieces_of(part.shape[0], FIRST):
+        u = mm(pick(send_col[c, :], 0, grid_rows), source) + mm(pick_goal[c, :], dest)
+        part[c, :] = u
+        if c.start:
+            hidden[c, :] = (u + u * jnp.tanh(u)).astype(BF16)
+    summed16[...] = mm(spread(live_goal[:, FIRST:], 0, coarse), hidden[FIRST:, :])
+    send2 = coarse_slots(as_row(sender2), rows, coarse, lax.axis_index("group"))
+    total, (send2, goal2) = arrange(flagged(send2 >= rows, counts[1]), [send2, as_row(target2)])
+    early[1:, :] = jnp.broadcast_to(total, (1, LANES)).astype(I32)
+    send_col2[...] = to_columns(send2)
+    goal_col2[...] = to_columns(goal2)
+    live_send2[...] = only_live(send2, counts[1])
+    live_goal2[...] = only_live(goal2, counts[1])
 
 
 def pieces_of(n, size):
@@ -167,28 +217,47 @@
 
 def encode_halo_kernel(
     coarse,
+    early,
     near,
     far,
     part,
+    hidden_local,
+    summed16,
     pick_rim,
     live_goal,
     mesh,
     w_source,
     w_out,
     gain,
+    half,
     hidden,
-    half,
     updated16,
 ):
+    number = jnp.max(early[:1, :])
     halo = jnp.concatenate([near[...], far[...]], axis=0)
     source = (0.5 * mm(halo, w_source[...])).astype(BF16)
-    for c in pieces_of(part.shape[0], 256):
+
+    def edges(c):
         u = part[c, :] + mm(pick_rim[c, :], source)
         half[c, :] = u
         hidden[c, :] = (u + u * jnp.tanh(u)).astype(BF16)
-    summed = mm(spread(live_goal[...], 0, coarse), hidden[...]).astype(BF16)
-    normed, _ = normalise(mm(summed, w_out[...]))
-    updated16[...] = (mesh[:coarse, :].astype(F32) + normed * as_row(gain)).astype(BF16)
+
+    def finish(summed):
+        normed, _ = normalise(mm(summed.astype(BF16), w_out[...]))
+        updated16[...] = (mesh[:coarse, :].astype(F32) + normed * as_row(gain)).astype(BF16)
+
+    edges(slice(0, FIRST))
+
+    @pl.when(number <= FIRST)
+    def _():
+        goal = spread(live_goal[:, :FIRST], 0, coarse)
+        finish(summed16[...] + mm(goal, hidden[:FIRST, :]))
+
+    @pl.when(number > FIRST)
+    def _():
+        for c in pieces_of(part.shape[0], FIRST)[1:]:
+            edges(c)
+        finish(mm(spread(live_goal[...], 0, coarse), hidden[...]))
 
 
 def process_local_kernel(
@@ -213,6 +282,8 @@
     sum_goal2,
     sum_coarse,
     centre2,
+    summed2,
+    hidden2,
 ):
     rows = mesh.shape[0]
     summed = mm(spread(live_goal[...], 0, rows), hidden[...]).astype(BF16)
@@ -227,48 +298,83 @@
     sum_goal2[...] = spread(live_goal2[...], 0, rows)
     sum_coarse[...] = spread(live_send2[...], rows, sum_coarse.shape[0])
     centre2[...] = centred(cotangent[...].astype(F32) * as_row(gain2))
-    part[...] = mm(pick(send_col2[...], 0, rows), source) + mm(pick_goal2[...], dest)
+    for c in pieces_of(part.shape[0], FIRST):
+        u = mm(pick(send_col2[c, :], 0, rows), source) + mm(pick_goal2[c, :], dest)
+        part[c, :] = u
+        if c.start:
+            hidden2[c, :] = (u + u * jnp.tanh(u)).astype(BF16)
+    summed2[...] = mm(sum_goal2[:, FIRST:], hidden2[FIRST:, :])
 
 
 def process_kernel(
     coarse,
+    early,
     part,
     pick_goal2,
     pick_coarse,
     sum_goal2,
     sum_coarse,
     centre2,
+    summed2,
     w_source,
     w_out,
     *refs,
 ):
     peers = sum_coarse.shape[0] // coarse
-    received, grad, returned = refs[:peers], refs[peers], refs[peers + 1 : -2]
-    hidden, slope = refs[-2:]
+    received, (half, grad_first, back_ref) = refs[:peers], refs[peers : peers + 3]
+    returned, (hidden, slope, grad) = refs[peers + 3 : -3], refs[-3:]
+    number = jnp.max(early[1:, :])
     rows = jnp.concatenate([r[...] for r in received], axis=0)
     source = (0.5 * mm(rows, w_source[...])).astype(BF16)
     spare = pick_coarse.shape[1] - source.shape[0]
     if spare:
         source = jnp.concatenate([source, jnp.zeros((spare, source.shape[1]), BF16)], axis=0)
-    for c in pieces_of(part.shape[0], 256):
-        value, double = half_silu(part[c, :] + mm(pick_coarse[c, :], source))
+
+    def edges(c):
+        u = part[c, :] + mm(pick_coarse[c, :], source)
+        half[c, :] = u
+        value, double = half_silu(u)
         hidden[c, :] = value.astype(BF16)
         slope[c, :] = double
-    summed = mm(sum_goal2[...], hidden[...]).astype(BF16)
-    normed, inverse = normalise(mm(summed, w_out[...]))
-    back = normalise_back(centre2[...], normed, inverse).astype(BF16)
-    back = (0.5 * mm_t(back, w_out[...])).astype(BF16)
-    for c in pieces_of(part.shape[0], 256):
-        grad[c, :] = (mm(pick_goal2[c, :], back) * slope[c, :]).astype(BF16)
-    sums = mm(sum_coarse[...], grad[...])
-    for i, out in enumerate(returned):
-        out[...] = sums[i * coarse : (i + 1) * coarse].astype(BF16)
+
+    def turn(summed):
+        normed, inverse = normalise(mm(summed.astype(BF16), w_out[...]))
+        back = normalise_back(centre2[...], normed, inverse).astype(BF16)
+        back = (0.5 * mm_t(back, w_out[...])).astype(BF16)
+        back_ref[...] = back
+        grad_first[...] = (mm(pick_goal2[:FIRST, :], back) * slope[:FIRST, :]).astype(BF16)
+        return back
+
+    def send(sums):
+        for i, out in enumerate(returned):
+            out[...] = sums[i * coarse : (i + 1) * coarse].astype(BF16)
+
+    edges(slice(0, FIRST))
+
+    @pl.when(number <= FIRST)
+    def _():
+        turn(summed2[...] + mm(sum_goal2[:, :FIRST], hidden[:FIRST, :]))
+        send(mm(sum_coarse[:, :FIRST], grad_first[...]))
+
+    @pl.when(number > FIRST)
+    def _():
+        later = pieces_of(part.shape[0], FIRST)[1:]
+        for c in later:
+            edges(c)
+        back = turn(mm(sum_goal2[...], hidden[...]))
+        grad[:FIRST, :] = grad_first[...]
+        for c in later:
+            grad[c, :] = (mm(pick_goal2[c, :], back) * slope[c, :]).astype(BF16)
+        send(mm(sum_coarse[...], grad[...]))
 
 
 def process_back_kernel(
     grid_rows,
     half,
-    grad,
+    half2,
+    grad_first,
+    back2,
+    pick_goal2,
     live_send,
     live_send2,
     sum_goal2,
@@ -283,28 +389,45 @@
     back_ref,
     slope,
     sum_rim,
+    grad,
 ):
     rows = cotangent.shape[0]
     rim = sum_rim.shape[0] // 2
-    near_first, far_first = rim_starts(grid_rows, rim)
-    sum_rim[:rim, :] = spread(live_send[...], near_first, rim)
-    sum_rim[rim:, :] = spread(live_send[...], far_first, rim)
+    grad[:FIRST, :] = grad_first[...]
+    for c in pieces_of(half2.shape[0], FIRST)[1:]:
+        double = half_silu(half2[c, :])[1]
+        grad[c, :] = (mm(pick_goal2[c, :], back2[...]) * double).astype(BF16)
     table = mm(spread(live_send2[...], 0, rows), grad[...]).astype(BF16)
     dest = mm(sum_goal2[...], grad[...]).astype(BF16)
     local = cotangent[...].astype(F32) + mm_t(table, w_source[...]) + mm_t(dest, w_dest[...])
     grad_local[...] = local
     back = normalise_back(centred(local * as_row(gain)), normed[...], inverse[:, :1])
     back_ref[...] = (0.5 * mm_t(back.astype(BF16), w_out[...])).astype(BF16)
-    for c in pieces_of(half.shape[0], 128):
-        slope[c, :] = half_silu(half[c, :])[1].astype(BF16)
+    near_first, far_first = rim_starts(grid_rows, rim)
+    sum_rim[:rim, :] = spread(live_send[...], near_first, rim)
+    sum_rim[rim:, :] = spread(live_send[...], far_first, rim)
+    slope[...] = half_silu(half[:FIRST, :])[1].astype(BF16)
 
 
 def encode_back_kernel(
-    grad_local, back_local, normed, inverse, slope, pick_goal, sum_rim, gain, w_source2, w_out, *refs
+    early,
+    grad_local,
+    back_local,
+    normed,
+    inverse,
+    half,
+    slope,
+    pick_goal,
+    sum_rim,
+    gain,
+    w_source2,
+    w_out,
+    *refs,
 ):
-    received, (grad, near, far, updated16) = refs[:-4], refs[-4:]
+    received, (back_ref, grad_first, near, far, updated16, grad) = refs[:-6], refs[-6:]
     coarse = updated16.shape[0]
     rim = near.shape[0]
+    number = jnp.max(early[:1, :])
     total = received[0][...].astype(F32)
     for r in received[1:]:
         total = total + r[...].astype(F32)
@@ -315,17 +438,48 @@
     )
     back = (0.5 * mm_t(back.astype(BF16), w_out[...])).astype(BF16)
     back = jnp.concatenate([back, back_local[coarse:, :]], axis=0)
-    for c in pieces_of(slope.shape[0], 256):
-        grad[c, :] = (mm(pick_goal[c, :], back) * slope[c, :].astype(F32)).astype(BF16)
-    near[...] = mm(sum_rim[:rim, :], grad[...]).astype(BF16)
-    far[...] = mm(sum_rim[rim:, :], grad[...]).astype(BF16)
+    back_ref[...] = back
+    first = mm(pick_goal[:FIRST, :], back) * slope[...].astype(F32)
+    grad_first[...] = first.astype(BF16)
+
+    @pl.when(number <= FIRST)
+    def _():
+        far[...] = mm(sum_rim[rim:, :FIRST], grad_first[...]).astype(BF16)
+        near[...] = mm(sum_rim[:rim, :FIRST], grad_first[...]).astype(BF16)
+
+    @pl.when(number > FIRST)
+    def _():
+        grad[:FIRST, :] = grad_first[...]
+        for c in pieces_of(half.shape[0], FIRST)[1:]:
+            grad[c, :] = edge_grad(c, pick_goal, back_ref[...], half)
+        far[...] = mm(sum_rim[rim:, :], grad[...]).astype(BF16)
+        near[...] = mm(sum_rim[:rim, :], grad[...]).astype(BF16)
+
+
+def edge_grad(c, pick_goal, back, half):
+    return (mm(pick_goal[c, :], back) * half_silu(half[c, :])[1]).astype(BF16)
 
 
 def own_back_kernel(
-    grad, live_send, live_goal, grad_local, updated16, w_source, w_dest, mesh_grad, own
+    grad_first,
+    back,
+    half,
+    pick_goal,
+    live_send,
+    live_goal,
+    grad_local,
+    updated16,
+    w_source,
+    w_dest,
+    mesh_grad,
+    own,
+    grad,
 ):
     coarse = updated16.shape[0]
     rows = grad_local.shape[0]
+    grad[:FIRST, :] = grad_first[...]
+    for c in pieces_of(half.shape[0], FIRST)[1:]:
+        grad[c, :] = edge_grad(c, pick_goal, back[...], half)
     dest = mm(spread(live_goal[...], 0, rows), grad[...]).astype(BF16)
     updated = jnp.concatenate([updated16[...], grad_local[coarse:, :]], axis=0)
     mesh_grad[...] = (updated + mm_t(dest, w_dest[...])).astype(BF16)
@@ -354,12 +508,13 @@
 MICROSECOND = 1 << 30
 
 
-def call(kernel, arrays, outs, cost, raw=0, scalars=0, scratch=(), out_space=None):
+def call(kernel, arrays, outs, cost, raw=0, scalars=0, scratch=(), out_specs=None, aliases=None):
     return pl.pallas_call(
         kernel,
         out_shape=[jax.ShapeDtypeStruct(s, d) for s, d in outs],
         in_specs=[HBM] * raw + [SMEM] * scalars + [VMEM] * (len(arrays) - raw - scalars),
-        out_specs=[out_space or VMEM] * len(outs),
+        out_specs=out_specs or [VMEM] * len(outs),
+        input_output_aliases=aliases or {},
         scratch_shapes=list(scratch),
         compiler_params=pltpu.CompilerParams(vmem_limit_bytes=24 << 20),
         cost_estimate=pl.CostEstimate(
@@ -411,7 +566,7 @@
     slots, slots2 = encoder_sender.shape[0], process_sender.shape[0]
 
     row_form, row_form2 = ((1, slots), I32), ((1, slots2), I32)
-    column_form2 = ((slots2, LANES), I32)
+    column_form2 = ((slots2, LANES), I16)
     remote = coarse * (groups - 1)
     near, far, grid = call(
         select_kernel,
@@ -423,7 +578,10 @@
     )
     near, far = swap_halo(near, far, patches)
     (
+        early,
         part,
+        hidden,
+        summed16,
         live_send,
         live_goal,
         live_send2,
@@ -445,18 +603,22 @@
             encoder_source,
             encoder_dest,
         ],
-        [((slots, hidden_size), F32), row_form, row_form, row_form2, row_form2]
+        [((2, LANES), I32), ((slots, hidden_size), F32), ((slots, hidden_size), BF16)]
+        + [((coarse, hidden_size), F32), row_form, row_form, row_form2, row_form2]
         + [column_form2, column_form2]
         + [((slots, 2 * rim), BF16), ((slots, mesh_rows), BF16)],
         2,
         scalars=1,
     )
-    hidden, half, updated16 = call(
+    half, hidden, updated16 = call(
         functools.partial(encode_halo_kernel, coarse),
         [
+            early,
             near,
             far,
             part,
+            hidden,
+            summed16,
             pick_rim,
             live_goal,
             mesh_latent,
@@ -464,11 +626,22 @@
             encoder_output,
             encoder_gain,
         ],
-        [((slots, hidden_size), BF16), ((slots, hidden_size), F32), ((coarse, width), BF16)],
+        [((slots, hidden_size), F32), ((slots, hidden_size), BF16), ((coarse, width), BF16)],
         2,
+        aliases={3: 0, 4: 1},
     )
     shifts = swap_coarse([updated16] * (groups - 1), groups)
-    normed, inverse, part2, pick_goal2, pick_coarse, sum_goal2, sum_coarse, centre2 = call(
+    (
+        normed,
+        inverse,
+        part2,
+        pick_goal2,
+        pick_coarse,
+        sum_goal2,
+        sum_coarse,
+        centre2,
+        summed2,
+    ) = call(
         process_local_kernel,
         [
             hidden,
@@ -494,32 +667,46 @@
             ((mesh_rows, slots2), BF16),
             ((remote, slots2), BF16),
             ((mesh_rows, width), F32),
+            ((mesh_rows, hidden_size), F32),
         ],
         2,
-    )
-    grad2, *pieces = call(
+        scratch=[pltpu.VMEM((slots2, hidden_size), BF16)],
+    )
+    half2, grad_first2, back2, *pieces = call(
         functools.partial(process_kernel, coarse),
         [
+            early,
             part2,
             pick_goal2,
             pick_coarse,
             sum_goal2,
             sum_coarse,
             centre2,
+            summed2,
             process_source,
             process_output,
             *shifts,
         ],
-        [((slots2, hidden_size), BF16)] + [((coarse, hidden_size), BF16)] * (groups - 1),
+        [((slots2, hidden_size), F32), ((FIRST, hidden_size), BF16)]
+        + [((mesh_rows, hidden_size), BF16)]
+        + [((coarse, hidden_size), BF16)] * (groups - 1),
         2,
-        scratch=[pltpu.VMEM((slots2, hidden_size), BF16), pltpu.VMEM((slots2, hidden_size), F32)],
+        scratch=[
+            pltpu.VMEM((slots2, hidden_size), BF16),
+            pltpu.VMEM((slots2, hidden_size), F32),
+            pltpu.VMEM((slots2, hidden_size), BF16),
+        ],
+        aliases={1: 0},
     )
     pieces = swap_coarse(pieces, groups)
     grad_local, back, slope, sum_rim = call(
         functools.partial(process_back_kernel, grid_rows),
         [
             half,
-            grad2,
+            half2,
+            grad_first2,
+            back2,
+            pick_goal2,
             live_send,
             live_send2,
             sum_goal2,
@@ -534,18 +721,21 @@
         [
             ((mesh_rows, width), F32),
             ((mesh_rows, hidden_size), BF16),
-            ((slots, hidden_size), BF16),
+            ((FIRST, hidden_size), BF16),
             ((2 * rim, slots), BF16),
         ],
         2,
-    )
-    grad, near, far, grad16 = call(
+        scratch=[pltpu.VMEM((slots2, hidden_size), BF16)],
+    )
+    back, grad_first, near, far, grad16 = call(
         encode_back_kernel,
         [
+            early,
             grad_local,
             back,
             normed,
             inverse,
+            half,
             slope,
             pick_goal,
             sum_rim,
@@ -554,17 +744,30 @@
             encoder_output,
             *pieces,
         ],
-        [((slots, hidden_size), BF16)]
+        [((mesh_rows, hidden_size), BF16), ((FIRST, hidden_size), BF16)]
         + [((rim, hidden_size), BF16)] * 2
         + [((coarse, width), F32)],
         2,
+        scratch=[pltpu.VMEM((slots, hidden_size), BF16)],
     )
     near, far = swap_halo(near, far, patches)
     mesh_grad, own = call(
         own_back_kernel,
-        [grad, live_send, live_goal, grad_local, grad16, encoder_source, encoder_dest],
+        [
+            grad_first,
+            back,
+            half,
+            pick_goal,
+            live_send,
+            live_goal,
+            grad_local,
+            grad16,
+            encoder_source,
+            encoder_dest,
+        ],
         [((mesh_rows, width), BF16), ((grid_rows, width), F32)],
         2,
+        scratch=[pltpu.VMEM((slots, hidden_size), BF16)],
     )
     (grid_grad,) = call(
         finish_kernel,
@@ -572,7 +775,7 @@
         [((grid_rows, width), BF16)],
         2,
         scratch=[pltpu.VMEM((grid_rows, width), BF16), pltpu.SemaphoreType.DMA((4,))],
-        out_space=HBM,
+        out_specs=[HBM],
     )
     return grid_grad, mesh_grad
 

time: 37.9 us -> 39.7 us (1.047)
  Pallas kernels: 14.2 us -> 15.7 us
  waiting for transfers between devices: 6.27 us -> 7.76 us
  starting transfers between devices: 14.9 us -> 13.7 us
    ppermute x2, waiting for transfers between devices: 2.65 us -> 4.2 us  [swap_halo(): far = lax.ppermute(far, 'patch', far_pairs)]
    pallas_call x9, Pallas kernels: 14.2 us -> 15.7 us  [call(): pl.pallas_call(kernel, out_shape=[jax.ShapeDtypeStruct(s, d) for s, d in...]
    ppermute x2, starting transfers between devices: 5.36 us -> 4.17 us  [swap_halo(): far = lax.ppermute(far, 'patch', far_pairs)]
  transfers between devices with their start and end apart: 10 -> 10, of which waited for: 4 -> 3; matrix products, arithmetic and copies ran while one was open for 0% -> 0% of each run, Pallas kernels for 18% -> 22%
where the time goes in v4:
time: 39.7 us; the launch traced here: 39.5 us
  Pallas kernels  15.7 us (40%)
  starting transfers between devices  13.7 us (35%)
  waiting for transfers between devices  7.76 us (20%)
  between operations  2.2 us (6%)
    pallas_call x9, Pallas kernels, call(): pl.pallas_call(kernel, out_shape=[jax.ShapeDtypeStruct(s, d) for s, d in...  15.7 us
    ppermute x6, starting transfers between devices, swap_coarse(): out.append(lax.ppermute(piece, 'group', [(i, i ^ k) for i in range(n)]))  8.9 us
    ppermute x2, waiting for transfers between devices, swap_halo(): far = lax.ppermute(far, 'patch', far_pairs)  4.2 us
    ppermute x2, starting transfers between devices, swap_halo(): far = lax.ppermute(far, 'patch', far_pairs)  4.17 us
    ppermute x6, waiting for transfers between devices, swap_coarse(): out.append(lax.ppermute(piece, 'group', [(i, i ^ k) for i in range(n)]))  3.56 us
  transfers between devices with their start and end apart: 10, of which 3 were waited for; matrix products, arithmetic and copies ran while one was open for 0% of the time, Pallas kernels for 22%

profile of v4, /device:TPU:0, one launch (start us, length us, event | category | flops | bytes accessed | tf_op | source)
XLA Modules:
  0.0 39.5 jit_solution(2870874139779544218)
XLA Ops:
  0.7 1.5 %shard_map.185 = (bf16[128,512]{1,0:T(8,128)(2,1)S(1)}, bf16[128,512]{1,0:T(8,128)(2,1)S(1)}, bf16[512,512]{1,0:T(8,128)(2,1)S(1)}) custom-call(s32[256]{0:T(256)} %halo.1, bf16[512,512]{1,0:T(8,128)(2,1)} %grid_hbm.1), custom_call_target="tpu_custom_call" | custom-call | flops 4294967296 | bytes 1048576 | tf_op jit(solution)/shard_map/pallas_call | solution.py:512
  2.2 0.6 %collective-permute-start = (bf16[128,512]{1,0:T(8,128)(2,1)S(1)}, bf16[128,512]{1,0:T(8,128)(2,1)S(1)}, u32[]{:S(2)}, u32[]{:S(2)}) collective-permute-start(bf16[128,512]{1,0:T(8,128)(2,1)S(1)} %get-tuple-element.48), channel_id=1, source_target_pairs={{0,4},{4,0},{8,12},{12,8},{16,20},{20,16},{24,28},{28,24},{1,5},{5... | collective-permute-start | bytes 393224 | tf_op jit(solution)/shard_map/ppermute | solution.py:529
  2.8 3.5 %collective-permute-start.1 = (bf16[128,512]{1,0:T(8,128)(2,1)S(1)}, bf16[128,512]{1,0:T(8,128)(2,1)S(1)}, u32[]{:S(2)}, u32[]{:S(2)}) collective-permute-start(bf16[128,512]{1,0:T(8,128)(2,1)S(1)} %get-tuple-element.49), channel_id=1, source_target_pairs={{0,28},{4,8},{8,4},{12,16},{16,12},{20,24},{24,20},{28,0},{1,29},{... | collective-permute-start | bytes 393224 | tf_op jit(solution)/shard_map/ppermute | solution.py:528
  7.6 0.1 pad_add_fusion.counts
  7.7 0.0 copy-start.2
  7.7 0.0 copy-start.13
  7.7 3.5 %shard_map.186 = (s32[2,128]{1,0:T(2,128)S(1)}, f32[768,512]{1,0:T(8,128)S(1)}, bf16[768,512]{1,0:T(8,128)(2,1)S(1)}, f32[16,512]{1,0:T(8,128)S(1)}, s32[1,768]{...) custom-call(s32[2]{0:T(128)S(1)} %pad_add_fusion.counts, ...), custom_call_target="tpu_custom_call" | custom-call | flops 2147483648 | bytes 1048576 | tf_op jit(solution)/shard_map/pallas_call | solution.py:512
  11.2 0.0 collective-permute-done.near
  11.2 0.0 collective-permute-done.1.far
  11.3 0.0 copy-start.1
  11.3 0.0 copy-start.3
  11.3 0.0 copy-start.7
  11.3 0.0 copy-start.12
  11.3 1.1 %shard_map.187 = (f32[768,512]{1,0:T(8,128)S(1)}, bf16[768,512]{1,0:T(8,128)(2,1)S(1)}, bf16[16,512]{1,0:T(8,128)(2,1)S(1)}) custom-call(s32[2,128]{1,0:T(2,128)S(1)} %get-tuple-element.47.early, bf16[128,512]{1,0:T(8,128)(2,1)S(1)} %collective-permute-done.near, ...), custom_call_target="tpu_custom_call", output_to_operand_aliasing={{0}: (3, {}), {1}: (4, {})} | custom-call | flops 2147483648 | bytes 1048576 | tf_op jit(solution)/shard_map/pallas_call | solution.py:512
  12.5 3.7 %collective-permute-start.4 = (bf16[16,512]{1,0:T(8,128)(2,1)S(1)}, bf16[16,512]{1,0:T(8,128)(2,1)S(1)}, u32[]{:S(2)}, u32[]{:S(2)}) collective-permute-start(bf16[16,512]{1,0:T(8,128)(2,1)S(1)} %get-tuple-element.68), channel_id=1, source_target_pairs={{0,3},{1,2},{2,1},{3,0},{4,7},{5,6},{6,5},{7,4},{8,11},{9,10},{10,... | collective-permute-start | bytes 49160 | tf_op jit(solution)/shard_map/ppermute | solution.py:536
  16.1 0.0 collective-permute-start.3
  16.1 0.8 %collective-permute-start.2 = (bf16[16,512]{1,0:T(8,128)(2,1)S(1)}, bf16[16,512]{1,0:T(8,128)(2,1)S(1)}, u32[]{:S(2)}, u32[]{:S(2)}) collective-permute-start(bf16[16,512]{1,0:T(8,128)(2,1)S(1)} %get-tuple-element.68), channel_id=1, source_target_pairs={{0,1},{1,0},{2,3},{3,2},{4,5},{5,4},{6,7},{7,6},{8,9},{9,8},{10,11... | collective-permute-start | bytes 49160 | tf_op jit(solution)/shard_map/ppermute | solution.py:536
  16.9 0.0 copy-start
  16.9 2.0 %shard_map.188 = (f32[256,512]{1,0:T(8,128)S(1)}, f32[256,128]{1,0:T(8,128)S(1)}, f32[768,512]{1,0:T(8,128)S(1)}, bf16[768,256]{1,0:T(8,128)(2,1)S(1)}, bf16[768...) custom-call(bf16[768,512]{1,0:T(8,128)(2,1)S(1)} %get-tuple-element., ...), custom_call_target="tpu_custom_call" | custom-call | flops 2147483648 | bytes 1048576 | tf_op jit(solution)/shard_map/pallas_call | solution.py:512
  18.9 1.8 %collective-permute-done.3.refs_1_ = bf16[16,512]{1,0:T(8,128)(2,1)S(1)} collective-permute-done((bf16[16,512]{1,0:T(8,128)(2,1)S(1)}, bf16[16,512]{1,0:T(8,128)(2,1)S(1)}, u32[]{:S(2)}, u32[]{:S(2)}) %collective-permute-start.3) | collective-permute-done | bytes 16416 | tf_op jit(solution)/shard_map/ppermute | solution.py:536
  20.8 1.8 %shard_map.189 = (f32[768,512]{1,0:T(8,128)S(1)}, bf16[256,512]{1,0:T(8,128)(2,1)S(1)}, bf16[256,512]{1,0:T(8,128)(2,1)S(1)}, bf16[16,512]{1,0:T(8,128)(2,1)S(1)...) custom-call(s32[2,128]{1,0:T(2,128)S(1)} %get-tuple-element.47.early, ...), custom_call_target="tpu_custom_call", output_to_operand_aliasing={{0}: (1, {})} | custom-call | flops 2147483648 | bytes 1048576 | tf_op jit(solution)/shard_map/pallas_call | solution.py:512
  22.6 0.1 collective-permute-start.5
  22.7 2.4 %collective-permute-start.6 = (bf16[16,512]{1,0:T(8,128)(2,1)S(1)}, bf16[16,512]{1,0:T(8,128)(2,1)S(1)}, u32[]{:S(2)}, u32[]{:S(2)}) collective-permute-start(bf16[16,512]{1,0:T(8,128)(2,1)S(1)} %get-tuple-element.81), channel_id=1, source_target_pairs={{0,2},{1,3},{2,0},{3,1},{4,6},{5,7},{6,4},{7,5},{8,10},{9,11},{10,... | collective-permute-start | bytes 49160 | tf_op jit(solution)/shard_map/ppermute | solution.py:536
  25.1 2.0 %collective-permute-start.7 = (bf16[16,512]{1,0:T(8,128)(2,1)S(1)}, bf16[16,512]{1,0:T(8,128)(2,1)S(1)}, u32[]{:S(2)}, u32[]{:S(2)}) collective-permute-start(bf16[16,512]{1,0:T(8,128)(2,1)S(1)} %get-tuple-element.82), channel_id=1, source_target_pairs={{0,3},{1,2},{2,1},{3,0},{4,7},{5,6},{6,5},{7,4},{8,11},{9,10},{10,... | collective-permute-start | bytes 49160 | tf_op jit(solution)/shard_map/ppermute | solution.py:536
  27.1 1.8 %shard_map.190 = (f32[256,512]{1,0:T(8,128)S(1)}, bf16[256,512]{1,0:T(8,128)(2,1)S(1)}, bf16[256,512]{1,0:T(8,128)(2,1)S(1)}, bf16[256,768]{1,0:T(8,128)(2,1)S(1)}) custom-call(f32[768,512]{1,0:T(8,128)S(1)} %get-tuple-element.55.half, f32[768,512]{1,0:T(8,128)S(1)} %get-tuple-element.69.half2, bf16[256,512]{1,0:T(8,128)(2,1)S(1)} %get-tuple-element.70.grad_first, ...), custom_call_target="tpu_custom_call" | custom-call | flops 2147483648 | bytes 1048576 | tf_op jit(solution)/shard_map/pallas_call | solution.py:512
  28.9 1.7 %collective-permute-done.7.refs_2_ = bf16[16,512]{1,0:T(8,128)(2,1)S(1)} collective-permute-done((bf16[16,512]{1,0:T(8,128)(2,1)S(1)}, bf16[16,512]{1,0:T(8,128)(2,1)S(1)}, u32[]{:S(2)}, u32[]{:S(2)}) %collective-permute-start.7) | collective-permute-done | bytes 16416 | tf_op jit(solution)/shard_map/ppermute | solution.py:536
  30.6 1.1 %shard_map.191 = (bf16[256,512]{1,0:T(8,128)(2,1)S(1)}, bf16[256,512]{1,0:T(8,128)(2,1)S(1)}, bf16[128,512]{1,0:T(8,128)(2,1)S(1)}, bf16[128,512]{1,0:T(8,128)(2,1)S(1)}, f32[16,512]{1,0:T(8,128)S(1)}) custom-call(s32[2,128]{1,0:T(2,128)S(1)} %get-tuple-element.47.early, f32[256,512]{1,0:T(8,128)S(1)} %get-tuple-element.75.grad_local, ...), custom_call_target="tpu_custom_call" | custom-call | flops 2147483648 | bytes 1048576 | tf_op jit(solution)/shard_map/pallas_call | solution.py:512
  31.7 0.1 collective-permute-start.8
  31.7 0.6 %collective-permute-start.9 = (bf16[128,512]{1,0:T(8,128)(2,1)S(1)}, bf16[128,512]{1,0:T(8,128)(2,1)S(1)}, u32[]{:S(2)}, u32[]{:S(2)}) collective-permute-start(bf16[128,512]{1,0:T(8,128)(2,1)S(1)} %get-tuple-element.88), channel_id=1, source_target_pairs={{0,28},{4,8},{8,4},{12,16},{16,12},{20,24},{24,20},{28,0},{1,29},{... | collective-permute-start | bytes 393224 | tf_op jit(solution)/shard_map/ppermute | solution.py:528
  32.4 1.6 %shard_map.192 = (bf16[256,512]{1,0:T(8,128)(2,1)}, f32[512,512]{1,0:T(8,128)S(1)}) custom-call(bf16[256,512]{1,0:T(8,128)(2,1)S(1)} %get-tuple-element.83.grad_first, bf16[256,512]{1,0:T(8,128)(2,1)S(1)} %get-tuple-element.84.back, f32[768,512]{1,0:T(8,128)S(1)} %get-tuple-element.55.half, bf16[768,256]{1,0:T(8,128)(2,1)S(1)} %get-tuple-element.78.pick_goal, ...), custom_call_target="tpu_custom_call" | custom-call | flops 2147483648 | bytes 1048576 | tf_op jit(solution)/shard_map/pallas_call | solution.py:512
  34.0 4.2 %collective-permute-done.9.far = bf16[128,512]{1,0:T(8,128)(2,1)S(1)} collective-permute-done((bf16[128,512]{1,0:T(8,128)(2,1)S(1)}, bf16[128,512]{1,0:T(8,128)(2,1)S(1)}, u32[]{:S(2)}, u32[]{:S(2)}) %collective-permute-start.9) | collective-permute-done | bytes 131104 | tf_op jit(solution)/shard_map/ppermute | solution.py:528
  38.2 1.3 %shard_map.193 = bf16[512,512]{1,0:T(8,128)(2,1)} custom-call(s32[256]{0:T(256)S(1)} %copy-done.14, f32[512,512]{1,0:T(8,128)S(1)} %get-tuple-element.86.own, bf16[128,512]{1,0:T(8,128)(2,1)S(1)} %collective-permute-done.8.near, bf16[128,512]{1,0:T(8,128)(2,1)S(1)} %collective-permute-done.9.far, bf16[512,512]{1,0:T(8,128)(2,1)S(1)} %copy-done.5), custom_call_target="tpu_custom_call" | custom-call | flops 2147483648 | bytes 1048576 | tf_op jit(solution)/shard_map/pallas_call | solution.py:512
  (28 shorter events, 0.1 us)
Async XLA Ops:
  0.6 7.0 %copy-start.5 = (bf16[512,512]{1,0:T(8,128)(2,1)S(1)}, bf16[512,512]{1,0:T(8,128)(2,1)}, u32[]{:S(2)}) copy-start(bf16[512,512]{1,0:T(8,128)(2,1)} %w_source.13) | copy-start | bytes 1572868
  0.6 7.0 %copy-start.6 = (bf16[256,512]{1,0:T(8,128)(2,1)S(1)}, bf16[256,512]{1,0:T(8,128)(2,1)}, u32[]{:S(2)}) copy-start(bf16[256,512]{1,0:T(8,128)(2,1)} %mesh.5) | copy-start | bytes 786436
  0.7 7.0 %copy-start.4 = (bf16[512,512]{1,0:T(8,128)(2,1)S(1)}, bf16[512,512]{1,0:T(8,128)(2,1)}, u32[]{:S(2)}) copy-start(bf16[512,512]{1,0:T(8,128)(2,1)} %w_dest.7) | copy-start | bytes 1572868
  0.7 7.0 %copy-start.11 = (s32[768]{0:T(1024)S(1)}, s32[768]{0:T(1024)}, u32[]{:S(2)}) copy-start(s32[768]{0:T(1024)} %target2.1) | copy-start | bytes 9220
  0.7 7.0 %copy-start.10 = (s32[768]{0:T(1024)S(1)}, s32[768]{0:T(1024)}, u32[]{:S(2)}) copy-start(s32[768]{0:T(1024)} %sender2.1) | copy-start | bytes 9220
  0.7 7.0 %copy-start.9 = (s32[768]{0:T(1024)S(1)}, s32[768]{0:T(1024)}, u32[]{:S(2)}) copy-start(s32[768]{0:T(1024)} %target.1) | copy-start | bytes 9220
  0.7 7.0 %copy-start.8 = (s32[768]{0:T(1024)S(1)}, s32[768]{0:T(1024)}, u32[]{:S(2)}) copy-start(s32[768]{0:T(1024)} %sender.1) | copy-start | bytes 9220
  2.2 9.0 %collective-permute-start = (bf16[128,512]{1,0:T(8,128)(2,1)S(1)}, bf16[128,512]{1,0:T(8,128)(2,1)S(1)}, u32[]{:S(2)}, u32[]{:S(2)}) collective-permute-start(bf16[128,512]{1,0:T(8,128)(2,1)S(1)} %get-tuple-element.48), channel_id=1, source_target_pairs={{0,4},{4,0},{8,12},{12,8},{16,20},{20,16},{24,28},{28,24},{1,5},{5... | collective-permute-start | bytes 393224 | tf_op jit(solution)/shard_map/ppermute | solution.py:529
  2.8 8.5 %collective-permute-start.1 = (bf16[128,512]{1,0:T(8,128)(2,1)S(1)}, bf16[128,512]{1,0:T(8,128)(2,1)S(1)}, u32[]{:S(2)}, u32[]{:S(2)}) collective-permute-start(bf16[128,512]{1,0:T(8,128)(2,1)S(1)} %get-tuple-element.49), channel_id=1, source_target_pairs={{0,28},{4,8},{8,4},{12,16},{16,12},{20,24},{24,20},{28,0},{1,29},{... | collective-permute-start | bytes 393224 | tf_op jit(solution)/shard_map/ppermute | solution.py:528
  7.7 3.5 %copy-start.2 = (bf16[512,512]{1,0:T(8,128)(2,1)S(1)}, bf16[512,512]{1,0:T(8,128)(2,1)}, u32[]{:S(2)}) copy-start(bf16[512,512]{1,0:T(8,128)(2,1)} %w_out.9) | copy-start | bytes 1572868
  7.7 3.5 %copy-start.13 = (f32[512]{0:T(512)S(1)}, f32[512]{0:T(512)}, u32[]{:S(2)}) copy-start(f32[512]{0:T(512)} %gain.7) | copy-start | bytes 6148
  11.3 5.6 %copy-start.1 = (bf16[512,512]{1,0:T(8,128)(2,1)S(1)}, bf16[512,512]{1,0:T(8,128)(2,1)}, u32[]{:S(2)}) copy-start(bf16[512,512]{1,0:T(8,128)(2,1)} %w_dest.6) | copy-start | bytes 1572868
  11.3 5.6 %copy-start.3 = (bf16[512,512]{1,0:T(8,128)(2,1)S(1)}, bf16[512,512]{1,0:T(8,128)(2,1)}, u32[]{:S(2)}) copy-start(bf16[512,512]{1,0:T(8,128)(2,1)} %w_source2.1) | copy-start | bytes 1572868
  11.3 5.6 %copy-start.7 = (bf16[256,512]{1,0:T(8,128)(2,1)S(1)}, bf16[256,512]{1,0:T(8,128)(2,1)}, u32[]{:S(2)}) copy-start(bf16[256,512]{1,0:T(8,128)(2,1)} %cotangent.3) | copy-start | bytes 786436
  11.3 5.6 %copy-start.12 = (f32[512]{0:T(512)S(1)}, f32[512]{0:T(512)}, u32[]{:S(2)}) copy-start(f32[512]{0:T(512)} %gain2.1) | copy-start | bytes 6148
  12.5 6.5 %collective-permute-start.4 = (bf16[16,512]{1,0:T(8,128)(2,1)S(1)}, bf16[16,512]{1,0:T(8,128)(2,1)S(1)}, u32[]{:S(2)}, u32[]{:S(2)}) collective-permute-start(bf16[16,512]{1,0:T(8,128)(2,1)S(1)} %get-tuple-element.68), channel_id=1, source_target_pairs={{0,3},{1,2},{2,1},{3,0},{4,7},{5,6},{6,5},{7,4},{8,11},{9,10},{10,... | collective-permute-start | bytes 49160 | tf_op jit(solution)/shard_map/ppermute | solution.py:536
  16.1 4.6 %collective-permute-start.3 = (bf16[16,512]{1,0:T(8,128)(2,1)S(1)}, bf16[16,512]{1,0:T(8,128)(2,1)S(1)}, u32[]{:S(2)}, u32[]{:S(2)}) collective-permute-start(bf16[16,512]{1,0:T(8,128)(2,1)S(1)} %get-tuple-element.68), channel_id=1, source_target_pairs={{0,2},{1,3},{2,0},{3,1},{4,6},{5,7},{6,4},{7,5},{8,10},{9,11},{10,... | collective-permute-start | bytes 49160 | tf_op jit(solution)/shard_map/ppermute | solution.py:536
  16.1 4.6 %collective-permute-start.2 = (bf16[16,512]{1,0:T(8,128)(2,1)S(1)}, bf16[16,512]{1,0:T(8,128)(2,1)S(1)}, u32[]{:S(2)}, u32[]{:S(2)}) collective-permute-start(bf16[16,512]{1,0:T(8,128)(2,1)S(1)} %get-tuple-element.68), channel_id=1, source_target_pairs={{0,1},{1,0},{2,3},{3,2},{4,5},{5,4},{6,7},{7,6},{8,9},{9,8},{10,11... | collective-permute-start | bytes 49160 | tf_op jit(solution)/shard_map/ppermute | solution.py:536
  16.9 3.8 %copy-start = (bf16[512,512]{1,0:T(8,128)(2,1)S(1)}, bf16[512,512]{1,0:T(8,128)(2,1)}, u32[]{:S(2)}) copy-start(bf16[512,512]{1,0:T(8,128)(2,1)} %w_out.7) | copy-start | bytes 1572868
  22.6 6.2 %collective-permute-start.5 = (bf16[16,512]{1,0:T(8,128)(2,1)S(1)}, bf16[16,512]{1,0:T(8,128)(2,1)S(1)}, u32[]{:S(2)}, u32[]{:S(2)}) collective-permute-start(bf16[16,512]{1,0:T(8,128)(2,1)S(1)} %get-tuple-element.80), channel_id=1, source_target_pairs={{0,1},{1,0},{2,3},{3,2},{4,5},{5,4},{6,7},{7,6},{8,9},{9,8},{10,11... | collective-permute-start | bytes 49160 | tf_op jit(solution)/shard_map/ppermute | solution.py:536
  22.7 6.2 %collective-permute-start.6 = (bf16[16,512]{1,0:T(8,128)(2,1)S(1)}, bf16[16,512]{1,0:T(8,128)(2,1)S(1)}, u32[]{:S(2)}, u32[]{:S(2)}) collective-permute-start(bf16[16,512]{1,0:T(8,128)(2,1)S(1)} %get-tuple-element.81), channel_id=1, source_target_pairs={{0,2},{1,3},{2,0},{3,1},{4,6},{5,7},{6,4},{7,5},{8,10},{9,11},{10,... | collective-permute-start | bytes 49160 | tf_op jit(solution)/shard_map/ppermute | solution.py:536
  25.1 5.5 %collective-permute-start.7 = (bf16[16,512]{1,0:T(8,128)(2,1)S(1)}, bf16[16,512]{1,0:T(8,128)(2,1)S(1)}, u32[]{:S(2)}, u32[]{:S(2)}) collective-permute-start(bf16[16,512]{1,0:T(8,128)(2,1)S(1)} %get-tuple-element.82), channel_id=1, source_target_pairs={{0,3},{1,2},{2,1},{3,0},{4,7},{5,6},{6,5},{7,4},{8,11},{9,10},{10,... | collective-permute-start | bytes 49160 | tf_op jit(solution)/shard_map/ppermute | solution.py:536
  31.7 2.3 %collective-permute-start.8 = (bf16[128,512]{1,0:T(8,128)(2,1)S(1)}, bf16[128,512]{1,0:T(8,128)(2,1)S(1)}, u32[]{:S(2)}, u32[]{:S(2)}) collective-permute-start(bf16[128,512]{1,0:T(8,128)(2,1)S(1)} %get-tuple-element.87), channel_id=1, source_target_pairs={{0,4},{4,0},{8,12},{12,8},{16,20},{20,16},{24,28},{28,24},{1,5},{5... | collective-permute-start | bytes 393224 | tf_op jit(solution)/shard_map/ppermute | solution.py:529
  31.7 6.4 %collective-permute-start.9 = (bf16[128,512]{1,0:T(8,128)(2,1)S(1)}, bf16[128,512]{1,0:T(8,128)(2,1)S(1)}, u32[]{:S(2)}, u32[]{:S(2)}) collective-permute-start(bf16[128,512]{1,0:T(8,128)(2,1)S(1)} %get-tuple-element.88), channel_id=1, source_target_pairs={{0,28},{4,8},{8,4},{12,16},{16,12},{20,24},{24,20},{28,0},{1,29},{... | collective-permute-start | bytes 393224 | tf_op jit(solution)/shard_map/ppermute | solution.py:528
  32.4 5.8 %copy-start.14 = (s32[256]{0:T(256)S(1)}, s32[256]{0:T(256)}, u32[]{:S(2)}) copy-start(s32[256]{0:T(256)} %halo.1) | copy-start | bytes 3076

commit v5 on v4

--- a/solution.py
+++ b/solution.py
@@ -36,12 +36,16 @@
     return (n + k - 1) // k * k
 
 
-def to_columns(row):
-    n = row.shape[1]
+def to_columns(*rows):
+    packed = rows[0] if len(rows) == 1 else rows[0] + rows[1] * 4096
     parts = []
-    for i in range(0, n, LANES):
-        parts.append(jnp.broadcast_to(row[:, i : i + LANES], (LANES, LANES)).T.astype(I16))
-    return jnp.concatenate(parts, axis=0)
+    for i in range(0, packed.shape[1], LANES):
+        parts.append(jnp.broadcast_to(packed[:, i : i + LANES], (LANES, LANES)).T)
+    columns = jnp.concatenate(parts, axis=0)
+    if len(rows) == 1:
+        return columns.astype(I16)
+    low = jnp.bitwise_and(columns, 4095).astype(I16)
+    return low, lax.shift_right_logical(columns, 12).astype(I16)
 
 
 def one_hot(equal):
@@ -85,12 +89,26 @@
     return jnp.where(even, second, first), jnp.where(even, first, second)
 
 
-def coarse_slots(sender, mesh_rows, coarse, me):
+def plans(n):
+    masks = [tuple(i ^ k for i in range(n)) for k in range(n - 1, 0, -1)]
+    if n == 4:
+        return [(1, 3, 0, 2), (3, 2, 1, 0), (2, 0, 3, 1)], masks
+    return masks, masks
+
+
+def look_up(table, index):
+    value = jnp.int32(table[0])
+    for i, entry in enumerate(table[1:], 1):
+        value = jnp.where(index == i, jnp.int32(entry), value)
+    return value
+
+
+def coarse_slots(sender, mesh_rows, coarse, owners):
     offset = sender - mesh_rows
     owner = offset // coarse
-    row = offset - owner * coarse
-    mask = owner ^ me
-    moved = jnp.where(mask == 0, row, mesh_rows + (mask - 1) * coarse + row)
+    moved = offset - owner * coarse
+    for k, other in enumerate(owners):
+        moved = moved + jnp.where(owner == other, mesh_rows + k * coarse, 0)
     return jnp.where(offset < 0, sender, moved)
 
 
@@ -144,12 +162,14 @@
     slot = lax.broadcasted_iota(I32, first.shape, 1).astype(F32)
     place = jnp.where(first > 0.0, counted - 1.0, total + slot - counted)
     order = spread(place.astype(I32), 0, slots)
-    digits = [d for row in rows for d in (row // LANES, row % LANES)]
+    digits = []
+    for row in rows:
+        digits += [lax.shift_right_logical(row, 7), jnp.bitwise_and(row, 127)]
     digits = [d.astype(F32) for d in digits]
     spare = ceil_to(len(digits), 8) - len(digits)
     digits = jnp.concatenate(digits + [jnp.zeros((spare, slots), F32)] * bool(spare), axis=0)
     moved = mm_t(digits.astype(BF16), order).astype(I32)
-    moved = [moved[2 * i : 2 * i + 1, :] * LANES + moved[2 * i + 1 : 2 * i + 2, :] for i in range(len(rows))]
+    moved = [moved[2 * i : 2 * i + 1, :] * 128 + moved[2 * i + 1 : 2 * i + 2, :] for i in range(len(rows))]
     return total, moved
 
 
@@ -159,6 +179,7 @@
 
 
 def encode_local_kernel(
+    groups,
     coarse,
     counts,
     sender,
@@ -182,33 +203,39 @@
     pick_rim,
     pick_goal,
 ):
+    count, count2 = counts[0], counts[1]
     rows, grid_rows = mesh.shape[0], grid.shape[0]
     rim = pick_rim.shape[1] // 2
     source = (0.5 * mm(grid[...], w_source[...])).astype(BF16)
     dest = (0.5 * mm(mesh[...], w_dest[...])).astype(BF16)
-    send = as_row(sender)
-    total, (send, goal) = arrange(flagged(send >= grid_rows, counts[0]), [send, as_row(target)])
+    me = lax.axis_index("group")
+    gather, reduce = plans(groups)
+    sources = [look_up([p.index(i) for i in range(groups)], me) for p in gather]
+    goals = [look_up(p, me) for p in reduce]
+    send, send2 = as_row(sender), as_row(sender2)
+    back2 = coarse_slots(send2, rows, coarse, goals)
+    send2 = coarse_slots(send2, rows, coarse, sources)
+    total, (send, goal) = arrange(flagged(send >= grid_rows, count), [send, as_row(target)])
+    moved = [send2, as_row(target2), back2]
+    total2, (send2, goal2, back2) = arrange(flagged(send2 >= rows, count2), moved)
     early[:1, :] = jnp.broadcast_to(total, (1, LANES)).astype(I32)
-    send_col = to_columns(send)
+    early[1:, :] = jnp.broadcast_to(total2, (1, LANES)).astype(I32)
+    send_col, goal_col = to_columns(send, goal)
+    send_col2[...], goal_col2[...] = to_columns(send2, goal2)
     near_first, far_first = rim_starts(grid_rows, rim)
     pick_rim[:, :rim] = pick(send_col, near_first, rim)
     pick_rim[:, rim:] = pick(send_col, far_first, rim)
-    pick_goal[...] = pick(to_columns(goal), 0, rows)
-    live_send[...] = only_live(send, counts[0])
-    live_goal[...] = only_live(goal, counts[0])
+    pick_goal[...] = pick(goal_col, 0, rows)
+    live_send[...] = only_live(send, count)
+    live_goal[...] = only_live(goal, count)
+    live_send2[...] = only_live(back2, count2)
+    live_goal2[...] = only_live(goal2, count2)
     for c in pieces_of(part.shape[0], FIRST):
         u = mm(pick(send_col[c, :], 0, grid_rows), source) + mm(pick_goal[c, :], dest)
         part[c, :] = u
         if c.start:
             hidden[c, :] = (u + u * jnp.tanh(u)).astype(BF16)
     summed16[...] = mm(spread(live_goal[:, FIRST:], 0, coarse), hidden[FIRST:, :])
-    send2 = coarse_slots(as_row(sender2), rows, coarse, lax.axis_index("group"))
-    total, (send2, goal2) = arrange(flagged(send2 >= rows, counts[1]), [send2, as_row(target2)])
-    early[1:, :] = jnp.broadcast_to(total, (1, LANES)).astype(I32)
-    send_col2[...] = to_columns(send2)
-    goal_col2[...] = to_columns(goal2)
-    live_send2[...] = only_live(send2, counts[1])
-    live_goal2[...] = only_live(goal2, counts[1])
 
 
 def pieces_of(n, size):
@@ -338,8 +365,11 @@
         slope[c, :] = double
 
     def turn(summed):
-        normed, inverse = normalise(mm(summed.astype(BF16), w_out[...]))
-        back = normalise_back(centre2[...], normed, inverse).astype(BF16)
+        center = centred(mm(summed.astype(BF16), w_out[...]))
+        inverse = lax.rsqrt(jnp.mean(center * center, axis=-1, keepdims=True) + EPSILON)
+        share = jnp.mean(center * centre2[...], axis=-1, keepdims=True)
+        share = share * inverse * inverse
+        back = (inverse * (centre2[...] - center * share)).astype(BF16)
         back = (0.5 * mm_t(back, w_out[...])).astype(BF16)
         back_ref[...] = back
         grad_first[...] = (mm(pick_goal2[:FIRST, :], back) * slope[:FIRST, :]).astype(BF16)
@@ -471,8 +501,11 @@
     updated16,
     w_source,
     w_dest,
+    halo,
+    near,
     mesh_grad,
     own,
+    sum_far,
     grad,
 ):
     coarse = updated16.shape[0]
@@ -484,18 +517,17 @@
     updated = jnp.concatenate([updated16[...], grad_local[coarse:, :]], axis=0)
     mesh_grad[...] = (updated + mm_t(dest, w_dest[...])).astype(BF16)
     source = mm(spread(live_send[...], 0, own.shape[0]), grad[...]).astype(BF16)
-    own[...] = mm_t(source, w_source[...])
-
-
-def finish_kernel(halo, own, near, far, w_source, out_hbm, out, sems):
     rows_near, rows_far = halves(as_row(halo), even_patch())
-    peers = jnp.concatenate([near[...], far[...]], axis=0)
-    projected = mm_t(peers, w_source[...]).astype(BF16)
-    where = jnp.concatenate([rows_near, rows_far], axis=1)
+    sum_far[...] = spread(rows_far, 0, own.shape[0])
+    back_near = mm_t(near[...], w_source[...]).astype(BF16)
+    own[...] = mm_t(source, w_source[...]) + mm(spread(rows_near, 0, own.shape[0]), back_near)
+
+
+def finish_kernel(own, sum_far, far, w_source, out_hbm, out, sems):
+    projected = mm_t(far[...], w_source[...]).astype(BF16)
     copies = []
-    for i, c in enumerate(pieces_of(own.shape[0], own.shape[0] // 4)):
-        chosen = spread(where, c.start, c.stop - c.start)
-        out[c, :] = (own[c, :] + mm(chosen, projected)).astype(BF16)
+    for i, c in enumerate(pieces_of(own.shape[0], own.shape[0] // 8)):
+        out[c, :] = (own[c, :] + mm(sum_far[c, :], projected)).astype(BF16)
         copies.append(pltpu.make_async_copy(out.at[c], out_hbm.at[c], sems.at[i]))
         copies[-1].start()
     for copy in copies:
@@ -530,10 +562,10 @@
     return near, far
 
 
-def swap_coarse(pieces, n):
+def exchange(pieces, plan):
     out = []
-    for k, piece in enumerate(pieces, 1):
-        out.append(lax.ppermute(piece, "group", [(i, i ^ k) for i in range(n)]))
+    for piece, goals in zip(pieces, plan):
+        out.append(lax.ppermute(piece, "group", list(enumerate(goals))))
     return out
 
 
@@ -591,7 +623,7 @@
         pick_rim,
         pick_goal,
     ) = call(
-        functools.partial(encode_local_kernel, coarse),
+        functools.partial(encode_local_kernel, groups, coarse),
         [
             jnp.concatenate([encoder_count, process_count]),
             encoder_sender,
@@ -630,7 +662,7 @@
         2,
         aliases={3: 0, 4: 1},
     )
-    shifts = swap_coarse([updated16] * (groups - 1), groups)
+    shifts = exchange([updated16] * (groups - 1), plans(groups)[0])
     (
         normed,
         inverse,
@@ -698,7 +730,7 @@
         ],
         aliases={1: 0},
     )
-    pieces = swap_coarse(pieces, groups)
+    pieces = exchange(pieces, plans(groups)[1])
     grad_local, back, slope, sum_rim = call(
         functools.partial(process_back_kernel, grid_rows),
         [
@@ -751,7 +783,7 @@
         scratch=[pltpu.VMEM((slots, hidden_size), BF16)],
     )
     near, far = swap_halo(near, far, patches)
-    mesh_grad, own = call(
+    mesh_grad, own, sum_far = call(
         own_back_kernel,
         [
             grad_first,
@@ -764,17 +796,19 @@
             grad16,
             encoder_source,
             encoder_dest,
-        ],
-        [((mesh_rows, width), BF16), ((grid_rows, width), F32)],
+            halo_rows,
+            near,
+        ],
+        [((mesh_rows, width), BF16), ((grid_rows, width), F32), ((grid_rows, rim), BF16)],
         2,
         scratch=[pltpu.VMEM((slots, hidden_size), BF16)],
     )
     (grid_grad,) = call(
         finish_kernel,
-        [halo_rows, own, near, far, encoder_source],
+        [own, sum_far, far, encoder_source],
         [((grid_rows, width), BF16)],
         2,
-        scratch=[pltpu.VMEM((grid_rows, width), BF16), pltpu.SemaphoreType.DMA((4,))],
+        scratch=[pltpu.VMEM((grid_rows, width), BF16), pltpu.SemaphoreType.DMA((8,))],
         out_specs=[HBM],
     )
     return grid_grad, mesh_grad

time: 39.7 us -> 38.9 us (0.980)
  waiting for transfers between devices: 7.76 us -> 6.24 us
  starting transfers between devices: 13.7 us -> 14.8 us
    ppermute x6, waiting for transfers between devices: 3.56 us -> 2.75 us  [exchange(): out.append(lax.ppermute(piece, 'group', list(enumerate(goals))))]
    ppermute x2, starting transfers between devices: 4.17 us -> 4.94 us  [swap_halo(): far = lax.ppermute(far, 'patch', far_pairs)]
    ppermute x2, waiting for transfers between devices: 4.2 us -> 3.49 us  [swap_halo(): far = lax.ppermute(far, 'patch', far_pairs)]
  transfers between devices with their start and end apart: 10 -> 10, of which waited for: 3 -> 4; matrix products, arithmetic and copies ran while one was open for 0% -> 0% of each run, Pallas kernels for 22% -> 22%
where the time goes in v5:
time: 38.9 us; the launch traced here: 38.8 us
  Pallas kernels  15.4 us (40%)
  starting transfers between devices  14.8 us (38%)
  waiting for transfers between devices  6.24 us (16%)
  between operations  2.17 us (6%)
    pallas_call x9, Pallas kernels, call(): pl.pallas_call(kernel, out_shape=[jax.ShapeDtypeStruct(s, d) for s, d in...  15.4 us
    ppermute x6, starting transfers between devices, exchange(): out.append(lax.ppermute(piece, 'group', list(enumerate(goals))))  9.24 us
    ppermute x2, starting transfers between devices, swap_halo(): far = lax.ppermute(far, 'patch', far_pairs)  4.94 us
    ppermute x2, waiting for transfers between devices, swap_halo(): far = lax.ppermute(far, 'patch', far_pairs)  3.49 us
    ppermute x6, waiting for transfers between devices, exchange(): out.append(lax.ppermute(piece, 'group', list(enumerate(goals))))  2.75 us
  transfers between devices with their start and end apart: 10, of which 4 were waited for; matrix products, arithmetic and copies ran while one was open for 0% of the time, Pallas kernels for 22%

profile of v5, /device:TPU:0, one launch (start us, length us, event | category | flops | bytes accessed | tf_op | source)
XLA Modules:
  0.0 38.8 jit_solution(9611860843222924472)
XLA Ops:
  0.7 1.5 %shard_map.185 = (bf16[128,512]{1,0:T(8,128)(2,1)S(1)}, bf16[128,512]{1,0:T(8,128)(2,1)S(1)}, bf16[512,512]{1,0:T(8,128)(2,1)S(1)}) custom-call(s32[256]{0:T(256)} %halo.1, bf16[512,512]{1,0:T(8,128)(2,1)} %grid_hbm.1), custom_call_target="tpu_custom_call" | custom-call | flops 4294967296 | bytes 1048576 | tf_op jit(solution)/shard_map/pallas_call | solution.py:544
  2.2 0.6 %collective-permute-start = (bf16[128,512]{1,0:T(8,128)(2,1)S(1)}, bf16[128,512]{1,0:T(8,128)(2,1)S(1)}, u32[]{:S(2)}, u32[]{:S(2)}) collective-permute-start(bf16[128,512]{1,0:T(8,128)(2,1)S(1)} %get-tuple-element.49), channel_id=1, source_target_pairs={{0,4},{4,0},{8,12},{12,8},{16,20},{20,16},{24,28},{28,24},{1,5},{5... | collective-permute-start | bytes 393224 | tf_op jit(solution)/shard_map/ppermute | solution.py:561
  2.8 3.5 %collective-permute-start.1 = (bf16[128,512]{1,0:T(8,128)(2,1)S(1)}, bf16[128,512]{1,0:T(8,128)(2,1)S(1)}, u32[]{:S(2)}, u32[]{:S(2)}) collective-permute-start(bf16[128,512]{1,0:T(8,128)(2,1)S(1)} %get-tuple-element.50), channel_id=1, source_target_pairs={{0,28},{4,8},{8,4},{12,16},{16,12},{20,24},{24,20},{28,0},{1,29},{... | collective-permute-start | bytes 393224 | tf_op jit(solution)/shard_map/ppermute | solution.py:560
  7.6 0.1 pad_add_fusion.counts
  7.7 0.0 copy-start.2
  7.7 0.0 copy-start.13
  7.7 3.0 %shard_map.186 = (s32[2,128]{1,0:T(2,128)S(1)}, f32[768,512]{1,0:T(8,128)S(1)}, bf16[768,512]{1,0:T(8,128)(2,1)S(1)}, f32[16,512]{1,0:T(8,128)S(1)}, s32[1,768]{...) custom-call(s32[2]{0:T(128)S(1)} %pad_add_fusion.counts, ...), custom_call_target="tpu_custom_call" | custom-call | flops 2147483648 | bytes 1048576 | tf_op jit(solution)/shard_map/pallas_call | solution.py:544
  10.8 0.0 collective-permute-done.1.far
  10.8 0.0 copy-start.1
  10.8 0.0 copy-start.3
  10.8 0.0 copy-start.7
  10.8 0.0 copy-start.12
  10.8 1.1 %shard_map.187 = (f32[768,512]{1,0:T(8,128)S(1)}, bf16[768,512]{1,0:T(8,128)(2,1)S(1)}, bf16[16,512]{1,0:T(8,128)(2,1)S(1)}) custom-call(s32[2,128]{1,0:T(2,128)S(1)} %get-tuple-element.48.early, bf16[128,512]{1,0:T(8,128)(2,1)S(1)} %collective-permute-done.near, ...), custom_call_target="tpu_custom_call", output_to_operand_aliasing={{0}: (3, {}), {1}: (4, {})} | custom-call | flops 2147483648 | bytes 1048576 | tf_op jit(solution)/shard_map/pallas_call | solution.py:544
  12.0 2.6 %collective-permute-start.4 = (bf16[16,512]{1,0:T(8,128)(2,1)S(1)}, bf16[16,512]{1,0:T(8,128)(2,1)S(1)}, u32[]{:S(2)}, u32[]{:S(2)}) collective-permute-start(bf16[16,512]{1,0:T(8,128)(2,1)S(1)} %get-tuple-element.69), channel_id=1, source_target_pairs={{0,2},{1,0},{2,3},{3,1},{4,6},{5,4},{6,7},{7,5},{8,10},{9,8},{10,1... | collective-permute-start | bytes 49160 | tf_op jit(solution)/shard_map/ppermute | solution.py:568
  14.6 1.4 %collective-permute-start.3 = (bf16[16,512]{1,0:T(8,128)(2,1)S(1)}, bf16[16,512]{1,0:T(8,128)(2,1)S(1)}, u32[]{:S(2)}, u32[]{:S(2)}) collective-permute-start(bf16[16,512]{1,0:T(8,128)(2,1)S(1)} %get-tuple-element.69), channel_id=1, source_target_pairs={{0,3},{1,2},{2,1},{3,0},{4,7},{5,6},{6,5},{7,4},{8,11},{9,10},{10,... | collective-permute-start | bytes 49160 | tf_op jit(solution)/shard_map/ppermute | solution.py:568
  16.0 0.8 %collective-permute-start.2 = (bf16[16,512]{1,0:T(8,128)(2,1)S(1)}, bf16[16,512]{1,0:T(8,128)(2,1)S(1)}, u32[]{:S(2)}, u32[]{:S(2)}) collective-permute-start(bf16[16,512]{1,0:T(8,128)(2,1)S(1)} %get-tuple-element.69), channel_id=1, source_target_pairs={{0,1},{1,3},{2,0},{3,2},{4,5},{5,7},{6,4},{7,6},{8,9},{9,11},{10,8... | collective-permute-start | bytes 49160 | tf_op jit(solution)/shard_map/ppermute | solution.py:568
  16.8 0.0 copy-start
  16.8 2.0 %shard_map.188 = (f32[256,512]{1,0:T(8,128)S(1)}, f32[256,128]{1,0:T(8,128)S(1)}, f32[768,512]{1,0:T(8,128)S(1)}, bf16[768,256]{1,0:T(8,128)(2,1)S(1)}, bf16[768...) custom-call(bf16[768,512]{1,0:T(8,128)(2,1)S(1)} %get-tuple-element., ...), custom_call_target="tpu_custom_call" | custom-call | flops 2147483648 | bytes 1048576 | tf_op jit(solution)/shard_map/pallas_call | solution.py:544
  18.8 1.4 %collective-permute-done.3.refs_1_ = bf16[16,512]{1,0:T(8,128)(2,1)S(1)} collective-permute-done((bf16[16,512]{1,0:T(8,128)(2,1)S(1)}, bf16[16,512]{1,0:T(8,128)(2,1)S(1)}, u32[]{:S(2)}, u32[]{:S(2)}) %collective-permute-start.3) | collective-permute-done | bytes 16416 | tf_op jit(solution)/shard_map/ppermute | solution.py:568
  20.2 0.5 %collective-permute-done.2.refs_0_ = bf16[16,512]{1,0:T(8,128)(2,1)S(1)} collective-permute-done((bf16[16,512]{1,0:T(8,128)(2,1)S(1)}, bf16[16,512]{1,0:T(8,128)(2,1)S(1)}, u32[]{:S(2)}, u32[]{:S(2)}) %collective-permute-start.2) | collective-permute-done | bytes 16416 | tf_op jit(solution)/shard_map/ppermute | solution.py:568
  20.6 1.8 %shard_map.189 = (f32[768,512]{1,0:T(8,128)S(1)}, bf16[256,512]{1,0:T(8,128)(2,1)S(1)}, bf16[256,512]{1,0:T(8,128)(2,1)S(1)}, bf16[16,512]{1,0:T(8,128)(2,1)S(1)...) custom-call(s32[2,128]{1,0:T(2,128)S(1)} %get-tuple-element.48.early, ...), custom_call_target="tpu_custom_call", output_to_operand_aliasing={{0}: (1, {})} | custom-call | flops 2147483648 | bytes 1048576 | tf_op jit(solution)/shard_map/pallas_call | solution.py:544
  22.4 2.5 %collective-permute-start.5 = (bf16[16,512]{1,0:T(8,128)(2,1)S(1)}, bf16[16,512]{1,0:T(8,128)(2,1)S(1)}, u32[]{:S(2)}, u32[]{:S(2)}) collective-permute-start(bf16[16,512]{1,0:T(8,128)(2,1)S(1)} %get-tuple-element.81), channel_id=1, source_target_pairs={{0,3},{1,2},{2,1},{3,0},{4,7},{5,6},{6,5},{7,4},{8,11},{9,10},{10,... | collective-permute-start | bytes 49160 | tf_op jit(solution)/shard_map/ppermute | solution.py:568
  24.9 0.0 collective-permute-start.6
  24.9 1.9 %collective-permute-start.7 = (bf16[16,512]{1,0:T(8,128)(2,1)S(1)}, bf16[16,512]{1,0:T(8,128)(2,1)S(1)}, u32[]{:S(2)}, u32[]{:S(2)}) collective-permute-start(bf16[16,512]{1,0:T(8,128)(2,1)S(1)} %get-tuple-element.83), channel_id=1, source_target_pairs={{0,1},{1,0},{2,3},{3,2},{4,5},{5,4},{6,7},{7,6},{8,9},{9,8},{10,11... | collective-permute-start | bytes 49160 | tf_op jit(solution)/shard_map/ppermute | solution.py:568
  26.8 1.8 %shard_map.190 = (f32[256,512]{1,0:T(8,128)S(1)}, bf16[256,512]{1,0:T(8,128)(2,1)S(1)}, bf16[256,512]{1,0:T(8,128)(2,1)S(1)}, bf16[256,768]{1,0:T(8,128)(2,1)S(1)}) custom-call(f32[768,512]{1,0:T(8,128)S(1)} %get-tuple-element.56.half, f32[768,512]{1,0:T(8,128)S(1)} %get-tuple-element.70.half2, bf16[256,512]{1,0:T(8,128)(2,1)S(1)} %get-tuple-element.71.grad_first, ...), custom_call_target="tpu_custom_call" | custom-call | flops 2147483648 | bytes 1048576 | tf_op jit(solution)/shard_map/pallas_call | solution.py:544
  28.6 0.9 %collective-permute-done.6.refs_1_ = bf16[16,512]{1,0:T(8,128)(2,1)S(1)} collective-permute-done((bf16[16,512]{1,0:T(8,128)(2,1)S(1)}, bf16[16,512]{1,0:T(8,128)(2,1)S(1)}, u32[]{:S(2)}, u32[]{:S(2)}) %collective-permute-start.6) | collective-permute-done | bytes 16416 | tf_op jit(solution)/shard_map/ppermute | solution.py:568
  29.6 1.1 %shard_map.191 = (bf16[256,512]{1,0:T(8,128)(2,1)S(1)}, bf16[256,512]{1,0:T(8,128)(2,1)S(1)}, bf16[128,512]{1,0:T(8,128)(2,1)S(1)}, bf16[128,512]{1,0:T(8,128)(2,1)S(1)}, f32[16,512]{1,0:T(8,128)S(1)}) custom-call(s32[2,128]{1,0:T(2,128)S(1)} %get-tuple-element.48.early, f32[256,512]{1,0:T(8,128)S(1)} %get-tuple-element.76.grad_local, ...), custom_call_target="tpu_custom_call" | custom-call | flops 2147483648 | bytes 1048576 | tf_op jit(solution)/shard_map/pallas_call | solution.py:544
  30.6 0.1 collective-permute-start.8
  30.7 1.4 %collective-permute-start.9 = (bf16[128,512]{1,0:T(8,128)(2,1)S(1)}, bf16[128,512]{1,0:T(8,128)(2,1)S(1)}, u32[]{:S(2)}, u32[]{:S(2)}) collective-permute-start(bf16[128,512]{1,0:T(8,128)(2,1)S(1)} %get-tuple-element.90), channel_id=1, source_target_pairs={{0,28},{4,8},{8,4},{12,16},{16,12},{20,24},{24,20},{28,0},{1,29},{... | collective-permute-start | bytes 393224 | tf_op jit(solution)/shard_map/ppermute | solution.py:560
  32.1 1.8 %shard_map.192 = (bf16[256,512]{1,0:T(8,128)(2,1)}, f32[512,512]{1,0:T(8,128)S(1)}, bf16[512,128]{1,0:T(8,128)(2,1)S(1)}) custom-call(bf16[256,512]{1,0:T(8,128)(2,1)S(1)} %get-tuple-element.84.grad_first, bf16[256,512]{1,0:T(8,128)(2,1)S(1)} %get-tuple-element.85.back, f32[768,512]{1,0:T(8,128)S(1)} %get-tuple-element.56.half, ...), custom_call_target="tpu_custom_call" | custom-call | flops 2147483648 | bytes 1048576 | tf_op jit(solution)/shard_map/pallas_call | solution.py:544
  34.0 3.5 %collective-permute-done.9.far = bf16[128,512]{1,0:T(8,128)(2,1)S(1)} collective-permute-done((bf16[128,512]{1,0:T(8,128)(2,1)S(1)}, bf16[128,512]{1,0:T(8,128)(2,1)S(1)}, u32[]{:S(2)}, u32[]{:S(2)}) %collective-permute-start.9) | collective-permute-done | bytes 131104 | tf_op jit(solution)/shard_map/ppermute | solution.py:560
  37.5 1.3 %shard_map.193 = bf16[512,512]{1,0:T(8,128)(2,1)} custom-call(f32[512,512]{1,0:T(8,128)S(1)} %get-tuple-element.88.own, bf16[512,128]{1,0:T(8,128)(2,1)S(1)} %get-tuple-element.89.sum_far, bf16[128,512]{1,0:T(8,128)(2,1)S(1)} %collective-permute-done.9.far, bf16[512,512]{1,0:T(8,128)(2,1)S(1)} %copy-done.5), custom_call_target="tpu_custom_call" | custom-call | flops 2147483648 | bytes 1048576 | tf_op jit(solution)/shard_map/pallas_call | solution.py:544
  (28 shorter events, 0.1 us)
Async XLA Ops:
  0.6 7.0 %copy-start.5 = (bf16[512,512]{1,0:T(8,128)(2,1)S(1)}, bf16[512,512]{1,0:T(8,128)(2,1)}, u32[]{:S(2)}) copy-start(bf16[512,512]{1,0:T(8,128)(2,1)} %w_source.13) | copy-start | bytes 1572868
  0.6 7.0 %copy-start.6 = (bf16[256,512]{1,0:T(8,128)(2,1)S(1)}, bf16[256,512]{1,0:T(8,128)(2,1)}, u32[]{:S(2)}) copy-start(bf16[256,512]{1,0:T(8,128)(2,1)} %mesh.5) | copy-start | bytes 786436
  0.7 7.0 %copy-start.4 = (bf16[512,512]{1,0:T(8,128)(2,1)S(1)}, bf16[512,512]{1,0:T(8,128)(2,1)}, u32[]{:S(2)}) copy-start(bf16[512,512]{1,0:T(8,128)(2,1)} %w_dest.7) | copy-start | bytes 1572868
  0.7 7.0 %copy-start.11 = (s32[768]{0:T(1024)S(1)}, s32[768]{0:T(1024)}, u32[]{:S(2)}) copy-start(s32[768]{0:T(1024)} %target2.1) | copy-start | bytes 9220
  0.7 7.0 %copy-start.10 = (s32[768]{0:T(1024)S(1)}, s32[768]{0:T(1024)}, u32[]{:S(2)}) copy-start(s32[768]{0:T(1024)} %sender2.1) | copy-start | bytes 9220
  0.7 7.0 %copy-start.9 = (s32[768]{0:T(1024)S(1)}, s32[768]{0:T(1024)}, u32[]{:S(2)}) copy-start(s32[768]{0:T(1024)} %target.1) | copy-start | bytes 9220
  0.7 7.0 %copy-start.8 = (s32[768]{0:T(1024)S(1)}, s32[768]{0:T(1024)}, u32[]{:S(2)}) copy-start(s32[768]{0:T(1024)} %sender.1) | copy-start | bytes 9220
  2.2 8.6 %collective-permute-start = (bf16[128,512]{1,0:T(8,128)(2,1)S(1)}, bf16[128,512]{1,0:T(8,128)(2,1)S(1)}, u32[]{:S(2)}, u32[]{:S(2)}) collective-permute-start(bf16[128,512]{1,0:T(8,128)(2,1)S(1)} %get-tuple-element.49), channel_id=1, source_target_pairs={{0,4},{4,0},{8,12},{12,8},{16,20},{20,16},{24,28},{28,24},{1,5},{5... | collective-permute-start | bytes 393224 | tf_op jit(solution)/shard_map/ppermute | solution.py:561
  2.8 8.0 %collective-permute-start.1 = (bf16[128,512]{1,0:T(8,128)(2,1)S(1)}, bf16[128,512]{1,0:T(8,128)(2,1)S(1)}, u32[]{:S(2)}, u32[]{:S(2)}) collective-permute-start(bf16[128,512]{1,0:T(8,128)(2,1)S(1)} %get-tuple-element.50), channel_id=1, source_target_pairs={{0,28},{4,8},{8,4},{12,16},{16,12},{20,24},{24,20},{28,0},{1,29},{... | collective-permute-start | bytes 393224 | tf_op jit(solution)/shard_map/ppermute | solution.py:560
  7.7 3.1 %copy-start.2 = (bf16[512,512]{1,0:T(8,128)(2,1)S(1)}, bf16[512,512]{1,0:T(8,128)(2,1)}, u32[]{:S(2)}) copy-start(bf16[512,512]{1,0:T(8,128)(2,1)} %w_out.9) | copy-start | bytes 1572868
  7.7 3.1 %copy-start.13 = (f32[512]{0:T(512)S(1)}, f32[512]{0:T(512)}, u32[]{:S(2)}) copy-start(f32[512]{0:T(512)} %gain.7) | copy-start | bytes 6148
  10.8 6.0 %copy-start.1 = (bf16[512,512]{1,0:T(8,128)(2,1)S(1)}, bf16[512,512]{1,0:T(8,128)(2,1)}, u32[]{:S(2)}) copy-start(bf16[512,512]{1,0:T(8,128)(2,1)} %w_dest.6) | copy-start | bytes 1572868
  10.8 6.0 %copy-start.3 = (bf16[512,512]{1,0:T(8,128)(2,1)S(1)}, bf16[512,512]{1,0:T(8,128)(2,1)}, u32[]{:S(2)}) copy-start(bf16[512,512]{1,0:T(8,128)(2,1)} %w_source2.1) | copy-start | bytes 1572868
  10.8 6.0 %copy-start.7 = (bf16[256,512]{1,0:T(8,128)(2,1)S(1)}, bf16[256,512]{1,0:T(8,128)(2,1)}, u32[]{:S(2)}) copy-start(bf16[256,512]{1,0:T(8,128)(2,1)} %cotangent.3) | copy-start | bytes 786436
  10.8 5.9 %copy-start.12 = (f32[512]{0:T(512)S(1)}, f32[512]{0:T(512)}, u32[]{:S(2)}) copy-start(f32[512]{0:T(512)} %gain2.1) | copy-start | bytes 6148
  12.0 6.8 %collective-permute-start.4 = (bf16[16,512]{1,0:T(8,128)(2,1)S(1)}, bf16[16,512]{1,0:T(8,128)(2,1)S(1)}, u32[]{:S(2)}, u32[]{:S(2)}) collective-permute-start(bf16[16,512]{1,0:T(8,128)(2,1)S(1)} %get-tuple-element.69), channel_id=1, source_target_pairs={{0,2},{1,0},{2,3},{3,1},{4,6},{5,4},{6,7},{7,5},{8,10},{9,8},{10,1... | collective-permute-start | bytes 49160 | tf_op jit(solution)/shard_map/ppermute | solution.py:568
  14.6 5.5 %collective-permute-start.3 = (bf16[16,512]{1,0:T(8,128)(2,1)S(1)}, bf16[16,512]{1,0:T(8,128)(2,1)S(1)}, u32[]{:S(2)}, u32[]{:S(2)}) collective-permute-start(bf16[16,512]{1,0:T(8,128)(2,1)S(1)} %get-tuple-element.69), channel_id=1, source_target_pairs={{0,3},{1,2},{2,1},{3,0},{4,7},{5,6},{6,5},{7,4},{8,11},{9,10},{10,... | collective-permute-start | bytes 49160 | tf_op jit(solution)/shard_map/ppermute | solution.py:568
  16.0 4.6 %collective-permute-start.2 = (bf16[16,512]{1,0:T(8,128)(2,1)S(1)}, bf16[16,512]{1,0:T(8,128)(2,1)S(1)}, u32[]{:S(2)}, u32[]{:S(2)}) collective-permute-start(bf16[16,512]{1,0:T(8,128)(2,1)S(1)} %get-tuple-element.69), channel_id=1, source_target_pairs={{0,1},{1,3},{2,0},{3,2},{4,5},{5,7},{6,4},{7,6},{8,9},{9,11},{10,8... | collective-permute-start | bytes 49160 | tf_op jit(solution)/shard_map/ppermute | solution.py:568
  16.8 3.8 %copy-start = (bf16[512,512]{1,0:T(8,128)(2,1)S(1)}, bf16[512,512]{1,0:T(8,128)(2,1)}, u32[]{:S(2)}) copy-start(bf16[512,512]{1,0:T(8,128)(2,1)} %w_out.7) | copy-start | bytes 1572868
  22.4 6.2 %collective-permute-start.5 = (bf16[16,512]{1,0:T(8,128)(2,1)S(1)}, bf16[16,512]{1,0:T(8,128)(2,1)S(1)}, u32[]{:S(2)}, u32[]{:S(2)}) collective-permute-start(bf16[16,512]{1,0:T(8,128)(2,1)S(1)} %get-tuple-element.81), channel_id=1, source_target_pairs={{0,3},{1,2},{2,1},{3,0},{4,7},{5,6},{6,5},{7,4},{8,11},{9,10},{10,... | collective-permute-start | bytes 49160 | tf_op jit(solution)/shard_map/ppermute | solution.py:568
  24.9 4.6 %collective-permute-start.6 = (bf16[16,512]{1,0:T(8,128)(2,1)S(1)}, bf16[16,512]{1,0:T(8,128)(2,1)S(1)}, u32[]{:S(2)}, u32[]{:S(2)}) collective-permute-start(bf16[16,512]{1,0:T(8,128)(2,1)S(1)} %get-tuple-element.82), channel_id=1, source_target_pairs={{0,2},{1,3},{2,0},{3,1},{4,6},{5,7},{6,4},{7,5},{8,10},{9,11},{10,... | collective-permute-start | bytes 49160 | tf_op jit(solution)/shard_map/ppermute | solution.py:568
  24.9 4.6 %collective-permute-start.7 = (bf16[16,512]{1,0:T(8,128)(2,1)S(1)}, bf16[16,512]{1,0:T(8,128)(2,1)S(1)}, u32[]{:S(2)}, u32[]{:S(2)}) collective-permute-start(bf16[16,512]{1,0:T(8,128)(2,1)S(1)} %get-tuple-element.83), channel_id=1, source_target_pairs={{0,1},{1,0},{2,3},{3,2},{4,5},{5,4},{6,7},{7,6},{8,9},{9,8},{10,11... | collective-permute-start | bytes 49160 | tf_op jit(solution)/shard_map/ppermute | solution.py:568
  29.6 2.6 %copy-start.14 = (s32[256]{0:T(256)S(1)}, s32[256]{0:T(256)}, u32[]{:S(2)}) copy-start(s32[256]{0:T(256)} %halo.1) | copy-start | bytes 3076
  30.6 1.5 %collective-permute-start.8 = (bf16[128,512]{1,0:T(8,128)(2,1)S(1)}, bf16[128,512]{1,0:T(8,128)(2,1)S(1)}, u32[]{:S(2)}, u32[]{:S(2)}) collective-permute-start(bf16[128,512]{1,0:T(8,128)(2,1)S(1)} %get-tuple-element.87), channel_id=1, source_target_pairs={{0,4},{4,0},{8,12},{12,8},{16,20},{20,16},{24,28},{28,24},{1,5},{5... | collective-permute-start | bytes 393224 | tf_op jit(solution)/shard_map/ppermute | solution.py:561
  30.7 6.7 %collective-permute-start.9 = (bf16[128,512]{1,0:T(8,128)(2,1)S(1)}, bf16[128,512]{1,0:T(8,128)(2,1)S(1)}, u32[]{:S(2)}, u32[]{:S(2)}) collective-permute-start(bf16[128,512]{1,0:T(8,128)(2,1)S(1)} %get-tuple-element.90), channel_id=1, source_target_pairs={{0,28},{4,8},{8,4},{12,16},{16,12},{20,24},{24,20},{28,0},{1,29},{... | collective-permute-start | bytes 393224 | tf_op jit(solution)/shard_map/ppermute | solution.py:560

commit v6 on v5

--- a/solution.py
+++ b/solution.py
@@ -273,15 +273,19 @@
         normed, _ = normalise(mm(summed.astype(BF16), w_out[...]))
         updated16[...] = (mesh[:coarse, :].astype(F32) + normed * as_row(gain)).astype(BF16)
 
-    edges(slice(0, FIRST))
+    def first_edges():
+        for c in pieces_of(FIRST, 128):
+            edges(c)
 
     @pl.when(number <= FIRST)
     def _():
+        first_edges()
         goal = spread(live_goal[:, :FIRST], 0, coarse)
         finish(summed16[...] + mm(goal, hidden[:FIRST, :]))
 
     @pl.when(number > FIRST)
     def _():
+        first_edges()
         for c in pieces_of(part.shape[0], FIRST)[1:]:
             edges(c)
         finish(mm(spread(live_goal[...], 0, coarse), hidden[...]))
@@ -359,10 +363,11 @@
 
     def edges(c):
         u = part[c, :] + mm(pick_coarse[c, :], source)
-        half[c, :] = u
+        if c.start >= FIRST:
+            half[c, :] = u
         value, double = half_silu(u)
         hidden[c, :] = value.astype(BF16)
-        slope[c, :] = double
+        slope[c, :] = double.astype(BF16)
 
     def turn(summed):
         center = centred(mm(summed.astype(BF16), w_out[...]))
@@ -372,29 +377,33 @@
         back = (inverse * (centre2[...] - center * share)).astype(BF16)
         back = (0.5 * mm_t(back, w_out[...])).astype(BF16)
         back_ref[...] = back
-        grad_first[...] = (mm(pick_goal2[:FIRST, :], back) * slope[:FIRST, :]).astype(BF16)
+        grad_first[...] = (mm(pick_goal2[:FIRST, :], back) * slope[:FIRST, :].astype(F32)).astype(BF16)
         return back
 
     def send(sums):
         for i, out in enumerate(returned):
             out[...] = sums[i * coarse : (i + 1) * coarse].astype(BF16)
 
-    edges(slice(0, FIRST))
+    def first_edges():
+        for c in pieces_of(FIRST, 128):
+            edges(c)
 
     @pl.when(number <= FIRST)
     def _():
+        first_edges()
         turn(summed2[...] + mm(sum_goal2[:, :FIRST], hidden[:FIRST, :]))
         send(mm(sum_coarse[:, :FIRST], grad_first[...]))
 
     @pl.when(number > FIRST)
     def _():
+        first_edges()
         later = pieces_of(part.shape[0], FIRST)[1:]
         for c in later:
             edges(c)
         back = turn(mm(sum_goal2[...], hidden[...]))
         grad[:FIRST, :] = grad_first[...]
         for c in later:
-            grad[c, :] = (mm(pick_goal2[c, :], back) * slope[c, :]).astype(BF16)
+            grad[c, :] = (mm(pick_goal2[c, :], back) * slope[c, :].astype(F32)).astype(BF16)
         send(mm(sum_coarse[...], grad[...]))
 
 
@@ -463,22 +472,26 @@
         total = total + r[...].astype(F32)
     updated = grad_local[:coarse, :] + mm_t(total.astype(BF16), w_source2[...])
     updated16[...] = updated
-    back = normalise_back(
-        centred(updated * as_row(gain)), normed[:coarse, :], inverse[:coarse, :1]
-    )
-    back = (0.5 * mm_t(back.astype(BF16), w_out[...])).astype(BF16)
-    back = jnp.concatenate([back, back_local[coarse:, :]], axis=0)
-    back_ref[...] = back
-    first = mm(pick_goal[:FIRST, :], back) * slope[...].astype(F32)
-    grad_first[...] = first.astype(BF16)
+
+    def turn():
+        back = normalise_back(
+            centred(updated * as_row(gain)), normed[:coarse, :], inverse[:coarse, :1]
+        )
+        back = (0.5 * mm_t(back.astype(BF16), w_out[...])).astype(BF16)
+        back = jnp.concatenate([back, back_local[coarse:, :]], axis=0)
+        back_ref[...] = back
+        first = mm(pick_goal[:FIRST, :], back) * slope[...].astype(F32)
+        grad_first[...] = first.astype(BF16)
 
     @pl.when(number <= FIRST)
     def _():
+        turn()
         far[...] = mm(sum_rim[rim:, :FIRST], grad_first[...]).astype(BF16)
         near[...] = mm(sum_rim[:rim, :FIRST], grad_first[...]).astype(BF16)
 
     @pl.when(number > FIRST)
     def _():
+        turn()
         grad[:FIRST, :] = grad_first[...]
         for c in pieces_of(half.shape[0], FIRST)[1:]:
             grad[c, :] = edge_grad(c, pick_goal, back_ref[...], half)
@@ -725,7 +738,7 @@
         2,
         scratch=[
             pltpu.VMEM((slots2, hidden_size), BF16),
-            pltpu.VMEM((slots2, hidden_size), F32),
+            pltpu.VMEM((slots2, hidden_size), BF16),
             pltpu.VMEM((slots2, hidden_size), BF16),
         ],
         aliases={1: 0},

time: 38.9 us -> 38.7 us (level)
  no operation moved by 1% of the time
where the time goes in v6:
time: 38.7 us; the launch traced here: 38.5 us
  Pallas kernels  15.2 us (39%)
  starting transfers between devices  14.7 us (38%)
  waiting for transfers between devices  6.28 us (16%)
  between operations  2.17 us (6%)
    pallas_call x9, Pallas kernels, call(): pl.pallas_call(kernel, out_shape=[jax.ShapeDtypeStruct(s, d) for s, d in...  15.2 us
    ppermute x6, starting transfers between devices, exchange(): out.append(lax.ppermute(piece, 'group', list(enumerate(goals))))  9.24 us
    ppermute x2, starting transfers between devices, swap_halo(): far = lax.ppermute(far, 'patch', far_pairs)  4.86 us
    ppermute x2, waiting for transfers between devices, swap_halo(): far = lax.ppermute(far, 'patch', far_pairs)  3.52 us
    ppermute x6, waiting for transfers between devices, exchange(): out.append(lax.ppermute(piece, 'group', list(enumerate(goals))))  2.75 us
  transfers between devices with their start and end apart: 10, of which 4 were waited for; matrix products, arithmetic and copies ran while one was open for 0% of the time, Pallas kernels for 22%

profile of v6, /device:TPU:0, one launch (start us, length us, event | category | flops | bytes accessed | tf_op | source)
XLA Modules:
  0.0 38.5 jit_solution(11259290974491074380)
XLA Ops:
  0.7 1.5 %shard_map.185 = (bf16[128,512]{1,0:T(8,128)(2,1)S(1)}, bf16[128,512]{1,0:T(8,128)(2,1)S(1)}, bf16[512,512]{1,0:T(8,128)(2,1)S(1)}) custom-call(s32[256]{0:T(256)} %halo.1, bf16[512,512]{1,0:T(8,128)(2,1)} %grid_hbm.1), custom_call_target="tpu_custom_call" | custom-call | flops 4294967296 | bytes 1048576 | tf_op jit(solution)/shard_map/pallas_call | solution.py:557
  2.2 0.6 %collective-permute-start = (bf16[128,512]{1,0:T(8,128)(2,1)S(1)}, bf16[128,512]{1,0:T(8,128)(2,1)S(1)}, u32[]{:S(2)}, u32[]{:S(2)}) collective-permute-start(bf16[128,512]{1,0:T(8,128)(2,1)S(1)} %get-tuple-element.49), channel_id=1, source_target_pairs={{0,4},{4,0},{8,12},{12,8},{16,20},{20,16},{24,28},{28,24},{1,5},{5... | collective-permute-start | bytes 393224 | tf_op jit(solution)/shard_map/ppermute | solution.py:574
  2.8 3.5 %collective-permute-start.1 = (bf16[128,512]{1,0:T(8,128)(2,1)S(1)}, bf16[128,512]{1,0:T(8,128)(2,1)S(1)}, u32[]{:S(2)}, u32[]{:S(2)}) collective-permute-start(bf16[128,512]{1,0:T(8,128)(2,1)S(1)} %get-tuple-element.50), channel_id=1, source_target_pairs={{0,28},{4,8},{8,4},{12,16},{16,12},{20,24},{24,20},{28,0},{1,29},{... | collective-permute-start | bytes 393224 | tf_op jit(solution)/shard_map/ppermute | solution.py:573
  7.6 0.1 pad_add_fusion.counts
  7.7 0.0 copy-start.2
  7.7 0.0 copy-start.13
  7.7 3.0 %shard_map.186 = (s32[2,128]{1,0:T(2,128)S(1)}, f32[768,512]{1,0:T(8,128)S(1)}, bf16[768,512]{1,0:T(8,128)(2,1)S(1)}, f32[16,512]{1,0:T(8,128)S(1)}, s32[1,768]{...) custom-call(s32[2]{0:T(128)S(1)} %pad_add_fusion.counts, ...), custom_call_target="tpu_custom_call" | custom-call | flops 2147483648 | bytes 1048576 | tf_op jit(solution)/shard_map/pallas_call | solution.py:557
  10.8 0.0 collective-permute-done.1.far
  10.8 0.0 copy-start.1
  10.8 0.0 copy-start.3
  10.8 0.0 copy-start.7
  10.8 0.0 copy-start.12
  10.8 1.1 %shard_map.187 = (f32[768,512]{1,0:T(8,128)S(1)}, bf16[768,512]{1,0:T(8,128)(2,1)S(1)}, bf16[16,512]{1,0:T(8,128)(2,1)S(1)}) custom-call(s32[2,128]{1,0:T(2,128)S(1)} %get-tuple-element.48.early, bf16[128,512]{1,0:T(8,128)(2,1)S(1)} %collective-permute-done.near, ...), custom_call_target="tpu_custom_call", output_to_operand_aliasing={{0}: (3, {}), {1}: (4, {})} | custom-call | flops 2147483648 | bytes 1048576 | tf_op jit(solution)/shard_map/pallas_call | solution.py:557
  12.0 2.6 %collective-permute-start.4 = (bf16[16,512]{1,0:T(8,128)(2,1)S(1)}, bf16[16,512]{1,0:T(8,128)(2,1)S(1)}, u32[]{:S(2)}, u32[]{:S(2)}) collective-permute-start(bf16[16,512]{1,0:T(8,128)(2,1)S(1)} %get-tuple-element.69), channel_id=1, source_target_pairs={{0,2},{1,0},{2,3},{3,1},{4,6},{5,4},{6,7},{7,5},{8,10},{9,8},{10,1... | collective-permute-start | bytes 49160 | tf_op jit(solution)/shard_map/ppermute | solution.py:581
  14.6 1.4 %collective-permute-start.3 = (bf16[16,512]{1,0:T(8,128)(2,1)S(1)}, bf16[16,512]{1,0:T(8,128)(2,1)S(1)}, u32[]{:S(2)}, u32[]{:S(2)}) collective-permute-start(bf16[16,512]{1,0:T(8,128)(2,1)S(1)} %get-tuple-element.69), channel_id=1, source_target_pairs={{0,3},{1,2},{2,1},{3,0},{4,7},{5,6},{6,5},{7,4},{8,11},{9,10},{10,... | collective-permute-start | bytes 49160 | tf_op jit(solution)/shard_map/ppermute | solution.py:581
  15.9 0.8 %collective-permute-start.2 = (bf16[16,512]{1,0:T(8,128)(2,1)S(1)}, bf16[16,512]{1,0:T(8,128)(2,1)S(1)}, u32[]{:S(2)}, u32[]{:S(2)}) collective-permute-start(bf16[16,512]{1,0:T(8,128)(2,1)S(1)} %get-tuple-element.69), channel_id=1, source_target_pairs={{0,1},{1,3},{2,0},{3,2},{4,5},{5,7},{6,4},{7,6},{8,9},{9,11},{10,8... | collective-permute-start | bytes 49160 | tf_op jit(solution)/shard_map/ppermute | solution.py:581
  16.7 0.0 copy-start
  16.8 2.0 %shard_map.188 = (f32[256,512]{1,0:T(8,128)S(1)}, f32[256,128]{1,0:T(8,128)S(1)}, f32[768,512]{1,0:T(8,128)S(1)}, bf16[768,256]{1,0:T(8,128)(2,1)S(1)}, bf16[768...) custom-call(bf16[768,512]{1,0:T(8,128)(2,1)S(1)} %get-tuple-element., ...), custom_call_target="tpu_custom_call" | custom-call | flops 2147483648 | bytes 1048576 | tf_op jit(solution)/shard_map/pallas_call | solution.py:557
  18.8 1.4 %collective-permute-done.3.refs_1_ = bf16[16,512]{1,0:T(8,128)(2,1)S(1)} collective-permute-done((bf16[16,512]{1,0:T(8,128)(2,1)S(1)}, bf16[16,512]{1,0:T(8,128)(2,1)S(1)}, u32[]{:S(2)}, u32[]{:S(2)}) %collective-permute-start.3) | collective-permute-done | bytes 16416 | tf_op jit(solution)/shard_map/ppermute | solution.py:581
  20.1 0.5 %collective-permute-done.2.refs_0_ = bf16[16,512]{1,0:T(8,128)(2,1)S(1)} collective-permute-done((bf16[16,512]{1,0:T(8,128)(2,1)S(1)}, bf16[16,512]{1,0:T(8,128)(2,1)S(1)}, u32[]{:S(2)}, u32[]{:S(2)}) %collective-permute-start.2) | collective-permute-done | bytes 16416 | tf_op jit(solution)/shard_map/ppermute | solution.py:581
  20.6 1.6 %shard_map.189 = (f32[768,512]{1,0:T(8,128)S(1)}, bf16[256,512]{1,0:T(8,128)(2,1)S(1)}, bf16[256,512]{1,0:T(8,128)(2,1)S(1)}, bf16[16,512]{1,0:T(8,128)(2,1)S(1)...) custom-call(s32[2,128]{1,0:T(2,128)S(1)} %get-tuple-element.48.early, ...), custom_call_target="tpu_custom_call", output_to_operand_aliasing={{0}: (1, {})} | custom-call | flops 2147483648 | bytes 1048576 | tf_op jit(solution)/shard_map/pallas_call | solution.py:557
  22.2 2.5 %collective-permute-start.5 = (bf16[16,512]{1,0:T(8,128)(2,1)S(1)}, bf16[16,512]{1,0:T(8,128)(2,1)S(1)}, u32[]{:S(2)}, u32[]{:S(2)}) collective-permute-start(bf16[16,512]{1,0:T(8,128)(2,1)S(1)} %get-tuple-element.81), channel_id=1, source_target_pairs={{0,3},{1,2},{2,1},{3,0},{4,7},{5,6},{6,5},{7,4},{8,11},{9,10},{10,... | collective-permute-start | bytes 49160 | tf_op jit(solution)/shard_map/ppermute | solution.py:581
  24.7 1.9 %collective-permute-start.7 = (bf16[16,512]{1,0:T(8,128)(2,1)S(1)}, bf16[16,512]{1,0:T(8,128)(2,1)S(1)}, u32[]{:S(2)}, u32[]{:S(2)}) collective-permute-start(bf16[16,512]{1,0:T(8,128)(2,1)S(1)} %get-tuple-element.83), channel_id=1, source_target_pairs={{0,1},{1,0},{2,3},{3,2},{4,5},{5,4},{6,7},{7,6},{8,9},{9,8},{10,11... | collective-permute-start | bytes 49160 | tf_op jit(solution)/shard_map/ppermute | solution.py:581
  26.7 1.8 %shard_map.190 = (f32[256,512]{1,0:T(8,128)S(1)}, bf16[256,512]{1,0:T(8,128)(2,1)S(1)}, bf16[256,512]{1,0:T(8,128)(2,1)S(1)}, bf16[256,768]{1,0:T(8,128)(2,1)S(1)}) custom-call(f32[768,512]{1,0:T(8,128)S(1)} %get-tuple-element.56.half, f32[768,512]{1,0:T(8,128)S(1)} %get-tuple-element.70.half2, bf16[256,512]{1,0:T(8,128)(2,1)S(1)} %get-tuple-element.71.grad_first, ...), custom_call_target="tpu_custom_call" | custom-call | flops 2147483648 | bytes 1048576 | tf_op jit(solution)/shard_map/pallas_call | solution.py:557
  28.5 0.9 %collective-permute-done.6.refs_1_ = bf16[16,512]{1,0:T(8,128)(2,1)S(1)} collective-permute-done((bf16[16,512]{1,0:T(8,128)(2,1)S(1)}, bf16[16,512]{1,0:T(8,128)(2,1)S(1)}, u32[]{:S(2)}, u32[]{:S(2)}) %collective-permute-start.6) | collective-permute-done | bytes 16416 | tf_op jit(solution)/shard_map/ppermute | solution.py:581
  29.4 1.1 %shard_map.191 = (bf16[256,512]{1,0:T(8,128)(2,1)S(1)}, bf16[256,512]{1,0:T(8,128)(2,1)S(1)}, bf16[128,512]{1,0:T(8,128)(2,1)S(1)}, bf16[128,512]{1,0:T(8,128)(2,1)S(1)}, f32[16,512]{1,0:T(8,128)S(1)}) custom-call(s32[2,128]{1,0:T(2,128)S(1)} %get-tuple-element.48.early, f32[256,512]{1,0:T(8,128)S(1)} %get-tuple-element.76.grad_local, ...), custom_call_target="tpu_custom_call" | custom-call | flops 2147483648 | bytes 1048576 | tf_op jit(solution)/shard_map/pallas_call | solution.py:557
  30.4 0.1 collective-permute-start.8
  30.5 1.3 %collective-permute-start.9 = (bf16[128,512]{1,0:T(8,128)(2,1)S(1)}, bf16[128,512]{1,0:T(8,128)(2,1)S(1)}, u32[]{:S(2)}, u32[]{:S(2)}) collective-permute-start(bf16[128,512]{1,0:T(8,128)(2,1)S(1)} %get-tuple-element.90), channel_id=1, source_target_pairs={{0,28},{4,8},{8,4},{12,16},{16,12},{20,24},{24,20},{28,0},{1,29},{... | collective-permute-start | bytes 393224 | tf_op jit(solution)/shard_map/ppermute | solution.py:573
  31.9 0.0 collective-permute-done.8.near
  31.9 1.8 %shard_map.192 = (bf16[256,512]{1,0:T(8,128)(2,1)}, f32[512,512]{1,0:T(8,128)S(1)}, bf16[512,128]{1,0:T(8,128)(2,1)S(1)}) custom-call(bf16[256,512]{1,0:T(8,128)(2,1)S(1)} %get-tuple-element.84.grad_first, bf16[256,512]{1,0:T(8,128)(2,1)S(1)} %get-tuple-element.85.back, f32[768,512]{1,0:T(8,128)S(1)} %get-tuple-element.56.half, ...), custom_call_target="tpu_custom_call" | custom-call | flops 2147483648 | bytes 1048576 | tf_op jit(solution)/shard_map/pallas_call | solution.py:557
  33.7 3.5 %collective-permute-done.9.far = bf16[128,512]{1,0:T(8,128)(2,1)S(1)} collective-permute-done((bf16[128,512]{1,0:T(8,128)(2,1)S(1)}, bf16[128,512]{1,0:T(8,128)(2,1)S(1)}, u32[]{:S(2)}, u32[]{:S(2)}) %collective-permute-start.9) | collective-permute-done | bytes 131104 | tf_op jit(solution)/shard_map/ppermute | solution.py:573
  37.2 1.3 %shard_map.193 = bf16[512,512]{1,0:T(8,128)(2,1)} custom-call(f32[512,512]{1,0:T(8,128)S(1)} %get-tuple-element.88.own, bf16[512,128]{1,0:T(8,128)(2,1)S(1)} %get-tuple-element.89.sum_far, bf16[128,512]{1,0:T(8,128)(2,1)S(1)} %collective-permute-done.9.far, bf16[512,512]{1,0:T(8,128)(2,1)S(1)} %copy-done.5), custom_call_target="tpu_custom_call" | custom-call | flops 2147483648 | bytes 1048576 | tf_op jit(solution)/shard_map/pallas_call | solution.py:557
  (28 shorter events, 0.1 us)
Async XLA Ops:
  0.6 7.0 %copy-start.5 = (bf16[512,512]{1,0:T(8,128)(2,1)S(1)}, bf16[512,512]{1,0:T(8,128)(2,1)}, u32[]{:S(2)}) copy-start(bf16[512,512]{1,0:T(8,128)(2,1)} %w_source.13) | copy-start | bytes 1572868
  0.6 7.0 %copy-start.6 = (bf16[256,512]{1,0:T(8,128)(2,1)S(1)}, bf16[256,512]{1,0:T(8,128)(2,1)}, u32[]{:S(2)}) copy-start(bf16[256,512]{1,0:T(8,128)(2,1)} %mesh.5) | copy-start | bytes 786436
  0.7 7.0 %copy-start.4 = (bf16[512,512]{1,0:T(8,128)(2,1)S(1)}, bf16[512,512]{1,0:T(8,128)(2,1)}, u32[]{:S(2)}) copy-start(bf16[512,512]{1,0:T(8,128)(2,1)} %w_dest.7) | copy-start | bytes 1572868
  0.7 7.0 %copy-start.11 = (s32[768]{0:T(1024)S(1)}, s32[768]{0:T(1024)}, u32[]{:S(2)}) copy-start(s32[768]{0:T(1024)} %target2.1) | copy-start | bytes 9220
  0.7 7.0 %copy-start.10 = (s32[768]{0:T(1024)S(1)}, s32[768]{0:T(1024)}, u32[]{:S(2)}) copy-start(s32[768]{0:T(1024)} %sender2.1) | copy-start | bytes 9220
  0.7 7.0 %copy-start.9 = (s32[768]{0:T(1024)S(1)}, s32[768]{0:T(1024)}, u32[]{:S(2)}) copy-start(s32[768]{0:T(1024)} %target.1) | copy-start | bytes 9220
  0.7 7.0 %copy-start.8 = (s32[768]{0:T(1024)S(1)}, s32[768]{0:T(1024)}, u32[]{:S(2)}) copy-start(s32[768]{0:T(1024)} %sender.1) | copy-start | bytes 9220
  2.2 8.6 %collective-permute-start = (bf16[128,512]{1,0:T(8,128)(2,1)S(1)}, bf16[128,512]{1,0:T(8,128)(2,1)S(1)}, u32[]{:S(2)}, u32[]{:S(2)}) collective-permute-start(bf16[128,512]{1,0:T(8,128)(2,1)S(1)} %get-tuple-element.49), channel_id=1, source_target_pairs={{0,4},{4,0},{8,12},{12,8},{16,20},{20,16},{24,28},{28,24},{1,5},{5... | collective-permute-start | bytes 393224 | tf_op jit(solution)/shard_map/ppermute | solution.py:574
  2.8 8.0 %collective-permute-start.1 = (bf16[128,512]{1,0:T(8,128)(2,1)S(1)}, bf16[128,512]{1,0:T(8,128)(2,1)S(1)}, u32[]{:S(2)}, u32[]{:S(2)}) collective-permute-start(bf16[128,512]{1,0:T(8,128)(2,1)S(1)} %get-tuple-element.50), channel_id=1, source_target_pairs={{0,28},{4,8},{8,4},{12,16},{16,12},{20,24},{24,20},{28,0},{1,29},{... | collective-permute-start | bytes 393224 | tf_op jit(solution)/shard_map/ppermute | solution.py:573
  7.7 3.1 %copy-start.2 = (bf16[512,512]{1,0:T(8,128)(2,1)S(1)}, bf16[512,512]{1,0:T(8,128)(2,1)}, u32[]{:S(2)}) copy-start(bf16[512,512]{1,0:T(8,128)(2,1)} %w_out.9) | copy-start | bytes 1572868
  7.7 3.1 %copy-start.13 = (f32[512]{0:T(512)S(1)}, f32[512]{0:T(512)}, u32[]{:S(2)}) copy-start(f32[512]{0:T(512)} %gain.7) | copy-start | bytes 6148
  10.8 6.0 %copy-start.1 = (bf16[512,512]{1,0:T(8,128)(2,1)S(1)}, bf16[512,512]{1,0:T(8,128)(2,1)}, u32[]{:S(2)}) copy-start(bf16[512,512]{1,0:T(8,128)(2,1)} %w_dest.6) | copy-start | bytes 1572868
  10.8 5.9 %copy-start.3 = (bf16[512,512]{1,0:T(8,128)(2,1)S(1)}, bf16[512,512]{1,0:T(8,128)(2,1)}, u32[]{:S(2)}) copy-start(bf16[512,512]{1,0:T(8,128)(2,1)} %w_source2.1) | copy-start | bytes 1572868
  10.8 5.9 %copy-start.7 = (bf16[256,512]{1,0:T(8,128)(2,1)S(1)}, bf16[256,512]{1,0:T(8,128)(2,1)}, u32[]{:S(2)}) copy-start(bf16[256,512]{1,0:T(8,128)(2,1)} %cotangent.3) | copy-start | bytes 786436
  10.8 5.9 %copy-start.12 = (f32[512]{0:T(512)S(1)}, f32[512]{0:T(512)}, u32[]{:S(2)}) copy-start(f32[512]{0:T(512)} %gain2.1) | copy-start | bytes 6148
  12.0 6.8 %collective-permute-start.4 = (bf16[16,512]{1,0:T(8,128)(2,1)S(1)}, bf16[16,512]{1,0:T(8,128)(2,1)S(1)}, u32[]{:S(2)}, u32[]{:S(2)}) collective-permute-start(bf16[16,512]{1,0:T(8,128)(2,1)S(1)} %get-tuple-element.69), channel_id=1, source_target_pairs={{0,2},{1,0},{2,3},{3,1},{4,6},{5,4},{6,7},{7,5},{8,10},{9,8},{10,1... | collective-permute-start | bytes 49160 | tf_op jit(solution)/shard_map/ppermute | solution.py:581
  14.6 5.5 %collective-permute-start.3 = (bf16[16,512]{1,0:T(8,128)(2,1)S(1)}, bf16[16,512]{1,0:T(8,128)(2,1)S(1)}, u32[]{:S(2)}, u32[]{:S(2)}) collective-permute-start(bf16[16,512]{1,0:T(8,128)(2,1)S(1)} %get-tuple-element.69), channel_id=1, source_target_pairs={{0,3},{1,2},{2,1},{3,0},{4,7},{5,6},{6,5},{7,4},{8,11},{9,10},{10,... | collective-permute-start | bytes 49160 | tf_op jit(solution)/shard_map/ppermute | solution.py:581
  15.9 4.6 %collective-permute-start.2 = (bf16[16,512]{1,0:T(8,128)(2,1)S(1)}, bf16[16,512]{1,0:T(8,128)(2,1)S(1)}, u32[]{:S(2)}, u32[]{:S(2)}) collective-permute-start(bf16[16,512]{1,0:T(8,128)(2,1)S(1)} %get-tuple-element.69), channel_id=1, source_target_pairs={{0,1},{1,3},{2,0},{3,2},{4,5},{5,7},{6,4},{7,6},{8,9},{9,11},{10,8... | collective-permute-start | bytes 49160 | tf_op jit(solution)/shard_map/ppermute | solution.py:581
  16.7 3.8 %copy-start = (bf16[512,512]{1,0:T(8,128)(2,1)S(1)}, bf16[512,512]{1,0:T(8,128)(2,1)}, u32[]{:S(2)}) copy-start(bf16[512,512]{1,0:T(8,128)(2,1)} %w_out.7) | copy-start | bytes 1572868
  22.2 6.2 %collective-permute-start.5 = (bf16[16,512]{1,0:T(8,128)(2,1)S(1)}, bf16[16,512]{1,0:T(8,128)(2,1)S(1)}, u32[]{:S(2)}, u32[]{:S(2)}) collective-permute-start(bf16[16,512]{1,0:T(8,128)(2,1)S(1)} %get-tuple-element.81), channel_id=1, source_target_pairs={{0,3},{1,2},{2,1},{3,0},{4,7},{5,6},{6,5},{7,4},{8,11},{9,10},{10,... | collective-permute-start | bytes 49160 | tf_op jit(solution)/shard_map/ppermute | solution.py:581
  24.7 4.6 %collective-permute-start.6 = (bf16[16,512]{1,0:T(8,128)(2,1)S(1)}, bf16[16,512]{1,0:T(8,128)(2,1)S(1)}, u32[]{:S(2)}, u32[]{:S(2)}) collective-permute-start(bf16[16,512]{1,0:T(8,128)(2,1)S(1)} %get-tuple-element.82), channel_id=1, source_target_pairs={{0,2},{1,3},{2,0},{3,1},{4,6},{5,7},{6,4},{7,5},{8,10},{9,11},{10,... | collective-permute-start | bytes 49160 | tf_op jit(solution)/shard_map/ppermute | solution.py:581
  24.7 4.6 %collective-permute-start.7 = (bf16[16,512]{1,0:T(8,128)(2,1)S(1)}, bf16[16,512]{1,0:T(8,128)(2,1)S(1)}, u32[]{:S(2)}, u32[]{:S(2)}) collective-permute-start(bf16[16,512]{1,0:T(8,128)(2,1)S(1)} %get-tuple-element.83), channel_id=1, source_target_pairs={{0,1},{1,0},{2,3},{3,2},{4,5},{5,4},{6,7},{7,6},{8,9},{9,8},{10,11... | collective-permute-start | bytes 49160 | tf_op jit(solution)/shard_map/ppermute | solution.py:581
  29.4 2.5 %copy-start.14 = (s32[256]{0:T(256)S(1)}, s32[256]{0:T(256)}, u32[]{:S(2)}) copy-start(s32[256]{0:T(256)} %halo.1) | copy-start | bytes 3076
  30.4 1.4 %collective-permute-start.8 = (bf16[128,512]{1,0:T(8,128)(2,1)S(1)}, bf16[128,512]{1,0:T(8,128)(2,1)S(1)}, u32[]{:S(2)}, u32[]{:S(2)}) collective-permute-start(bf16[128,512]{1,0:T(8,128)(2,1)S(1)} %get-tuple-element.87), channel_id=1, source_target_pairs={{0,4},{4,0},{8,12},{12,8},{16,20},{20,16},{24,28},{28,24},{1,5},{5... | collective-permute-start | bytes 393224 | tf_op jit(solution)/shard_map/ppermute | solution.py:574
  30.5 6.7 %collective-permute-start.9 = (bf16[128,512]{1,0:T(8,128)(2,1)S(1)}, bf16[128,512]{1,0:T(8,128)(2,1)S(1)}, u32[]{:S(2)}, u32[]{:S(2)}) collective-permute-start(bf16[128,512]{1,0:T(8,128)(2,1)S(1)} %get-tuple-element.90), channel_id=1, source_target_pairs={{0,28},{4,8},{8,4},{12,16},{16,12},{20,24},{24,20},{28,0},{1,29},{... | collective-permute-start | bytes 393224 | tf_op jit(solution)/shard_map/ppermute | solution.py:573

commit v7 on v6

--- a/solution.py
+++ b/solution.py
@@ -190,7 +190,9 @@
     mesh,
     w_source,
     w_dest,
+    near,
     early,
+    near_source,
     part,
     hidden,
     summed16,
@@ -208,6 +210,7 @@
     rim = pick_rim.shape[1] // 2
     source = (0.5 * mm(grid[...], w_source[...])).astype(BF16)
     dest = (0.5 * mm(mesh[...], w_dest[...])).astype(BF16)
+    near_source[...] = (0.5 * mm(near[...], w_source[...])).astype(BF16)
     me = lax.axis_index("group")
     gather, reduce = plans(groups)
     sources = [look_up([p.index(i) for i in range(groups)], me) for p in gather]
@@ -245,7 +248,7 @@
 def encode_halo_kernel(
     coarse,
     early,
-    near,
+    near_source,
     far,
     part,
     hidden_local,
@@ -261,8 +264,8 @@
     updated16,
 ):
     number = jnp.max(early[:1, :])
-    halo = jnp.concatenate([near[...], far[...]], axis=0)
-    source = (0.5 * mm(halo, w_source[...])).astype(BF16)
+    far_source = (0.5 * mm(far[...], w_source[...])).astype(BF16)
+    source = jnp.concatenate([near_source[...], far_source], axis=0)
 
     def edges(c):
         u = part[c, :] + mm(pick_rim[c, :], source)
@@ -353,7 +356,7 @@
 ):
     peers = sum_coarse.shape[0] // coarse
     received, (half, grad_first, back_ref) = refs[:peers], refs[peers : peers + 3]
-    returned, (hidden, slope, grad) = refs[peers + 3 : -3], refs[-3:]
+    returned, (hidden, slope, grad, gathered, turned) = refs[peers + 3 : -5], refs[-5:]
     number = jnp.max(early[1:, :])
     rows = jnp.concatenate([r[...] for r in received], axis=0)
     source = (0.5 * mm(rows, w_source[...])).astype(BF16)
@@ -370,12 +373,14 @@
         slope[c, :] = double.astype(BF16)
 
     def turn(summed):
-        center = centred(mm(summed.astype(BF16), w_out[...]))
-        inverse = lax.rsqrt(jnp.mean(center * center, axis=-1, keepdims=True) + EPSILON)
-        share = jnp.mean(center * centre2[...], axis=-1, keepdims=True)
-        share = share * inverse * inverse
-        back = (inverse * (centre2[...] - center * share)).astype(BF16)
-        back = (0.5 * mm_t(back, w_out[...])).astype(BF16)
+        gathered[...] = mm(summed.astype(BF16), w_out[...])
+        for r in pieces_of(gathered.shape[0], 32):
+            center = centred(gathered[r, :])
+            inverse = lax.rsqrt(jnp.mean(center * center, axis=-1, keepdims=True) + EPSILON)
+            share = jnp.mean(center * centre2[r, :], axis=-1, keepdims=True)
+            share = share * inverse * inverse
+            turned[r, :] = (inverse * (centre2[r, :] - center * share)).astype(BF16)
+        back = (0.5 * mm_t(turned[...], w_out[...])).astype(BF16)
         back_ref[...] = back
         grad_first[...] = (mm(pick_goal2[:FIRST, :], back) * slope[:FIRST, :].astype(F32)).astype(BF16)
         return back
@@ -624,6 +629,7 @@
     near, far = swap_halo(near, far, patches)
     (
         early,
+        near_source,
         part,
         hidden,
         summed16,
@@ -647,8 +653,9 @@
             mesh_latent,
             encoder_source,
             encoder_dest,
-        ],
-        [((2, LANES), I32), ((slots, hidden_size), F32), ((slots, hidden_size), BF16)]
+            near,
+        ],
+        [((2, LANES), I32), ((rim, hidden_size), BF16), ((slots, hidden_size), F32), ((slots, hidden_size), BF16)]
         + [((coarse, hidden_size), F32), row_form, row_form, row_form2, row_form2]
         + [column_form2, column_form2]
         + [((slots, 2 * rim), BF16), ((slots, mesh_rows), BF16)],
@@ -659,7 +666,7 @@
         functools.partial(encode_halo_kernel, coarse),
         [
             early,
-            near,
+            near_source,
             far,
             part,
             hidden,
@@ -740,6 +747,8 @@
             pltpu.VMEM((slots2, hidden_size), BF16),
             pltpu.VMEM((slots2, hidden_size), BF16),
             pltpu.VMEM((slots2, hidden_size), BF16),
+            pltpu.VMEM((mesh_rows, width), F32),
+            pltpu.VMEM((mesh_rows, width), BF16),
         ],
         aliases={1: 0},
     )

time: 38.7 us -> 38.6 us (level)
  no operation moved by 1% of the time
where the time goes in v7:
time: 38.6 us; the launch traced here: 38.4 us
  Pallas kernels  15.1 us (39%)
  starting transfers between devices  14.8 us (38%)
  waiting for transfers between devices  6.2 us (16%)
  between operations  2.18 us (6%)
    pallas_call x9, Pallas kernels, call(): pl.pallas_call(kernel, out_shape=[jax.ShapeDtypeStruct(s, d) for s, d in...  15.1 us
    ppermute x6, starting transfers between devices, exchange(): out.append(lax.ppermute(piece, 'group', list(enumerate(goals))))  9.23 us
    ppermute x2, starting transfers between devices, swap_halo(): far = lax.ppermute(far, 'patch', far_pairs)  4.93 us
    ppermute x2, waiting for transfers between devices, swap_halo(): far = lax.ppermute(far, 'patch', far_pairs)  3.45 us
    ppermute x6, waiting for transfers between devices, exchange(): out.append(lax.ppermute(piece, 'group', list(enumerate(goals))))  2.75 us
  transfers between devices with their start and end apart: 10, of which 4 were waited for; matrix products, arithmetic and copies ran while one was open for 0% of the time, Pallas kernels for 22%

profile of v7, /device:TPU:0, one launch (start us, length us, event | category | flops | bytes accessed | tf_op | source)
XLA Modules:
  0.0 38.4 jit_solution(10586101979358522155)
XLA Ops:
  0.7 1.5 %shard_map.185 = (bf16[128,512]{1,0:T(8,128)(2,1)S(1)}, bf16[128,512]{1,0:T(8,128)(2,1)S(1)}, bf16[512,512]{1,0:T(8,128)(2,1)S(1)}) custom-call(s32[256]{0:T(256)} %halo.1, bf16[512,512]{1,0:T(8,128)(2,1)} %grid_hbm.1), custom_call_target="tpu_custom_call" | custom-call | flops 4294967296 | bytes 1048576 | tf_op jit(solution)/shard_map/pallas_call | solution.py:562
  2.2 0.6 %collective-permute-start = (bf16[128,512]{1,0:T(8,128)(2,1)S(1)}, bf16[128,512]{1,0:T(8,128)(2,1)S(1)}, u32[]{:S(2)}, u32[]{:S(2)}) collective-permute-start(bf16[128,512]{1,0:T(8,128)(2,1)S(1)} %get-tuple-element.49), channel_id=1, source_target_pairs={{0,4},{4,0},{8,12},{12,8},{16,20},{20,16},{24,28},{28,24},{1,5},{5... | collective-permute-start | bytes 393224 | tf_op jit(solution)/shard_map/ppermute | solution.py:579
  2.7 3.5 %collective-permute-start.1 = (bf16[128,512]{1,0:T(8,128)(2,1)S(1)}, bf16[128,512]{1,0:T(8,128)(2,1)S(1)}, u32[]{:S(2)}, u32[]{:S(2)}) collective-permute-start(bf16[128,512]{1,0:T(8,128)(2,1)S(1)} %get-tuple-element.52), channel_id=1, source_target_pairs={{0,28},{4,8},{8,4},{12,16},{16,12},{20,24},{24,20},{28,0},{1,29},{... | collective-permute-start | bytes 393224 | tf_op jit(solution)/shard_map/ppermute | solution.py:578
  7.6 0.1 pad_add_fusion.counts
  7.7 0.0 collective-permute-done.near
  7.7 0.0 copy-start.2
  7.7 0.0 copy-start.13
  7.8 3.0 %shard_map.186 = (s32[2,128]{1,0:T(2,128)S(1)}, bf16[128,512]{1,0:T(8,128)(2,1)S(1)}, f32[768,512]{1,0:T(8,128)S(1)}, bf16[768,512]{1,0:T(8,128)(2,1)S(1)}, f32[...) custom-call(s32[2]{0:T(128)S(1)} %pad_add_fusion.counts, ...), custom_call_target="tpu_custom_call" | custom-call | flops 2147483648 | bytes 1048576 | tf_op jit(solution)/shard_map/pallas_call | solution.py:562
  10.7 0.0 copy-start.1
  10.8 0.0 copy-start.3
  10.8 0.0 copy-start.7
  10.8 0.0 copy-start.12
  10.8 1.0 %shard_map.187 = (f32[768,512]{1,0:T(8,128)S(1)}, bf16[768,512]{1,0:T(8,128)(2,1)S(1)}, bf16[16,512]{1,0:T(8,128)(2,1)S(1)}) custom-call(s32[2,128]{1,0:T(2,128)S(1)} %get-tuple-element.50.early, bf16[128,512]{1,0:T(8,128)(2,1)S(1)} %get-tuple-element.51.near_source, ...), custom_call_target="tpu_custom_call", output_to_operand_aliasing={{0}: (3, {}), {1}: (4, {})} | custom-call | flops 2147483648 | bytes 1048576 | tf_op jit(solution)/shard_map/pallas_call | solution.py:562
  11.8 2.6 %collective-permute-start.4 = (bf16[16,512]{1,0:T(8,128)(2,1)S(1)}, bf16[16,512]{1,0:T(8,128)(2,1)S(1)}, u32[]{:S(2)}, u32[]{:S(2)}) collective-permute-start(bf16[16,512]{1,0:T(8,128)(2,1)S(1)} %get-tuple-element.71), channel_id=1, source_target_pairs={{0,2},{1,0},{2,3},{3,1},{4,6},{5,4},{6,7},{7,5},{8,10},{9,8},{10,1... | collective-permute-start | bytes 49160 | tf_op jit(solution)/shard_map/ppermute | solution.py:586
  14.5 1.3 %collective-permute-start.3 = (bf16[16,512]{1,0:T(8,128)(2,1)S(1)}, bf16[16,512]{1,0:T(8,128)(2,1)S(1)}, u32[]{:S(2)}, u32[]{:S(2)}) collective-permute-start(bf16[16,512]{1,0:T(8,128)(2,1)S(1)} %get-tuple-element.71), channel_id=1, source_target_pairs={{0,3},{1,2},{2,1},{3,0},{4,7},{5,6},{6,5},{7,4},{8,11},{9,10},{10,... | collective-permute-start | bytes 49160 | tf_op jit(solution)/shard_map/ppermute | solution.py:586
  15.8 0.8 %collective-permute-start.2 = (bf16[16,512]{1,0:T(8,128)(2,1)S(1)}, bf16[16,512]{1,0:T(8,128)(2,1)S(1)}, u32[]{:S(2)}, u32[]{:S(2)}) collective-permute-start(bf16[16,512]{1,0:T(8,128)(2,1)S(1)} %get-tuple-element.71), channel_id=1, source_target_pairs={{0,1},{1,3},{2,0},{3,2},{4,5},{5,7},{6,4},{7,6},{8,9},{9,11},{10,8... | collective-permute-start | bytes 49160 | tf_op jit(solution)/shard_map/ppermute | solution.py:586
  16.6 0.0 copy-start
  16.6 2.0 %shard_map.188 = (f32[256,512]{1,0:T(8,128)S(1)}, f32[256,128]{1,0:T(8,128)S(1)}, f32[768,512]{1,0:T(8,128)S(1)}, bf16[768,256]{1,0:T(8,128)(2,1)S(1)}, bf16[768...) custom-call(bf16[768,512]{1,0:T(8,128)(2,1)S(1)} %get-tuple-element., ...), custom_call_target="tpu_custom_call" | custom-call | flops 2147483648 | bytes 1048576 | tf_op jit(solution)/shard_map/pallas_call | solution.py:562
  18.6 0.0 collective-permute-done.4.refs_2_
  18.6 1.4 %collective-permute-done.3.refs_1_ = bf16[16,512]{1,0:T(8,128)(2,1)S(1)} collective-permute-done((bf16[16,512]{1,0:T(8,128)(2,1)S(1)}, bf16[16,512]{1,0:T(8,128)(2,1)S(1)}, u32[]{:S(2)}, u32[]{:S(2)}) %collective-permute-start.3) | collective-permute-done | bytes 16416 | tf_op jit(solution)/shard_map/ppermute | solution.py:586
  20.0 0.4 %collective-permute-done.2.refs_0_ = bf16[16,512]{1,0:T(8,128)(2,1)S(1)} collective-permute-done((bf16[16,512]{1,0:T(8,128)(2,1)S(1)}, bf16[16,512]{1,0:T(8,128)(2,1)S(1)}, u32[]{:S(2)}, u32[]{:S(2)}) %collective-permute-start.2) | collective-permute-done | bytes 16416 | tf_op jit(solution)/shard_map/ppermute | solution.py:586
  20.5 1.6 %shard_map.189 = (f32[768,512]{1,0:T(8,128)S(1)}, bf16[256,512]{1,0:T(8,128)(2,1)S(1)}, bf16[256,512]{1,0:T(8,128)(2,1)S(1)}, bf16[16,512]{1,0:T(8,128)(2,1)S(1)...) custom-call(s32[2,128]{1,0:T(2,128)S(1)} %get-tuple-element.50.early, ...), custom_call_target="tpu_custom_call", output_to_operand_aliasing={{0}: (1, {})} | custom-call | flops 2147483648 | bytes 1048576 | tf_op jit(solution)/shard_map/pallas_call | solution.py:562
  22.1 2.5 %collective-permute-start.5 = (bf16[16,512]{1,0:T(8,128)(2,1)S(1)}, bf16[16,512]{1,0:T(8,128)(2,1)S(1)}, u32[]{:S(2)}, u32[]{:S(2)}) collective-permute-start(bf16[16,512]{1,0:T(8,128)(2,1)S(1)} %get-tuple-element.83), channel_id=1, source_target_pairs={{0,3},{1,2},{2,1},{3,0},{4,7},{5,6},{6,5},{7,4},{8,11},{9,10},{10,... | collective-permute-start | bytes 49160 | tf_op jit(solution)/shard_map/ppermute | solution.py:586
  24.6 1.9 %collective-permute-start.7 = (bf16[16,512]{1,0:T(8,128)(2,1)S(1)}, bf16[16,512]{1,0:T(8,128)(2,1)S(1)}, u32[]{:S(2)}, u32[]{:S(2)}) collective-permute-start(bf16[16,512]{1,0:T(8,128)(2,1)S(1)} %get-tuple-element.85), channel_id=1, source_target_pairs={{0,1},{1,0},{2,3},{3,2},{4,5},{5,4},{6,7},{7,6},{8,9},{9,8},{10,11... | collective-permute-start | bytes 49160 | tf_op jit(solution)/shard_map/ppermute | solution.py:586
  26.5 1.8 %shard_map.190 = (f32[256,512]{1,0:T(8,128)S(1)}, bf16[256,512]{1,0:T(8,128)(2,1)S(1)}, bf16[256,512]{1,0:T(8,128)(2,1)S(1)}, bf16[256,768]{1,0:T(8,128)(2,1)S(1)}) custom-call(f32[768,512]{1,0:T(8,128)S(1)} %get-tuple-element.58.half, f32[768,512]{1,0:T(8,128)S(1)} %get-tuple-element.72.half2, bf16[256,512]{1,0:T(8,128)(2,1)S(1)} %get-tuple-element.73.grad_first, ...), custom_call_target="tpu_custom_call" | custom-call | flops 2147483648 | bytes 1048576 | tf_op jit(solution)/shard_map/pallas_call | solution.py:562
  28.3 0.9 %collective-permute-done.6.refs_1_ = bf16[16,512]{1,0:T(8,128)(2,1)S(1)} collective-permute-done((bf16[16,512]{1,0:T(8,128)(2,1)S(1)}, bf16[16,512]{1,0:T(8,128)(2,1)S(1)}, u32[]{:S(2)}, u32[]{:S(2)}) %collective-permute-start.6) | collective-permute-done | bytes 16416 | tf_op jit(solution)/shard_map/ppermute | solution.py:586
  29.3 1.1 %shard_map.191 = (bf16[256,512]{1,0:T(8,128)(2,1)S(1)}, bf16[256,512]{1,0:T(8,128)(2,1)S(1)}, bf16[128,512]{1,0:T(8,128)(2,1)S(1)}, bf16[128,512]{1,0:T(8,128)(2,1)S(1)}, f32[16,512]{1,0:T(8,128)S(1)}) custom-call(s32[2,128]{1,0:T(2,128)S(1)} %get-tuple-element.50.early, f32[256,512]{1,0:T(8,128)S(1)} %get-tuple-element.78.grad_local, ...), custom_call_target="tpu_custom_call" | custom-call | flops 2147483648 | bytes 1048576 | tf_op jit(solution)/shard_map/pallas_call | solution.py:562
  30.3 0.1 collective-permute-start.8
  30.4 1.4 %collective-permute-start.9 = (bf16[128,512]{1,0:T(8,128)(2,1)S(1)}, bf16[128,512]{1,0:T(8,128)(2,1)S(1)}, u32[]{:S(2)}, u32[]{:S(2)}) collective-permute-start(bf16[128,512]{1,0:T(8,128)(2,1)S(1)} %get-tuple-element.92), channel_id=1, source_target_pairs={{0,28},{4,8},{8,4},{12,16},{16,12},{20,24},{24,20},{28,0},{1,29},{... | collective-permute-start | bytes 393224 | tf_op jit(solution)/shard_map/ppermute | solution.py:578
  31.8 1.8 %shard_map.192 = (bf16[256,512]{1,0:T(8,128)(2,1)}, f32[512,512]{1,0:T(8,128)S(1)}, bf16[512,128]{1,0:T(8,128)(2,1)S(1)}) custom-call(bf16[256,512]{1,0:T(8,128)(2,1)S(1)} %get-tuple-element.86.grad_first, bf16[256,512]{1,0:T(8,128)(2,1)S(1)} %get-tuple-element.87.back, f32[768,512]{1,0:T(8,128)S(1)} %get-tuple-element.58.half, ...), custom_call_target="tpu_custom_call" | custom-call | flops 2147483648 | bytes 1048576 | tf_op jit(solution)/shard_map/pallas_call | solution.py:562
  33.6 3.4 %collective-permute-done.9.far = bf16[128,512]{1,0:T(8,128)(2,1)S(1)} collective-permute-done((bf16[128,512]{1,0:T(8,128)(2,1)S(1)}, bf16[128,512]{1,0:T(8,128)(2,1)S(1)}, u32[]{:S(2)}, u32[]{:S(2)}) %collective-permute-start.9) | collective-permute-done | bytes 131104 | tf_op jit(solution)/shard_map/ppermute | solution.py:578
  37.1 1.3 %shard_map.193 = bf16[512,512]{1,0:T(8,128)(2,1)} custom-call(f32[512,512]{1,0:T(8,128)S(1)} %get-tuple-element.90.own, bf16[512,128]{1,0:T(8,128)(2,1)S(1)} %get-tuple-element.91.sum_far, bf16[128,512]{1,0:T(8,128)(2,1)S(1)} %collective-permute-done.9.far, bf16[512,512]{1,0:T(8,128)(2,1)S(1)} %copy-done.5), custom_call_target="tpu_custom_call" | custom-call | flops 2147483648 | bytes 1048576 | tf_op jit(solution)/shard_map/pallas_call | solution.py:562
  (28 shorter events, 0.1 us)
Async XLA Ops:
  0.6 7.0 %copy-start.5 = (bf16[512,512]{1,0:T(8,128)(2,1)S(1)}, bf16[512,512]{1,0:T(8,128)(2,1)}, u32[]{:S(2)}) copy-start(bf16[512,512]{1,0:T(8,128)(2,1)} %w_source.13) | copy-start | bytes 1572868
  0.6 7.0 %copy-start.6 = (bf16[256,512]{1,0:T(8,128)(2,1)S(1)}, bf16[256,512]{1,0:T(8,128)(2,1)}, u32[]{:S(2)}) copy-start(bf16[256,512]{1,0:T(8,128)(2,1)} %mesh.5) | copy-start | bytes 786436
  0.7 7.0 %copy-start.4 = (bf16[512,512]{1,0:T(8,128)(2,1)S(1)}, bf16[512,512]{1,0:T(8,128)(2,1)}, u32[]{:S(2)}) copy-start(bf16[512,512]{1,0:T(8,128)(2,1)} %w_dest.7) | copy-start | bytes 1572868
  0.7 7.0 %copy-start.11 = (s32[768]{0:T(1024)S(1)}, s32[768]{0:T(1024)}, u32[]{:S(2)}) copy-start(s32[768]{0:T(1024)} %target2.1) | copy-start | bytes 9220
  0.7 7.0 %copy-start.10 = (s32[768]{0:T(1024)S(1)}, s32[768]{0:T(1024)}, u32[]{:S(2)}) copy-start(s32[768]{0:T(1024)} %sender2.1) | copy-start | bytes 9220
  0.7 7.0 %copy-start.9 = (s32[768]{0:T(1024)S(1)}, s32[768]{0:T(1024)}, u32[]{:S(2)}) copy-start(s32[768]{0:T(1024)} %target.1) | copy-start | bytes 9220
  0.7 7.0 %copy-start.8 = (s32[768]{0:T(1024)S(1)}, s32[768]{0:T(1024)}, u32[]{:S(2)}) copy-start(s32[768]{0:T(1024)} %sender.1) | copy-start | bytes 9220
  2.2 5.5 %collective-permute-start = (bf16[128,512]{1,0:T(8,128)(2,1)S(1)}, bf16[128,512]{1,0:T(8,128)(2,1)S(1)}, u32[]{:S(2)}, u32[]{:S(2)}) collective-permute-start(bf16[128,512]{1,0:T(8,128)(2,1)S(1)} %get-tuple-element.49), channel_id=1, source_target_pairs={{0,4},{4,0},{8,12},{12,8},{16,20},{20,16},{24,28},{28,24},{1,5},{5... | collective-permute-start | bytes 393224 | tf_op jit(solution)/shard_map/ppermute | solution.py:579
  2.7 8.0 %collective-permute-start.1 = (bf16[128,512]{1,0:T(8,128)(2,1)S(1)}, bf16[128,512]{1,0:T(8,128)(2,1)S(1)}, u32[]{:S(2)}, u32[]{:S(2)}) collective-permute-start(bf16[128,512]{1,0:T(8,128)(2,1)S(1)} %get-tuple-element.52), channel_id=1, source_target_pairs={{0,28},{4,8},{8,4},{12,16},{16,12},{20,24},{24,20},{28,0},{1,29},{... | collective-permute-start | bytes 393224 | tf_op jit(solution)/shard_map/ppermute | solution.py:578
  7.7 3.0 %copy-start.2 = (bf16[512,512]{1,0:T(8,128)(2,1)S(1)}, bf16[512,512]{1,0:T(8,128)(2,1)}, u32[]{:S(2)}) copy-start(bf16[512,512]{1,0:T(8,128)(2,1)} %w_out.9) | copy-start | bytes 1572868
  7.7 3.0 %copy-start.13 = (f32[512]{0:T(512)S(1)}, f32[512]{0:T(512)}, u32[]{:S(2)}) copy-start(f32[512]{0:T(512)} %gain.7) | copy-start | bytes 6148
  10.7 5.9 %copy-start.1 = (bf16[512,512]{1,0:T(8,128)(2,1)S(1)}, bf16[512,512]{1,0:T(8,128)(2,1)}, u32[]{:S(2)}) copy-start(bf16[512,512]{1,0:T(8,128)(2,1)} %w_dest.6) | copy-start | bytes 1572868
  10.8 5.9 %copy-start.3 = (bf16[512,512]{1,0:T(8,128)(2,1)S(1)}, bf16[512,512]{1,0:T(8,128)(2,1)}, u32[]{:S(2)}) copy-start(bf16[512,512]{1,0:T(8,128)(2,1)} %w_source2.1) | copy-start | bytes 1572868
  10.8 5.9 %copy-start.7 = (bf16[256,512]{1,0:T(8,128)(2,1)S(1)}, bf16[256,512]{1,0:T(8,128)(2,1)}, u32[]{:S(2)}) copy-start(bf16[256,512]{1,0:T(8,128)(2,1)} %cotangent.3) | copy-start | bytes 786436
  10.8 5.9 %copy-start.12 = (f32[512]{0:T(512)S(1)}, f32[512]{0:T(512)}, u32[]{:S(2)}) copy-start(f32[512]{0:T(512)} %gain2.1) | copy-start | bytes 6148
  11.8 6.8 %collective-permute-start.4 = (bf16[16,512]{1,0:T(8,128)(2,1)S(1)}, bf16[16,512]{1,0:T(8,128)(2,1)S(1)}, u32[]{:S(2)}, u32[]{:S(2)}) collective-permute-start(bf16[16,512]{1,0:T(8,128)(2,1)S(1)} %get-tuple-element.71), channel_id=1, source_target_pairs={{0,2},{1,0},{2,3},{3,1},{4,6},{5,4},{6,7},{7,5},{8,10},{9,8},{10,1... | collective-permute-start | bytes 49160 | tf_op jit(solution)/shard_map/ppermute | solution.py:586
  14.5 5.5 %collective-permute-start.3 = (bf16[16,512]{1,0:T(8,128)(2,1)S(1)}, bf16[16,512]{1,0:T(8,128)(2,1)S(1)}, u32[]{:S(2)}, u32[]{:S(2)}) collective-permute-start(bf16[16,512]{1,0:T(8,128)(2,1)S(1)} %get-tuple-element.71), channel_id=1, source_target_pairs={{0,3},{1,2},{2,1},{3,0},{4,7},{5,6},{6,5},{7,4},{8,11},{9,10},{10,... | collective-permute-start | bytes 49160 | tf_op jit(solution)/shard_map/ppermute | solution.py:586
  15.8 4.6 %collective-permute-start.2 = (bf16[16,512]{1,0:T(8,128)(2,1)S(1)}, bf16[16,512]{1,0:T(8,128)(2,1)S(1)}, u32[]{:S(2)}, u32[]{:S(2)}) collective-permute-start(bf16[16,512]{1,0:T(8,128)(2,1)S(1)} %get-tuple-element.71), channel_id=1, source_target_pairs={{0,1},{1,3},{2,0},{3,2},{4,5},{5,7},{6,4},{7,6},{8,9},{9,11},{10,8... | collective-permute-start | bytes 49160 | tf_op jit(solution)/shard_map/ppermute | solution.py:586
  16.6 3.8 %copy-start = (bf16[512,512]{1,0:T(8,128)(2,1)S(1)}, bf16[512,512]{1,0:T(8,128)(2,1)}, u32[]{:S(2)}) copy-start(bf16[512,512]{1,0:T(8,128)(2,1)} %w_out.7) | copy-start | bytes 1572868
  22.1 6.2 %collective-permute-start.5 = (bf16[16,512]{1,0:T(8,128)(2,1)S(1)}, bf16[16,512]{1,0:T(8,128)(2,1)S(1)}, u32[]{:S(2)}, u32[]{:S(2)}) collective-permute-start(bf16[16,512]{1,0:T(8,128)(2,1)S(1)} %get-tuple-element.83), channel_id=1, source_target_pairs={{0,3},{1,2},{2,1},{3,0},{4,7},{5,6},{6,5},{7,4},{8,11},{9,10},{10,... | collective-permute-start | bytes 49160 | tf_op jit(solution)/shard_map/ppermute | solution.py:586
  24.6 4.6 %collective-permute-start.6 = (bf16[16,512]{1,0:T(8,128)(2,1)S(1)}, bf16[16,512]{1,0:T(8,128)(2,1)S(1)}, u32[]{:S(2)}, u32[]{:S(2)}) collective-permute-start(bf16[16,512]{1,0:T(8,128)(2,1)S(1)} %get-tuple-element.84), channel_id=1, source_target_pairs={{0,2},{1,3},{2,0},{3,1},{4,6},{5,7},{6,4},{7,5},{8,10},{9,11},{10,... | collective-permute-start | bytes 49160 | tf_op jit(solution)/shard_map/ppermute | solution.py:586
  24.6 4.6 %collective-permute-start.7 = (bf16[16,512]{1,0:T(8,128)(2,1)S(1)}, bf16[16,512]{1,0:T(8,128)(2,1)S(1)}, u32[]{:S(2)}, u32[]{:S(2)}) collective-permute-start(bf16[16,512]{1,0:T(8,128)(2,1)S(1)} %get-tuple-element.85), channel_id=1, source_target_pairs={{0,1},{1,0},{2,3},{3,2},{4,5},{5,4},{6,7},{7,6},{8,9},{9,8},{10,11... | collective-permute-start | bytes 49160 | tf_op jit(solution)/shard_map/ppermute | solution.py:586
  29.3 2.5 %copy-start.14 = (s32[256]{0:T(256)S(1)}, s32[256]{0:T(256)}, u32[]{:S(2)}) copy-start(s32[256]{0:T(256)} %halo.1) | copy-start | bytes 3076
  30.3 1.5 %collective-permute-start.8 = (bf16[128,512]{1,0:T(8,128)(2,1)S(1)}, bf16[128,512]{1,0:T(8,128)(2,1)S(1)}, u32[]{:S(2)}, u32[]{:S(2)}) collective-permute-start(bf16[128,512]{1,0:T(8,128)(2,1)S(1)} %get-tuple-element.89), channel_id=1, source_target_pairs={{0,4},{4,0},{8,12},{12,8},{16,20},{20,16},{24,28},{28,24},{1,5},{5... | collective-permute-start | bytes 393224 | tf_op jit(solution)/shard_map/ppermute | solution.py:579
  30.4 6.7 %collective-permute-start.9 = (bf16[128,512]{1,0:T(8,128)(2,1)S(1)}, bf16[128,512]{1,0:T(8,128)(2,1)S(1)}, u32[]{:S(2)}, u32[]{:S(2)}) collective-permute-start(bf16[128,512]{1,0:T(8,128)(2,1)S(1)} %get-tuple-element.92), channel_id=1, source_target_pairs={{0,28},{4,8},{8,4},{12,16},{16,12},{20,24},{24,20},{28,0},{1,29},{... | collective-permute-start | bytes 393224 | tf_op jit(solution)/shard_map/ppermute | solution.py:578

commit v8 on v7

--- a/solution.py
+++ b/solution.py
@@ -11,6 +11,7 @@
 EPSILON = 1e-05
 LANES = 128
 FIRST = 256
+FIRST2 = 128
 F32 = jnp.float32
 BF16 = jnp.bfloat16
 I32 = jnp.int32
@@ -332,12 +333,12 @@
     sum_goal2[...] = spread(live_goal2[...], 0, rows)
     sum_coarse[...] = spread(live_send2[...], rows, sum_coarse.shape[0])
     centre2[...] = centred(cotangent[...].astype(F32) * as_row(gain2))
-    for c in pieces_of(part.shape[0], FIRST):
+    for c in pieces_of(part.shape[0], FIRST2):
         u = mm(pick(send_col2[c, :], 0, rows), source) + mm(pick_goal2[c, :], dest)
         part[c, :] = u
         if c.start:
             hidden2[c, :] = (u + u * jnp.tanh(u)).astype(BF16)
-    summed2[...] = mm(sum_goal2[:, FIRST:], hidden2[FIRST:, :])
+    summed2[...] = mm(sum_goal2[:, FIRST2:], hidden2[FIRST2:, :])
 
 
 def process_kernel(
@@ -366,7 +367,7 @@
 
     def edges(c):
         u = part[c, :] + mm(pick_coarse[c, :], source)
-        if c.start >= FIRST:
+        if c.start >= FIRST2:
             half[c, :] = u
         value, double = half_silu(u)
         hidden[c, :] = value.astype(BF16)
@@ -382,7 +383,7 @@
             turned[r, :] = (inverse * (centre2[r, :] - center * share)).astype(BF16)
         back = (0.5 * mm_t(turned[...], w_out[...])).astype(BF16)
         back_ref[...] = back
-        grad_first[...] = (mm(pick_goal2[:FIRST, :], back) * slope[:FIRST, :].astype(F32)).astype(BF16)
+        grad_first[...] = (mm(pick_goal2[:FIRST2, :], back) * slope[:FIRST2, :].astype(F32)).astype(BF16)
         return back
 
     def send(sums):
@@ -390,23 +391,23 @@
             out[...] = sums[i * coarse : (i + 1) * coarse].astype(BF16)
 
     def first_edges():
-        for c in pieces_of(FIRST, 128):
+        for c in pieces_of(FIRST2, 128):
             edges(c)
 
-    @pl.when(number <= FIRST)
+    @pl.when(number <= FIRST2)
     def _():
         first_edges()
-        turn(summed2[...] + mm(sum_goal2[:, :FIRST], hidden[:FIRST, :]))
-        send(mm(sum_coarse[:, :FIRST], grad_first[...]))
-
-    @pl.when(number > FIRST)
+        turn(summed2[...] + mm(sum_goal2[:, :FIRST2], hidden[:FIRST2, :]))
+        send(mm(sum_coarse[:, :FIRST2], grad_first[...]))
+
+    @pl.when(number > FIRST2)
     def _():
         first_edges()
-        later = pieces_of(part.shape[0], FIRST)[1:]
+        later = pieces_of(part.shape[0], FIRST2)[1:]
         for c in later:
             edges(c)
         back = turn(mm(sum_goal2[...], hidden[...]))
-        grad[:FIRST, :] = grad_first[...]
+        grad[:FIRST2, :] = grad_first[...]
         for c in later:
             grad[c, :] = (mm(pick_goal2[c, :], back) * slope[c, :].astype(F32)).astype(BF16)
         send(mm(sum_coarse[...], grad[...]))
@@ -437,8 +438,8 @@
 ):
     rows = cotangent.shape[0]
     rim = sum_rim.shape[0] // 2
-    grad[:FIRST, :] = grad_first[...]
-    for c in pieces_of(half2.shape[0], FIRST)[1:]:
+    grad[:FIRST2, :] = grad_first[...]
+    for c in pieces_of(half2.shape[0], FIRST2)[1:]:
         double = half_silu(half2[c, :])[1]
         grad[c, :] = (mm(pick_goal2[c, :], back2[...]) * double).astype(BF16)
     table = mm(spread(live_send2[...], 0, rows), grad[...]).astype(BF16)
@@ -739,7 +740,7 @@
             process_output,
             *shifts,
         ],
-        [((slots2, hidden_size), F32), ((FIRST, hidden_size), BF16)]
+        [((slots2, hidden_size), F32), ((FIRST2, hidden_size), BF16)]
         + [((mesh_rows, hidden_size), BF16)]
         + [((coarse, hidden_size), BF16)] * (groups - 1),
         2,

time: 38.6 us -> 38.5 us (level)
  transfers between devices with their start and end apart: 10 -> 10, of which waited for: 4 -> 4; matrix products, arithmetic and copies ran while one was open for 0% -> 0% of each run, Pallas kernels for 22% -> 23%
where the time goes in v8:
time: 38.5 us; the launch traced here: 38.3 us
  Pallas kernels  15.2 us (39%)
  starting transfers between devices  14.8 us (38%)
  waiting for transfers between devices  6.1 us (16%)
  between operations  2.18 us (6%)
    pallas_call x9, Pallas kernels, call(): pl.pallas_call(kernel, out_shape=[jax.ShapeDtypeStruct(s, d) for s, d in...  15.2 us
    ppermute x6, starting transfers between devices, exchange(): out.append(lax.ppermute(piece, 'group', list(enumerate(goals))))  9.23 us
    ppermute x2, starting transfers between devices, swap_halo(): far = lax.ppermute(far, 'patch', far_pairs)  4.9 us
    ppermute x2, waiting for transfers between devices, swap_halo(): far = lax.ppermute(far, 'patch', far_pairs)  3.49 us
    ppermute x6, waiting for transfers between devices, exchange(): out.append(lax.ppermute(piece, 'group', list(enumerate(goals))))  2.6 us
  transfers between devices with their start and end apart: 10, of which 4 were waited for; matrix products, arithmetic and copies ran while one was open for 0% of the time, Pallas kernels for 23%

profile of v8, /device:TPU:0, one launch (start us, length us, event | category | flops | bytes accessed | tf_op | source)
XLA Modules:
  0.0 38.3 jit_solution(2415637031830602960)
XLA Ops:
  0.7 1.5 %shard_map.185 = (bf16[128,512]{1,0:T(8,128)(2,1)S(1)}, bf16[128,512]{1,0:T(8,128)(2,1)S(1)}, bf16[512,512]{1,0:T(8,128)(2,1)S(1)}) custom-call(s32[256]{0:T(256)} %halo.1, bf16[512,512]{1,0:T(8,128)(2,1)} %grid_hbm.1), custom_call_target="tpu_custom_call" | custom-call | flops 4294967296 | bytes 1048576 | tf_op jit(solution)/shard_map/pallas_call | solution.py:563
  2.2 0.6 %collective-permute-start = (bf16[128,512]{1,0:T(8,128)(2,1)S(1)}, bf16[128,512]{1,0:T(8,128)(2,1)S(1)}, u32[]{:S(2)}, u32[]{:S(2)}) collective-permute-start(bf16[128,512]{1,0:T(8,128)(2,1)S(1)} %get-tuple-element.49), channel_id=1, source_target_pairs={{0,4},{4,0},{8,12},{12,8},{16,20},{20,16},{24,28},{28,24},{1,5},{5... | collective-permute-start | bytes 393224 | tf_op jit(solution)/shard_map/ppermute | solution.py:580
  2.7 3.5 %collective-permute-start.1 = (bf16[128,512]{1,0:T(8,128)(2,1)S(1)}, bf16[128,512]{1,0:T(8,128)(2,1)S(1)}, u32[]{:S(2)}, u32[]{:S(2)}) collective-permute-start(bf16[128,512]{1,0:T(8,128)(2,1)S(1)} %get-tuple-element.52), channel_id=1, source_target_pairs={{0,28},{4,8},{8,4},{12,16},{16,12},{20,24},{24,20},{28,0},{1,29},{... | collective-permute-start | bytes 393224 | tf_op jit(solution)/shard_map/ppermute | solution.py:579
  7.6 0.1 pad_add_fusion.counts
  7.7 0.0 collective-permute-done.near
  7.7 0.0 copy-start.2
  7.7 0.0 copy-start.13
  7.8 3.0 %shard_map.186 = (s32[2,128]{1,0:T(2,128)S(1)}, bf16[128,512]{1,0:T(8,128)(2,1)S(1)}, f32[768,512]{1,0:T(8,128)S(1)}, bf16[768,512]{1,0:T(8,128)(2,1)S(1)}, f32[...) custom-call(s32[2]{0:T(128)S(1)} %pad_add_fusion.counts, ...), custom_call_target="tpu_custom_call" | custom-call | flops 2147483648 | bytes 1048576 | tf_op jit(solution)/shard_map/pallas_call | solution.py:563
  10.7 0.0 copy-start.1
  10.8 0.0 copy-start.3
  10.8 0.0 copy-start.7
  10.8 0.0 copy-start.12
  10.8 1.0 %shard_map.187 = (f32[768,512]{1,0:T(8,128)S(1)}, bf16[768,512]{1,0:T(8,128)(2,1)S(1)}, bf16[16,512]{1,0:T(8,128)(2,1)S(1)}) custom-call(s32[2,128]{1,0:T(2,128)S(1)} %get-tuple-element.50.early, bf16[128,512]{1,0:T(8,128)(2,1)S(1)} %get-tuple-element.51.near_source, ...), custom_call_target="tpu_custom_call", output_to_operand_aliasing={{0}: (3, {}), {1}: (4, {})} | custom-call | flops 2147483648 | bytes 1048576 | tf_op jit(solution)/shard_map/pallas_call | solution.py:563
  11.9 2.6 %collective-permute-start.4 = (bf16[16,512]{1,0:T(8,128)(2,1)S(1)}, bf16[16,512]{1,0:T(8,128)(2,1)S(1)}, u32[]{:S(2)}, u32[]{:S(2)}) collective-permute-start(bf16[16,512]{1,0:T(8,128)(2,1)S(1)} %get-tuple-element.71), channel_id=1, source_target_pairs={{0,2},{1,0},{2,3},{3,1},{4,6},{5,4},{6,7},{7,5},{8,10},{9,8},{10,1... | collective-permute-start | bytes 49160 | tf_op jit(solution)/shard_map/ppermute | solution.py:587
  14.5 1.4 %collective-permute-start.3 = (bf16[16,512]{1,0:T(8,128)(2,1)S(1)}, bf16[16,512]{1,0:T(8,128)(2,1)S(1)}, u32[]{:S(2)}, u32[]{:S(2)}) collective-permute-start(bf16[16,512]{1,0:T(8,128)(2,1)S(1)} %get-tuple-element.71), channel_id=1, source_target_pairs={{0,3},{1,2},{2,1},{3,0},{4,7},{5,6},{6,5},{7,4},{8,11},{9,10},{10,... | collective-permute-start | bytes 49160 | tf_op jit(solution)/shard_map/ppermute | solution.py:587
  15.8 0.8 %collective-permute-start.2 = (bf16[16,512]{1,0:T(8,128)(2,1)S(1)}, bf16[16,512]{1,0:T(8,128)(2,1)S(1)}, u32[]{:S(2)}, u32[]{:S(2)}) collective-permute-start(bf16[16,512]{1,0:T(8,128)(2,1)S(1)} %get-tuple-element.71), channel_id=1, source_target_pairs={{0,1},{1,3},{2,0},{3,2},{4,5},{5,7},{6,4},{7,6},{8,9},{9,11},{10,8... | collective-permute-start | bytes 49160 | tf_op jit(solution)/shard_map/ppermute | solution.py:587
  16.6 0.0 copy-start
  16.7 2.0 %shard_map.188 = (f32[256,512]{1,0:T(8,128)S(1)}, f32[256,128]{1,0:T(8,128)S(1)}, f32[768,512]{1,0:T(8,128)S(1)}, bf16[768,256]{1,0:T(8,128)(2,1)S(1)}, bf16[768...) custom-call(bf16[768,512]{1,0:T(8,128)(2,1)S(1)} %get-tuple-element., ...), custom_call_target="tpu_custom_call" | custom-call | flops 2147483648 | bytes 1048576 | tf_op jit(solution)/shard_map/pallas_call | solution.py:563
  18.7 0.0 collective-permute-done.4.refs_2_
  18.7 1.3 %collective-permute-done.3.refs_1_ = bf16[16,512]{1,0:T(8,128)(2,1)S(1)} collective-permute-done((bf16[16,512]{1,0:T(8,128)(2,1)S(1)}, bf16[16,512]{1,0:T(8,128)(2,1)S(1)}, u32[]{:S(2)}, u32[]{:S(2)}) %collective-permute-start.3) | collective-permute-done | bytes 16416 | tf_op jit(solution)/shard_map/ppermute | solution.py:587
  20.0 0.5 %collective-permute-done.2.refs_0_ = bf16[16,512]{1,0:T(8,128)(2,1)S(1)} collective-permute-done((bf16[16,512]{1,0:T(8,128)(2,1)S(1)}, bf16[16,512]{1,0:T(8,128)(2,1)S(1)}, u32[]{:S(2)}, u32[]{:S(2)}) %collective-permute-start.2) | collective-permute-done | bytes 16416 | tf_op jit(solution)/shard_map/ppermute | solution.py:587
  20.5 1.5 %shard_map.189 = (f32[768,512]{1,0:T(8,128)S(1)}, bf16[128,512]{1,0:T(8,128)(2,1)S(1)}, bf16[256,512]{1,0:T(8,128)(2,1)S(1)}, bf16[16,512]{1,0:T(8,128)(2,1)S(1)...) custom-call(s32[2,128]{1,0:T(2,128)S(1)} %get-tuple-element.50.early, ...), custom_call_target="tpu_custom_call", output_to_operand_aliasing={{0}: (1, {})} | custom-call | flops 2147483648 | bytes 1048576 | tf_op jit(solution)/shard_map/pallas_call | solution.py:563
  22.0 2.5 %collective-permute-start.5 = (bf16[16,512]{1,0:T(8,128)(2,1)S(1)}, bf16[16,512]{1,0:T(8,128)(2,1)S(1)}, u32[]{:S(2)}, u32[]{:S(2)}) collective-permute-start(bf16[16,512]{1,0:T(8,128)(2,1)S(1)} %get-tuple-element.83), channel_id=1, source_target_pairs={{0,3},{1,2},{2,1},{3,0},{4,7},{5,6},{6,5},{7,4},{8,11},{9,10},{10,... | collective-permute-start | bytes 49160 | tf_op jit(solution)/shard_map/ppermute | solution.py:587
  24.5 1.9 %collective-permute-start.7 = (bf16[16,512]{1,0:T(8,128)(2,1)S(1)}, bf16[16,512]{1,0:T(8,128)(2,1)S(1)}, u32[]{:S(2)}, u32[]{:S(2)}) collective-permute-start(bf16[16,512]{1,0:T(8,128)(2,1)S(1)} %get-tuple-element.85), channel_id=1, source_target_pairs={{0,1},{1,0},{2,3},{3,2},{4,5},{5,4},{6,7},{7,6},{8,9},{9,8},{10,11... | collective-permute-start | bytes 49160 | tf_op jit(solution)/shard_map/ppermute | solution.py:587
  26.5 1.9 %shard_map.190 = (f32[256,512]{1,0:T(8,128)S(1)}, bf16[256,512]{1,0:T(8,128)(2,1)S(1)}, bf16[256,512]{1,0:T(8,128)(2,1)S(1)}, bf16[256,768]{1,0:T(8,128)(2,1)S(1)}) custom-call(f32[768,512]{1,0:T(8,128)S(1)} %get-tuple-element.58.half, f32[768,512]{1,0:T(8,128)S(1)} %get-tuple-element.72.half2, bf16[128,512]{1,0:T(8,128)(2,1)S(1)} %get-tuple-element.73.grad_first, ...), custom_call_target="tpu_custom_call" | custom-call | flops 2147483648 | bytes 1048576 | tf_op jit(solution)/shard_map/pallas_call | solution.py:563
  28.4 0.8 %collective-permute-done.6.refs_1_ = bf16[16,512]{1,0:T(8,128)(2,1)S(1)} collective-permute-done((bf16[16,512]{1,0:T(8,128)(2,1)S(1)}, bf16[16,512]{1,0:T(8,128)(2,1)S(1)}, u32[]{:S(2)}, u32[]{:S(2)}) %collective-permute-start.6) | collective-permute-done | bytes 16416 | tf_op jit(solution)/shard_map/ppermute | solution.py:587
  29.2 1.1 %shard_map.191 = (bf16[256,512]{1,0:T(8,128)(2,1)S(1)}, bf16[256,512]{1,0:T(8,128)(2,1)S(1)}, bf16[128,512]{1,0:T(8,128)(2,1)S(1)}, bf16[128,512]{1,0:T(8,128)(2,1)S(1)}, f32[16,512]{1,0:T(8,128)S(1)}) custom-call(s32[2,128]{1,0:T(2,128)S(1)} %get-tuple-element.50.early, f32[256,512]{1,0:T(8,128)S(1)} %get-tuple-element.78.grad_local, ...), custom_call_target="tpu_custom_call" | custom-call | flops 2147483648 | bytes 1048576 | tf_op jit(solution)/shard_map/pallas_call | solution.py:563
  30.3 0.1 collective-permute-start.8
  30.3 1.4 %collective-permute-start.9 = (bf16[128,512]{1,0:T(8,128)(2,1)S(1)}, bf16[128,512]{1,0:T(8,128)(2,1)S(1)}, u32[]{:S(2)}, u32[]{:S(2)}) collective-permute-start(bf16[128,512]{1,0:T(8,128)(2,1)S(1)} %get-tuple-element.92), channel_id=1, source_target_pairs={{0,28},{4,8},{8,4},{12,16},{16,12},{20,24},{24,20},{28,0},{1,29},{... | collective-permute-start | bytes 393224 | tf_op jit(solution)/shard_map/ppermute | solution.py:579
  31.7 1.8 %shard_map.192 = (bf16[256,512]{1,0:T(8,128)(2,1)}, f32[512,512]{1,0:T(8,128)S(1)}, bf16[512,128]{1,0:T(8,128)(2,1)S(1)}) custom-call(bf16[256,512]{1,0:T(8,128)(2,1)S(1)} %get-tuple-element.86.grad_first, bf16[256,512]{1,0:T(8,128)(2,1)S(1)} %get-tuple-element.87.back, f32[768,512]{1,0:T(8,128)S(1)} %get-tuple-element.58.half, ...), custom_call_target="tpu_custom_call" | custom-call | flops 2147483648 | bytes 1048576 | tf_op jit(solution)/shard_map/pallas_call | solution.py:563
  33.5 3.5 %collective-permute-done.9.far = bf16[128,512]{1,0:T(8,128)(2,1)S(1)} collective-permute-done((bf16[128,512]{1,0:T(8,128)(2,1)S(1)}, bf16[128,512]{1,0:T(8,128)(2,1)S(1)}, u32[]{:S(2)}, u32[]{:S(2)}) %collective-permute-start.9) | collective-permute-done | bytes 131104 | tf_op jit(solution)/shard_map/ppermute | solution.py:579
  37.0 1.3 %shard_map.193 = bf16[512,512]{1,0:T(8,128)(2,1)} custom-call(f32[512,512]{1,0:T(8,128)S(1)} %get-tuple-element.90.own, bf16[512,128]{1,0:T(8,128)(2,1)S(1)} %get-tuple-element.91.sum_far, bf16[128,512]{1,0:T(8,128)(2,1)S(1)} %collective-permute-done.9.far, bf16[512,512]{1,0:T(8,128)(2,1)S(1)} %copy-done.5), custom_call_target="tpu_custom_call" | custom-call | flops 2147483648 | bytes 1048576 | tf_op jit(solution)/shard_map/pallas_call | solution.py:563
  (28 shorter events, 0.1 us)
Async XLA Ops:
  0.6 7.0 %copy-start.5 = (bf16[512,512]{1,0:T(8,128)(2,1)S(1)}, bf16[512,512]{1,0:T(8,128)(2,1)}, u32[]{:S(2)}) copy-start(bf16[512,512]{1,0:T(8,128)(2,1)} %w_source.13) | copy-start | bytes 1572868
  0.6 7.0 %copy-start.6 = (bf16[256,512]{1,0:T(8,128)(2,1)S(1)}, bf16[256,512]{1,0:T(8,128)(2,1)}, u32[]{:S(2)}) copy-start(bf16[256,512]{1,0:T(8,128)(2,1)} %mesh.5) | copy-start | bytes 786436
  0.7 7.0 %copy-start.4 = (bf16[512,512]{1,0:T(8,128)(2,1)S(1)}, bf16[512,512]{1,0:T(8,128)(2,1)}, u32[]{:S(2)}) copy-start(bf16[512,512]{1,0:T(8,128)(2,1)} %w_dest.7) | copy-start | bytes 1572868
  0.7 7.0 %copy-start.11 = (s32[768]{0:T(1024)S(1)}, s32[768]{0:T(1024)}, u32[]{:S(2)}) copy-start(s32[768]{0:T(1024)} %target2.1) | copy-start | bytes 9220
  0.7 7.0 %copy-start.10 = (s32[768]{0:T(1024)S(1)}, s32[768]{0:T(1024)}, u32[]{:S(2)}) copy-start(s32[768]{0:T(1024)} %sender2.1) | copy-start | bytes 9220
  0.7 7.0 %copy-start.9 = (s32[768]{0:T(1024)S(1)}, s32[768]{0:T(1024)}, u32[]{:S(2)}) copy-start(s32[768]{0:T(1024)} %target.1) | copy-start | bytes 9220
  0.7 7.0 %copy-start.8 = (s32[768]{0:T(1024)S(1)}, s32[768]{0:T(1024)}, u32[]{:S(2)}) copy-start(s32[768]{0:T(1024)} %sender.1) | copy-start | bytes 9220
  2.2 5.5 %collective-permute-start = (bf16[128,512]{1,0:T(8,128)(2,1)S(1)}, bf16[128,512]{1,0:T(8,128)(2,1)S(1)}, u32[]{:S(2)}, u32[]{:S(2)}) collective-permute-start(bf16[128,512]{1,0:T(8,128)(2,1)S(1)} %get-tuple-element.49), channel_id=1, source_target_pairs={{0,4},{4,0},{8,12},{12,8},{16,20},{20,16},{24,28},{28,24},{1,5},{5... | collective-permute-start | bytes 393224 | tf_op jit(solution)/shard_map/ppermute | solution.py:580
  2.7 8.0 %collective-permute-start.1 = (bf16[128,512]{1,0:T(8,128)(2,1)S(1)}, bf16[128,512]{1,0:T(8,128)(2,1)S(1)}, u32[]{:S(2)}, u32[]{:S(2)}) collective-permute-start(bf16[128,512]{1,0:T(8,128)(2,1)S(1)} %get-tuple-element.52), channel_id=1, source_target_pairs={{0,28},{4,8},{8,4},{12,16},{16,12},{20,24},{24,20},{28,0},{1,29},{... | collective-permute-start | bytes 393224 | tf_op jit(solution)/shard_map/ppermute | solution.py:579
  7.7 3.0 %copy-start.2 = (bf16[512,512]{1,0:T(8,128)(2,1)S(1)}, bf16[512,512]{1,0:T(8,128)(2,1)}, u32[]{:S(2)}) copy-start(bf16[512,512]{1,0:T(8,128)(2,1)} %w_out.9) | copy-start | bytes 1572868
  7.7 3.0 %copy-start.13 = (f32[512]{0:T(512)S(1)}, f32[512]{0:T(512)}, u32[]{:S(2)}) copy-start(f32[512]{0:T(512)} %gain.7) | copy-start | bytes 6148
  10.7 5.9 %copy-start.1 = (bf16[512,512]{1,0:T(8,128)(2,1)S(1)}, bf16[512,512]{1,0:T(8,128)(2,1)}, u32[]{:S(2)}) copy-start(bf16[512,512]{1,0:T(8,128)(2,1)} %w_dest.6) | copy-start | bytes 1572868
  10.8 5.9 %copy-start.3 = (bf16[512,512]{1,0:T(8,128)(2,1)S(1)}, bf16[512,512]{1,0:T(8,128)(2,1)}, u32[]{:S(2)}) copy-start(bf16[512,512]{1,0:T(8,128)(2,1)} %w_source2.1) | copy-start | bytes 1572868
  10.8 5.9 %copy-start.7 = (bf16[256,512]{1,0:T(8,128)(2,1)S(1)}, bf16[256,512]{1,0:T(8,128)(2,1)}, u32[]{:S(2)}) copy-start(bf16[256,512]{1,0:T(8,128)(2,1)} %cotangent.3) | copy-start | bytes 786436
  10.8 5.9 %copy-start.12 = (f32[512]{0:T(512)S(1)}, f32[512]{0:T(512)}, u32[]{:S(2)}) copy-start(f32[512]{0:T(512)} %gain2.1) | copy-start | bytes 6148
  11.9 6.8 %collective-permute-start.4 = (bf16[16,512]{1,0:T(8,128)(2,1)S(1)}, bf16[16,512]{1,0:T(8,128)(2,1)S(1)}, u32[]{:S(2)}, u32[]{:S(2)}) collective-permute-start(bf16[16,512]{1,0:T(8,128)(2,1)S(1)} %get-tuple-element.71), channel_id=1, source_target_pairs={{0,2},{1,0},{2,3},{3,1},{4,6},{5,4},{6,7},{7,5},{8,10},{9,8},{10,1... | collective-permute-start | bytes 49160 | tf_op jit(solution)/shard_map/ppermute | solution.py:587
  14.5 5.5 %collective-permute-start.3 = (bf16[16,512]{1,0:T(8,128)(2,1)S(1)}, bf16[16,512]{1,0:T(8,128)(2,1)S(1)}, u32[]{:S(2)}, u32[]{:S(2)}) collective-permute-start(bf16[16,512]{1,0:T(8,128)(2,1)S(1)} %get-tuple-element.71), channel_id=1, source_target_pairs={{0,3},{1,2},{2,1},{3,0},{4,7},{5,6},{6,5},{7,4},{8,11},{9,10},{10,... | collective-permute-start | bytes 49160 | tf_op jit(solution)/shard_map/ppermute | solution.py:587
  15.8 4.6 %collective-permute-start.2 = (bf16[16,512]{1,0:T(8,128)(2,1)S(1)}, bf16[16,512]{1,0:T(8,128)(2,1)S(1)}, u32[]{:S(2)}, u32[]{:S(2)}) collective-permute-start(bf16[16,512]{1,0:T(8,128)(2,1)S(1)} %get-tuple-element.71), channel_id=1, source_target_pairs={{0,1},{1,3},{2,0},{3,2},{4,5},{5,7},{6,4},{7,6},{8,9},{9,11},{10,8... | collective-permute-start | bytes 49160 | tf_op jit(solution)/shard_map/ppermute | solution.py:587
  16.6 3.8 %copy-start = (bf16[512,512]{1,0:T(8,128)(2,1)S(1)}, bf16[512,512]{1,0:T(8,128)(2,1)}, u32[]{:S(2)}) copy-start(bf16[512,512]{1,0:T(8,128)(2,1)} %w_out.7) | copy-start | bytes 1572868
  22.0 6.4 %collective-permute-start.5 = (bf16[16,512]{1,0:T(8,128)(2,1)S(1)}, bf16[16,512]{1,0:T(8,128)(2,1)S(1)}, u32[]{:S(2)}, u32[]{:S(2)}) collective-permute-start(bf16[16,512]{1,0:T(8,128)(2,1)S(1)} %get-tuple-element.83), channel_id=1, source_target_pairs={{0,3},{1,2},{2,1},{3,0},{4,7},{5,6},{6,5},{7,4},{8,11},{9,10},{10,... | collective-permute-start | bytes 49160 | tf_op jit(solution)/shard_map/ppermute | solution.py:587
  24.5 4.6 %collective-permute-start.6 = (bf16[16,512]{1,0:T(8,128)(2,1)S(1)}, bf16[16,512]{1,0:T(8,128)(2,1)S(1)}, u32[]{:S(2)}, u32[]{:S(2)}) collective-permute-start(bf16[16,512]{1,0:T(8,128)(2,1)S(1)} %get-tuple-element.84), channel_id=1, source_target_pairs={{0,2},{1,3},{2,0},{3,1},{4,6},{5,7},{6,4},{7,5},{8,10},{9,11},{10,... | collective-permute-start | bytes 49160 | tf_op jit(solution)/shard_map/ppermute | solution.py:587
  24.5 4.6 %collective-permute-start.7 = (bf16[16,512]{1,0:T(8,128)(2,1)S(1)}, bf16[16,512]{1,0:T(8,128)(2,1)S(1)}, u32[]{:S(2)}, u32[]{:S(2)}) collective-permute-start(bf16[16,512]{1,0:T(8,128)(2,1)S(1)} %get-tuple-element.85), channel_id=1, source_target_pairs={{0,1},{1,0},{2,3},{3,2},{4,5},{5,4},{6,7},{7,6},{8,9},{9,8},{10,11... | collective-permute-start | bytes 49160 | tf_op jit(solution)/shard_map/ppermute | solution.py:587
  29.2 2.5 %copy-start.14 = (s32[256]{0:T(256)S(1)}, s32[256]{0:T(256)}, u32[]{:S(2)}) copy-start(s32[256]{0:T(256)} %halo.1) | copy-start | bytes 3076
  30.3 1.4 %collective-permute-start.8 = (bf16[128,512]{1,0:T(8,128)(2,1)S(1)}, bf16[128,512]{1,0:T(8,128)(2,1)S(1)}, u32[]{:S(2)}, u32[]{:S(2)}) collective-permute-start(bf16[128,512]{1,0:T(8,128)(2,1)S(1)} %get-tuple-element.89), channel_id=1, source_target_pairs={{0,4},{4,0},{8,12},{12,8},{16,20},{20,16},{24,28},{28,24},{1,5},{5... | collective-permute-start | bytes 393224 | tf_op jit(solution)/shard_map/ppermute | solution.py:580
  30.3 6.7 %collective-permute-start.9 = (bf16[128,512]{1,0:T(8,128)(2,1)S(1)}, bf16[128,512]{1,0:T(8,128)(2,1)S(1)}, u32[]{:S(2)}, u32[]{:S(2)}) collective-permute-start(bf16[128,512]{1,0:T(8,128)(2,1)S(1)} %get-tuple-element.92), channel_id=1, source_target_pairs={{0,28},{4,8},{8,4},{12,16},{16,12},{20,24},{24,20},{28,0},{1,29},{... | collective-permute-start | bytes 393224 | tf_op jit(solution)/shard_map/ppermute | solution.py:579

commit v9 on v8

--- a/solution.py
+++ b/solution.py
@@ -486,14 +486,16 @@
         back = (0.5 * mm_t(back.astype(BF16), w_out[...])).astype(BF16)
         back = jnp.concatenate([back, back_local[coarse:, :]], axis=0)
         back_ref[...] = back
-        first = mm(pick_goal[:FIRST, :], back) * slope[...].astype(F32)
-        grad_first[...] = first.astype(BF16)
+        for c in pieces_of(FIRST, 128):
+            first = mm(pick_goal[c, :], back) * slope[c, :].astype(F32)
+            grad_first[c, :] = first.astype(BF16)
 
     @pl.when(number <= FIRST)
     def _():
         turn()
-        far[...] = mm(sum_rim[rim:, :FIRST], grad_first[...]).astype(BF16)
-        near[...] = mm(sum_rim[:rim, :FIRST], grad_first[...]).astype(BF16)
+        rows = mm(sum_rim[:, :FIRST], grad_first[...]).astype(BF16)
+        near[...] = rows[:rim]
+        far[...] = rows[rim:]
 
     @pl.when(number > FIRST)
     def _():

time: 38.5 us -> 38.5 us (level)
  no operation moved by 1% of the time
where the time goes in v9:
time: 38.5 us; the launch traced here: 38.3 us
  Pallas kernels  15.2 us (39%)
  starting transfers between devices  14.8 us (38%)
  waiting for transfers between devices  6.05 us (16%)
  between operations  2.18 us (6%)
    pallas_call x9, Pallas kernels, call(): pl.pallas_call(kernel, out_shape=[jax.ShapeDtypeStruct(s, d) for s, d in...  15.2 us
    ppermute x6, starting transfers between devices, exchange(): out.append(lax.ppermute(piece, 'group', list(enumerate(goals))))  9.23 us
    ppermute x2, starting transfers between devices, swap_halo(): far = lax.ppermute(far, 'patch', far_pairs)  4.91 us
    ppermute x2, waiting for transfers between devices, swap_halo(): far = lax.ppermute(far, 'patch', far_pairs)  3.45 us
    ppermute x6, waiting for transfers between devices, exchange(): out.append(lax.ppermute(piece, 'group', list(enumerate(goals))))  2.6 us
  transfers between devices with their start and end apart: 10, of which 4 were waited for; matrix products, arithmetic and copies ran while one was open for 0% of the time, Pallas kernels for 23%

profile of v9, /device:TPU:0, one launch (start us, length us, event | category | flops | bytes accessed | tf_op | source)
XLA Modules:
  0.0 38.3 jit_solution(3856356182134394661)
XLA Ops:
  0.7 1.5 %shard_map.185 = (bf16[128,512]{1,0:T(8,128)(2,1)S(1)}, bf16[128,512]{1,0:T(8,128)(2,1)S(1)}, bf16[512,512]{1,0:T(8,128)(2,1)S(1)}) custom-call(s32[256]{0:T(256)} %halo.1, bf16[512,512]{1,0:T(8,128)(2,1)} %grid_hbm.1), custom_call_target="tpu_custom_call" | custom-call | flops 4294967296 | bytes 1048576 | tf_op jit(solution)/shard_map/pallas_call | solution.py:565
  2.2 0.6 %collective-permute-start = (bf16[128,512]{1,0:T(8,128)(2,1)S(1)}, bf16[128,512]{1,0:T(8,128)(2,1)S(1)}, u32[]{:S(2)}, u32[]{:S(2)}) collective-permute-start(bf16[128,512]{1,0:T(8,128)(2,1)S(1)} %get-tuple-element.49), channel_id=1, source_target_pairs={{0,4},{4,0},{8,12},{12,8},{16,20},{20,16},{24,28},{28,24},{1,5},{5... | collective-permute-start | bytes 393224 | tf_op jit(solution)/shard_map/ppermute | solution.py:582
  2.7 3.5 %collective-permute-start.1 = (bf16[128,512]{1,0:T(8,128)(2,1)S(1)}, bf16[128,512]{1,0:T(8,128)(2,1)S(1)}, u32[]{:S(2)}, u32[]{:S(2)}) collective-permute-start(bf16[128,512]{1,0:T(8,128)(2,1)S(1)} %get-tuple-element.52), channel_id=1, source_target_pairs={{0,28},{4,8},{8,4},{12,16},{16,12},{20,24},{24,20},{28,0},{1,29},{... | collective-permute-start | bytes 393224 | tf_op jit(solution)/shard_map/ppermute | solution.py:581
  7.6 0.1 pad_add_fusion.counts
  7.7 0.0 collective-permute-done.near
  7.7 0.0 copy-start.2
  7.7 0.0 copy-start.13
  7.8 3.0 %shard_map.186 = (s32[2,128]{1,0:T(2,128)S(1)}, bf16[128,512]{1,0:T(8,128)(2,1)S(1)}, f32[768,512]{1,0:T(8,128)S(1)}, bf16[768,512]{1,0:T(8,128)(2,1)S(1)}, f32[...) custom-call(s32[2]{0:T(128)S(1)} %pad_add_fusion.counts, ...), custom_call_target="tpu_custom_call" | custom-call | flops 2147483648 | bytes 1048576 | tf_op jit(solution)/shard_map/pallas_call | solution.py:565
  10.7 0.0 copy-start.1
  10.8 0.0 copy-start.3
  10.8 0.0 copy-start.7
  10.8 0.0 copy-start.12
  10.8 1.0 %shard_map.187 = (f32[768,512]{1,0:T(8,128)S(1)}, bf16[768,512]{1,0:T(8,128)(2,1)S(1)}, bf16[16,512]{1,0:T(8,128)(2,1)S(1)}) custom-call(s32[2,128]{1,0:T(2,128)S(1)} %get-tuple-element.50.early, bf16[128,512]{1,0:T(8,128)(2,1)S(1)} %get-tuple-element.51.near_source, ...), custom_call_target="tpu_custom_call", output_to_operand_aliasing={{0}: (3, {}), {1}: (4, {})} | custom-call | flops 2147483648 | bytes 1048576 | tf_op jit(solution)/shard_map/pallas_call | solution.py:565
  11.9 2.6 %collective-permute-start.4 = (bf16[16,512]{1,0:T(8,128)(2,1)S(1)}, bf16[16,512]{1,0:T(8,128)(2,1)S(1)}, u32[]{:S(2)}, u32[]{:S(2)}) collective-permute-start(bf16[16,512]{1,0:T(8,128)(2,1)S(1)} %get-tuple-element.71), channel_id=1, source_target_pairs={{0,2},{1,0},{2,3},{3,1},{4,6},{5,4},{6,7},{7,5},{8,10},{9,8},{10,1... | collective-permute-start | bytes 49160 | tf_op jit(solution)/shard_map/ppermute | solution.py:589
  14.5 1.4 %collective-permute-start.3 = (bf16[16,512]{1,0:T(8,128)(2,1)S(1)}, bf16[16,512]{1,0:T(8,128)(2,1)S(1)}, u32[]{:S(2)}, u32[]{:S(2)}) collective-permute-start(bf16[16,512]{1,0:T(8,128)(2,1)S(1)} %get-tuple-element.71), channel_id=1, source_target_pairs={{0,3},{1,2},{2,1},{3,0},{4,7},{5,6},{6,5},{7,4},{8,11},{9,10},{10,... | collective-permute-start | bytes 49160 | tf_op jit(solution)/shard_map/ppermute | solution.py:589
  15.8 0.8 %collective-permute-start.2 = (bf16[16,512]{1,0:T(8,128)(2,1)S(1)}, bf16[16,512]{1,0:T(8,128)(2,1)S(1)}, u32[]{:S(2)}, u32[]{:S(2)}) collective-permute-start(bf16[16,512]{1,0:T(8,128)(2,1)S(1)} %get-tuple-element.71), channel_id=1, source_target_pairs={{0,1},{1,3},{2,0},{3,2},{4,5},{5,7},{6,4},{7,6},{8,9},{9,11},{10,8... | collective-permute-start | bytes 49160 | tf_op jit(solution)/shard_map/ppermute | solution.py:589
  16.6 0.0 copy-start
  16.7 2.0 %shard_map.188 = (f32[256,512]{1,0:T(8,128)S(1)}, f32[256,128]{1,0:T(8,128)S(1)}, f32[768,512]{1,0:T(8,128)S(1)}, bf16[768,256]{1,0:T(8,128)(2,1)S(1)}, bf16[768...) custom-call(bf16[768,512]{1,0:T(8,128)(2,1)S(1)} %get-tuple-element., ...), custom_call_target="tpu_custom_call" | custom-call | flops 2147483648 | bytes 1048576 | tf_op jit(solution)/shard_map/pallas_call | solution.py:565
  18.7 0.0 collective-permute-done.4.refs_2_
  18.7 1.3 %collective-permute-done.3.refs_1_ = bf16[16,512]{1,0:T(8,128)(2,1)S(1)} collective-permute-done((bf16[16,512]{1,0:T(8,128)(2,1)S(1)}, bf16[16,512]{1,0:T(8,128)(2,1)S(1)}, u32[]{:S(2)}, u32[]{:S(2)}) %collective-permute-start.3) | collective-permute-done | bytes 16416 | tf_op jit(solution)/shard_map/ppermute | solution.py:589
  20.0 0.5 %collective-permute-done.2.refs_0_ = bf16[16,512]{1,0:T(8,128)(2,1)S(1)} collective-permute-done((bf16[16,512]{1,0:T(8,128)(2,1)S(1)}, bf16[16,512]{1,0:T(8,128)(2,1)S(1)}, u32[]{:S(2)}, u32[]{:S(2)}) %collective-permute-start.2) | collective-permute-done | bytes 16416 | tf_op jit(solution)/shard_map/ppermute | solution.py:589
  20.5 1.5 %shard_map.189 = (f32[768,512]{1,0:T(8,128)S(1)}, bf16[128,512]{1,0:T(8,128)(2,1)S(1)}, bf16[256,512]{1,0:T(8,128)(2,1)S(1)}, bf16[16,512]{1,0:T(8,128)(2,1)S(1)...) custom-call(s32[2,128]{1,0:T(2,128)S(1)} %get-tuple-element.50.early, ...), custom_call_target="tpu_custom_call", output_to_operand_aliasing={{0}: (1, {})} | custom-call | flops 2147483648 | bytes 1048576 | tf_op jit(solution)/shard_map/pallas_call | solution.py:565
  22.0 2.5 %collective-permute-start.5 = (bf16[16,512]{1,0:T(8,128)(2,1)S(1)}, bf16[16,512]{1,0:T(8,128)(2,1)S(1)}, u32[]{:S(2)}, u32[]{:S(2)}) collective-permute-start(bf16[16,512]{1,0:T(8,128)(2,1)S(1)} %get-tuple-element.83), channel_id=1, source_target_pairs={{0,3},{1,2},{2,1},{3,0},{4,7},{5,6},{6,5},{7,4},{8,11},{9,10},{10,... | collective-permute-start | bytes 49160 | tf_op jit(solution)/shard_map/ppermute | solution.py:589
  24.5 1.9 %collective-permute-start.7 = (bf16[16,512]{1,0:T(8,128)(2,1)S(1)}, bf16[16,512]{1,0:T(8,128)(2,1)S(1)}, u32[]{:S(2)}, u32[]{:S(2)}) collective-permute-start(bf16[16,512]{1,0:T(8,128)(2,1)S(1)} %get-tuple-element.85), channel_id=1, source_target_pairs={{0,1},{1,0},{2,3},{3,2},{4,5},{5,4},{6,7},{7,6},{8,9},{9,8},{10,11... | collective-permute-start | bytes 49160 | tf_op jit(solution)/shard_map/ppermute | solution.py:589
  26.5 1.9 %shard_map.190 = (f32[256,512]{1,0:T(8,128)S(1)}, bf16[256,512]{1,0:T(8,128)(2,1)S(1)}, bf16[256,512]{1,0:T(8,128)(2,1)S(1)}, bf16[256,768]{1,0:T(8,128)(2,1)S(1)}) custom-call(f32[768,512]{1,0:T(8,128)S(1)} %get-tuple-element.58.half, f32[768,512]{1,0:T(8,128)S(1)} %get-tuple-element.72.half2, bf16[128,512]{1,0:T(8,128)(2,1)S(1)} %get-tuple-element.73.grad_first, ...), custom_call_target="tpu_custom_call" | custom-call | flops 2147483648 | bytes 1048576 | tf_op jit(solution)/shard_map/pallas_call | solution.py:565
  28.4 0.8 %collective-permute-done.6.refs_1_ = bf16[16,512]{1,0:T(8,128)(2,1)S(1)} collective-permute-done((bf16[16,512]{1,0:T(8,128)(2,1)S(1)}, bf16[16,512]{1,0:T(8,128)(2,1)S(1)}, u32[]{:S(2)}, u32[]{:S(2)}) %collective-permute-start.6) | collective-permute-done | bytes 16416 | tf_op jit(solution)/shard_map/ppermute | solution.py:589
  29.2 1.1 %shard_map.191 = (bf16[256,512]{1,0:T(8,128)(2,1)S(1)}, bf16[256,512]{1,0:T(8,128)(2,1)S(1)}, bf16[128,512]{1,0:T(8,128)(2,1)S(1)}, bf16[128,512]{1,0:T(8,128)(2,1)S(1)}, f32[16,512]{1,0:T(8,128)S(1)}) custom-call(s32[2,128]{1,0:T(2,128)S(1)} %get-tuple-element.50.early, f32[256,512]{1,0:T(8,128)S(1)} %get-tuple-element.78.grad_local, ...), custom_call_target="tpu_custom_call" | custom-call | flops 2147483648 | bytes 1048576 | tf_op jit(solution)/shard_map/pallas_call | solution.py:565
  30.2 0.1 collective-permute-start.8
  30.3 1.4 %collective-permute-start.9 = (bf16[128,512]{1,0:T(8,128)(2,1)S(1)}, bf16[128,512]{1,0:T(8,128)(2,1)S(1)}, u32[]{:S(2)}, u32[]{:S(2)}) collective-permute-start(bf16[128,512]{1,0:T(8,128)(2,1)S(1)} %get-tuple-element.92), channel_id=1, source_target_pairs={{0,28},{4,8},{8,4},{12,16},{16,12},{20,24},{24,20},{28,0},{1,29},{... | collective-permute-start | bytes 393224 | tf_op jit(solution)/shard_map/ppermute | solution.py:581
  31.7 1.9 %shard_map.192 = (bf16[256,512]{1,0:T(8,128)(2,1)}, f32[512,512]{1,0:T(8,128)S(1)}, bf16[512,128]{1,0:T(8,128)(2,1)S(1)}) custom-call(bf16[256,512]{1,0:T(8,128)(2,1)S(1)} %get-tuple-element.86.grad_first, bf16[256,512]{1,0:T(8,128)(2,1)S(1)} %get-tuple-element.87.back, f32[768,512]{1,0:T(8,128)S(1)} %get-tuple-element.58.half, ...), custom_call_target="tpu_custom_call" | custom-call | flops 2147483648 | bytes 1048576 | tf_op jit(solution)/shard_map/pallas_call | solution.py:565
  33.6 3.4 %collective-permute-done.9.far = bf16[128,512]{1,0:T(8,128)(2,1)S(1)} collective-permute-done((bf16[128,512]{1,0:T(8,128)(2,1)S(1)}, bf16[128,512]{1,0:T(8,128)(2,1)S(1)}, u32[]{:S(2)}, u32[]{:S(2)}) %collective-permute-start.9) | collective-permute-done | bytes 131104 | tf_op jit(solution)/shard_map/ppermute | solution.py:581
  37.0 1.3 %shard_map.193 = bf16[512,512]{1,0:T(8,128)(2,1)} custom-call(f32[512,512]{1,0:T(8,128)S(1)} %get-tuple-element.90.own, bf16[512,128]{1,0:T(8,128)(2,1)S(1)} %get-tuple-element.91.sum_far, bf16[128,512]{1,0:T(8,128)(2,1)S(1)} %collective-permute-done.9.far, bf16[512,512]{1,0:T(8,128)(2,1)S(1)} %copy-done.5), custom_call_target="tpu_custom_call" | custom-call | flops 2147483648 | bytes 1048576 | tf_op jit(solution)/shard_map/pallas_call | solution.py:565
  (28 shorter events, 0.1 us)
Async XLA Ops:
  0.6 7.0 %copy-start.5 = (bf16[512,512]{1,0:T(8,128)(2,1)S(1)}, bf16[512,512]{1,0:T(8,128)(2,1)}, u32[]{:S(2)}) copy-start(bf16[512,512]{1,0:T(8,128)(2,1)} %w_source.13) | copy-start | bytes 1572868
  0.6 7.0 %copy-start.6 = (bf16[256,512]{1,0:T(8,128)(2,1)S(1)}, bf16[256,512]{1,0:T(8,128)(2,1)}, u32[]{:S(2)}) copy-start(bf16[256,512]{1,0:T(8,128)(2,1)} %mesh.5) | copy-start | bytes 786436
  0.7 7.0 %copy-start.4 = (bf16[512,512]{1,0:T(8,128)(2,1)S(1)}, bf16[512,512]{1,0:T(8,128)(2,1)}, u32[]{:S(2)}) copy-start(bf16[512,512]{1,0:T(8,128)(2,1)} %w_dest.7) | copy-start | bytes 1572868
  0.7 7.0 %copy-start.11 = (s32[768]{0:T(1024)S(1)}, s32[768]{0:T(1024)}, u32[]{:S(2)}) copy-start(s32[768]{0:T(1024)} %target2.1) | copy-start | bytes 9220
  0.7 7.0 %copy-start.10 = (s32[768]{0:T(1024)S(1)}, s32[768]{0:T(1024)}, u32[]{:S(2)}) copy-start(s32[768]{0:T(1024)} %sender2.1) | copy-start | bytes 9220
  0.7 7.0 %copy-start.9 = (s32[768]{0:T(1024)S(1)}, s32[768]{0:T(1024)}, u32[]{:S(2)}) copy-start(s32[768]{0:T(1024)} %target.1) | copy-start | bytes 9220
  0.7 7.0 %copy-start.8 = (s32[768]{0:T(1024)S(1)}, s32[768]{0:T(1024)}, u32[]{:S(2)}) copy-start(s32[768]{0:T(1024)} %sender.1) | copy-start | bytes 9220
  2.2 5.5 %collective-permute-start = (bf16[128,512]{1,0:T(8,128)(2,1)S(1)}, bf16[128,512]{1,0:T(8,128)(2,1)S(1)}, u32[]{:S(2)}, u32[]{:S(2)}) collective-permute-start(bf16[128,512]{1,0:T(8,128)(2,1)S(1)} %get-tuple-element.49), channel_id=1, source_target_pairs={{0,4},{4,0},{8,12},{12,8},{16,20},{20,16},{24,28},{28,24},{1,5},{5... | collective-permute-start | bytes 393224 | tf_op jit(solution)/shard_map/ppermute | solution.py:582
  2.7 8.0 %collective-permute-start.1 = (bf16[128,512]{1,0:T(8,128)(2,1)S(1)}, bf16[128,512]{1,0:T(8,128)(2,1)S(1)}, u32[]{:S(2)}, u32[]{:S(2)}) collective-permute-start(bf16[128,512]{1,0:T(8,128)(2,1)S(1)} %get-tuple-element.52), channel_id=1, source_target_pairs={{0,28},{4,8},{8,4},{12,16},{16,12},{20,24},{24,20},{28,0},{1,29},{... | collective-permute-start | bytes 393224 | tf_op jit(solution)/shard_map/ppermute | solution.py:581
  7.7 3.0 %copy-start.2 = (bf16[512,512]{1,0:T(8,128)(2,1)S(1)}, bf16[512,512]{1,0:T(8,128)(2,1)}, u32[]{:S(2)}) copy-start(bf16[512,512]{1,0:T(8,128)(2,1)} %w_out.9) | copy-start | bytes 1572868
  7.7 3.0 %copy-start.13 = (f32[512]{0:T(512)S(1)}, f32[512]{0:T(512)}, u32[]{:S(2)}) copy-start(f32[512]{0:T(512)} %gain.7) | copy-start | bytes 6148
  10.7 5.9 %copy-start.1 = (bf16[512,512]{1,0:T(8,128)(2,1)S(1)}, bf16[512,512]{1,0:T(8,128)(2,1)}, u32[]{:S(2)}) copy-start(bf16[512,512]{1,0:T(8,128)(2,1)} %w_dest.6) | copy-start | bytes 1572868
  10.8 5.9 %copy-start.3 = (bf16[512,512]{1,0:T(8,128)(2,1)S(1)}, bf16[512,512]{1,0:T(8,128)(2,1)}, u32[]{:S(2)}) copy-start(bf16[512,512]{1,0:T(8,128)(2,1)} %w_source2.1) | copy-start | bytes 1572868
  10.8 5.9 %copy-start.7 = (bf16[256,512]{1,0:T(8,128)(2,1)S(1)}, bf16[256,512]{1,0:T(8,128)(2,1)}, u32[]{:S(2)}) copy-start(bf16[256,512]{1,0:T(8,128)(2,1)} %cotangent.3) | copy-start | bytes 786436
  10.8 5.9 %copy-start.12 = (f32[512]{0:T(512)S(1)}, f32[512]{0:T(512)}, u32[]{:S(2)}) copy-start(f32[512]{0:T(512)} %gain2.1) | copy-start | bytes 6148
  11.9 6.8 %collective-permute-start.4 = (bf16[16,512]{1,0:T(8,128)(2,1)S(1)}, bf16[16,512]{1,0:T(8,128)(2,1)S(1)}, u32[]{:S(2)}, u32[]{:S(2)}) collective-permute-start(bf16[16,512]{1,0:T(8,128)(2,1)S(1)} %get-tuple-element.71), channel_id=1, source_target_pairs={{0,2},{1,0},{2,3},{3,1},{4,6},{5,4},{6,7},{7,5},{8,10},{9,8},{10,1... | collective-permute-start | bytes 49160 | tf_op jit(solution)/shard_map/ppermute | solution.py:589
  14.5 5.5 %collective-permute-start.3 = (bf16[16,512]{1,0:T(8,128)(2,1)S(1)}, bf16[16,512]{1,0:T(8,128)(2,1)S(1)}, u32[]{:S(2)}, u32[]{:S(2)}) collective-permute-start(bf16[16,512]{1,0:T(8,128)(2,1)S(1)} %get-tuple-element.71), channel_id=1, source_target_pairs={{0,3},{1,2},{2,1},{3,0},{4,7},{5,6},{6,5},{7,4},{8,11},{9,10},{10,... | collective-permute-start | bytes 49160 | tf_op jit(solution)/shard_map/ppermute | solution.py:589
  15.8 4.6 %collective-permute-start.2 = (bf16[16,512]{1,0:T(8,128)(2,1)S(1)}, bf16[16,512]{1,0:T(8,128)(2,1)S(1)}, u32[]{:S(2)}, u32[]{:S(2)}) collective-permute-start(bf16[16,512]{1,0:T(8,128)(2,1)S(1)} %get-tuple-element.71), channel_id=1, source_target_pairs={{0,1},{1,3},{2,0},{3,2},{4,5},{5,7},{6,4},{7,6},{8,9},{9,11},{10,8... | collective-permute-start | bytes 49160 | tf_op jit(solution)/shard_map/ppermute | solution.py:589
  16.6 3.8 %copy-start = (bf16[512,512]{1,0:T(8,128)(2,1)S(1)}, bf16[512,512]{1,0:T(8,128)(2,1)}, u32[]{:S(2)}) copy-start(bf16[512,512]{1,0:T(8,128)(2,1)} %w_out.7) | copy-start | bytes 1572868
  22.0 6.4 %collective-permute-start.5 = (bf16[16,512]{1,0:T(8,128)(2,1)S(1)}, bf16[16,512]{1,0:T(8,128)(2,1)S(1)}, u32[]{:S(2)}, u32[]{:S(2)}) collective-permute-start(bf16[16,512]{1,0:T(8,128)(2,1)S(1)} %get-tuple-element.83), channel_id=1, source_target_pairs={{0,3},{1,2},{2,1},{3,0},{4,7},{5,6},{6,5},{7,4},{8,11},{9,10},{10,... | collective-permute-start | bytes 49160 | tf_op jit(solution)/shard_map/ppermute | solution.py:589
  24.5 4.6 %collective-permute-start.6 = (bf16[16,512]{1,0:T(8,128)(2,1)S(1)}, bf16[16,512]{1,0:T(8,128)(2,1)S(1)}, u32[]{:S(2)}, u32[]{:S(2)}) collective-permute-start(bf16[16,512]{1,0:T(8,128)(2,1)S(1)} %get-tuple-element.84), channel_id=1, source_target_pairs={{0,2},{1,3},{2,0},{3,1},{4,6},{5,7},{6,4},{7,5},{8,10},{9,11},{10,... | collective-permute-start | bytes 49160 | tf_op jit(solution)/shard_map/ppermute | solution.py:589
  24.5 4.6 %collective-permute-start.7 = (bf16[16,512]{1,0:T(8,128)(2,1)S(1)}, bf16[16,512]{1,0:T(8,128)(2,1)S(1)}, u32[]{:S(2)}, u32[]{:S(2)}) collective-permute-start(bf16[16,512]{1,0:T(8,128)(2,1)S(1)} %get-tuple-element.85), channel_id=1, source_target_pairs={{0,1},{1,0},{2,3},{3,2},{4,5},{5,4},{6,7},{7,6},{8,9},{9,8},{10,11... | collective-permute-start | bytes 49160 | tf_op jit(solution)/shard_map/ppermute | solution.py:589
  29.2 2.5 %copy-start.14 = (s32[256]{0:T(256)S(1)}, s32[256]{0:T(256)}, u32[]{:S(2)}) copy-start(s32[256]{0:T(256)} %halo.1) | copy-start | bytes 3076
  30.2 1.4 %collective-permute-start.8 = (bf16[128,512]{1,0:T(8,128)(2,1)S(1)}, bf16[128,512]{1,0:T(8,128)(2,1)S(1)}, u32[]{:S(2)}, u32[]{:S(2)}) collective-permute-start(bf16[128,512]{1,0:T(8,128)(2,1)S(1)} %get-tuple-element.89), channel_id=1, source_target_pairs={{0,4},{4,0},{8,12},{12,8},{16,20},{20,16},{24,28},{28,24},{1,5},{5... | collective-permute-start | bytes 393224 | tf_op jit(solution)/shard_map/ppermute | solution.py:582
  30.3 6.7 %collective-permute-start.9 = (bf16[128,512]{1,0:T(8,128)(2,1)S(1)}, bf16[128,512]{1,0:T(8,128)(2,1)S(1)}, u32[]{:S(2)}, u32[]{:S(2)}) collective-permute-start(bf16[128,512]{1,0:T(8,128)(2,1)S(1)} %get-tuple-element.92), channel_id=1, source_target_pairs={{0,28},{4,8},{8,4},{12,16},{16,12},{20,24},{24,20},{28,0},{1,29},{... | collective-permute-start | bytes 393224 | tf_op jit(solution)/shard_map/ppermute | solution.py:581
